TPU v7x, 256 devices: a whole 4x4x8 slice. The times are simulated.
256 devices in a mesh: pts: 64 (over x, z, core), rep: 4 (over y).
Axes of the slice: x: 4, y: 4, z: 8, core: 2. Of those that a mesh axis runs over, the one named last changes fastest.
Arguments:
- points: bfloat16 [4, 131072, 512], P('rep', 'pts'), may hold values from -60 to 60
- counts: int32 [4, 64], P('rep', 'pts'), may hold values from 0 to 2048, as said below
- hilbert_rank: int32 [4, 131072], P('rep', 'pts'), may hold values from 0 to 65535, as said below
- patch_shift: int32 [4], P('rep'), may hold values from 1 to 1023
- norm_gain: float32 [512], replicated, may hold values from 0.1 to 1.9
- project_in: bfloat16 [512, 1536], replicated, may hold values from -8 to 8
- project_out: bfloat16 [512, 512], replicated, may hold values from -0.25 to 0.25
- cotangent: bfloat16 [4, 65536, 512], P('rep', 'pts'), may hold values from -6 to 6
Outputs:
- block_out: bfloat16 [4, 65536, 512], P('rep', 'pts')
- grad_points: bfloat16 [4, 131072, 512], P('rep', 'pts')
- grad_project_in: float32 [512, 1536], replicated
- grad_project_out: float32 [512, 512], replicated
- grad_gain: float32 [512], replicated
Inputs may be any that keep to these rules, and one draw needn't show every extreme that they name: The valid points of shard d fill its first counts[b, d] slots; the counts of a scan sum to 65536, and in every scan some shard holds exactly 2048. `hilbert_rank`: the ranks of the valid slots of a scan are a permutation of 0 to 65535. At most 32 valid slots of one shard have ranks in one block [m * 1024, (m + 1) * 1024); in every scan some shard has exactly 32 in every block. Slots beyond the count hold arbitrary ranks.
All inputs are finite; a program needn't handle non-finite values.
Results may differ from a plain program's by a relative error of at most 0.012.
The roundings to bfloat16 on the way count: a program that leaves them out, or rounds other values in their place, can miss the bound.
Values may be sent and summed in bfloat16 or wider, within the bound.
A program may use at most 128 MiB of HBM per device.

v0:
```python
import math

import jax
import jax.numpy as jnp
from jax import lax
from jax.sharding import PartitionSpec as P

HEAD_DIM = 64
PATCH = 1024


EPSILON = 1e-05


def shifted(value, axis, steps):
    count = lax.axis_size(axis)
    pairs = [(source, (source + steps) % count) for source in range(count)]
    return lax.ppermute(value, axis, pairs)


def layer_stats(rows_in):
    values = rows_in.astype(jnp.float32)
    centre = jnp.mean(values, axis=-1, keepdims=True)
    deviation = values - centre
    inverse = lax.rsqrt(jnp.mean(deviation * deviation, axis=-1, keepdims=True) + EPSILON)
    return (deviation * inverse, inverse)


def split_heads(projected):
    row_count = projected.shape[0]
    head_count = projected.shape[1] // (3 * HEAD_DIM)
    shaped = projected.reshape(row_count // PATCH, PATCH, 3, head_count, HEAD_DIM)
    return jnp.transpose(shaped, (2, 3, 0, 1, 4))


def join_heads(per_head):
    head_count, group_count, patch_rows, depth = per_head.shape
    return jnp.transpose(per_head, (1, 2, 0, 3)).reshape(
        group_count * patch_rows, head_count * depth
    )


def head_forward(triple):
    queries, key_rows, value_rows = triple
    logits = jnp.einsum(
        "gqd,gkd->gqk", queries, key_rows, preferred_element_type=jnp.float32
    ) * HEAD_DIM ** (-0.5)
    attention = jax.nn.softmax(logits, axis=-1).astype(jnp.bfloat16)
    return jnp.einsum(
        "gqk,gkd->gqd", attention, value_rows, preferred_element_type=jnp.float32
    ).astype(jnp.bfloat16)


def attend_forward(projected):
    parts = split_heads(projected)
    return join_heads(lax.map(head_forward, (parts[0], parts[1], parts[2])))


def head_backward(quadruple):
    queries, key_rows, value_rows, grad_rows = quadruple
    logits = jnp.einsum(
        "gqd,gkd->gqk", queries, key_rows, preferred_element_type=jnp.float32
    ) * HEAD_DIM ** (-0.5)
    attention_f32 = jax.nn.softmax(logits, axis=-1)
    attention = attention_f32.astype(jnp.bfloat16)
    grad_values = jnp.einsum(
        "gqk,gqd->gkd", attention, grad_rows, preferred_element_type=jnp.float32
    ).astype(jnp.bfloat16)
    grad_attention = jnp.einsum(
        "gqd,gkd->gqk", grad_rows, value_rows, preferred_element_type=jnp.float32
    )
    row_dot = jnp.sum(grad_attention * attention_f32, axis=-1, keepdims=True)
    grad_logits = (attention_f32 * (grad_attention - row_dot) * HEAD_DIM ** (-0.5)).astype(
        jnp.bfloat16
    )
    grad_queries = jnp.einsum(
        "gqk,gkd->gqd", grad_logits, key_rows, preferred_element_type=jnp.float32
    ).astype(jnp.bfloat16)
    grad_keys = jnp.einsum(
        "gqk,gqd->gkd", grad_logits, queries, preferred_element_type=jnp.float32
    ).astype(jnp.bfloat16)
    return jnp.stack([grad_queries, grad_keys, grad_values])


def attend_backward(projected, grad_mixed):
    parts = split_heads(projected)
    row_count = projected.shape[0]
    head_count = parts.shape[1]
    grad_parts = jnp.transpose(
        grad_mixed.reshape(row_count // PATCH, PATCH, head_count, HEAD_DIM), (2, 0, 1, 3)
    )
    stacked = lax.map(head_backward, (parts[0], parts[1], parts[2], grad_parts))
    return jnp.transpose(stacked, (2, 3, 1, 0, 4)).reshape(row_count, 3 * head_count * HEAD_DIM)


def route_slots(rank_row, point_count, total, row_count, shard_count, send_size):
    slot_total = rank_row.shape[0]
    live_slot = jnp.arange(slot_total, dtype=jnp.int32) < point_count
    moved = rank_row % total
    target_shard = jnp.where(live_slot, moved // row_count, shard_count)
    matches = (target_shard[:, None] == jnp.arange(shard_count, dtype=jnp.int32)[None, :]).astype(
        jnp.int32
    )
    ordinal = jnp.sum((jnp.cumsum(matches, axis=0) - 1) * matches, axis=1)
    target = jnp.where(live_slot, target_shard * send_size + ordinal, shard_count * send_size)
    return (live_slot, target, moved % row_count)


def on_device(
    points, counts, hilbert_rank, patch_shift, norm_gain, project_in, project_out, cotangent
):
    shard_count = lax.axis_size("pts")
    row_count = cotangent.shape[1]
    width = points.shape[2]
    slot_size = points.shape[1] // shard_count
    total = row_count * shard_count
    offset = patch_shift[0]
    live_slot, target, position = route_slots(
        hilbert_rank[0], counts[0, 0], total, row_count, shard_count, slot_size
    )
    outgoing = (
        jnp.zeros((shard_count * slot_size, width), jnp.bfloat16)
        .at[target]
        .set(points[0], mode="drop")
    )
    out_position = (
        jnp.full((shard_count * slot_size,), -1, jnp.int32).at[target].set(position, mode="drop")
    )
    incoming, in_position = (
        lax.all_to_all(outgoing, "pts", split_axis=0, concat_axis=0, tiled=True),
        lax.all_to_all(out_position, "pts", split_axis=0, concat_axis=0, tiled=True),
    )
    placed = jnp.where(in_position < 0, row_count, in_position)
    ordered = jnp.zeros((row_count, width), jnp.bfloat16).at[placed].set(incoming, mode="drop")
    unit_rows, inverse = layer_stats(ordered)
    normed = (unit_rows * norm_gain).astype(jnp.bfloat16)
    projected = jnp.dot(normed, project_in, preferred_element_type=jnp.float32).astype(jnp.bfloat16)
    cot_rows = cotangent[0]
    next_rows = shifted(projected, "pts", -1)
    window_in = lax.dynamic_slice_in_dim(
        jnp.concatenate([projected, next_rows], axis=0), offset, row_count, 0
    )
    window_mixed = attend_forward(window_in)
    tail_rows = shifted(window_mixed, "pts", 1)
    mixed_rows = lax.dynamic_slice_in_dim(
        jnp.concatenate([tail_rows, window_mixed], axis=0), PATCH - offset, row_count, 0
    )
    block_rows = (
        ordered.astype(jnp.float32)
        + jnp.dot(mixed_rows, project_out, preferred_element_type=jnp.float32)
    ).astype(jnp.bfloat16)
    grad_mixed = jnp.dot(cot_rows, project_out.T, preferred_element_type=jnp.float32).astype(
        jnp.bfloat16
    )
    grad_out = jnp.dot(mixed_rows.T, cot_rows, preferred_element_type=jnp.float32)
    next_grads = shifted(grad_mixed, "pts", -1)
    window_grad = lax.dynamic_slice_in_dim(
        jnp.concatenate([grad_mixed, next_grads], axis=0), offset, row_count, 0
    )
    grad_window = attend_backward(window_in, window_grad)
    spread = lax.dynamic_update_slice(
        jnp.zeros((row_count + PATCH, 3 * width), jnp.bfloat16), grad_window, (offset, jnp.int32(0))
    )
    returned = shifted(spread[row_count:], "pts", 1)
    grad_projected = spread[:row_count].at[:PATCH].add(returned)
    grad_in = jnp.dot(normed.T, grad_projected, preferred_element_type=jnp.float32)
    grad_normed = jnp.dot(grad_projected, project_in.T, preferred_element_type=jnp.float32)
    grad_scale = jnp.sum(grad_normed * unit_rows, axis=0)
    weighted = grad_normed * norm_gain
    branch = inverse * (
        weighted
        - jnp.mean(weighted, axis=-1, keepdims=True)
        - unit_rows * jnp.mean(weighted * unit_rows, axis=-1, keepdims=True)
    )
    grad_ordered = (cot_rows.astype(jnp.float32) + branch).astype(jnp.bfloat16)
    safe_position = jnp.clip(in_position, 0, row_count - 1)
    returning = jnp.where(
        in_position[:, None] >= 0, grad_ordered[safe_position], jnp.zeros((), jnp.bfloat16)
    )
    arrived = lax.all_to_all(returning, "pts", split_axis=0, concat_axis=0, tiled=True)
    safe_target = jnp.clip(target, 0, shard_count * slot_size - 1)
    grad_points = jnp.where(live_slot[:, None], arrived[safe_target], jnp.zeros((), jnp.bfloat16))
    summed_in, summed_out, summed_scale = lax.psum((grad_in, grad_out, grad_scale), ("pts", "rep"))
    factor = 1.0 / math.sqrt(total * lax.axis_size("rep"))
    return (
        block_rows[None],
        grad_points[None],
        summed_in * factor,
        summed_out * factor,
        summed_scale * factor,
    )


def solution(mesh):
    return jax.shard_map(
        on_device,
        mesh=mesh,
        in_specs=(
            P("rep", "pts", None),
            P("rep", "pts"),
            P("rep", "pts"),
            P("rep"),
            P(),
            P(),
            P(),
            P("rep", "pts", None),
        ),
        out_specs=(P("rep", "pts", None), P("rep", "pts", None), P(), P(), P()),
        check_vma=False,
    )
```

profile of v0, /device:TPU:97, one launch (start us, length us, event | category | flops | bytes accessed | tf_op | source)
XLA Modules:
  0.0 731.6 jit_solution(16514262569084634420)
XLA Ops:
  8.8 18.1 %reduce-window.6 = s32[64,16,128]{2,1,0:T(8,128)S(1)} reduce-window(s32[64,16,128]{2,1,0:T(8,128)S(1)} %fusion.81, s32[]{:T(128)} %constant.143.clone.1), window={size=1x1x128 pad=0_0x0_0x127_0}, to_apply=%region_0.1 | reduce-window | flops 16646144 | bytes 1048580 | tf_op jit(solution)/shard_map/reduce-window
  28.9 8.0 %scatter_custom_fusion = s32[2048]{0:T(1024)S(1)} fusion(s32[2048]{0:T(1024)S(1)} %bitcast.195, s32[2048]{0:T(1024)S(1)} %get-tuple-element.159, s32[]{:T(128)} %constant.142.clone.1), kind=kCustom, calls=%fused_computation.164 | custom fusion | bytes 8196 | tf_op jit(solution)/shard_map/scatter | solution.py:127
  37.6 11.0 %all-to-all-start = ((s32[64,32,1]{1,2,0:T(1,128)}), s32[64,32,1]{1,2,0:T(1,128)S(1)}, u32[]{:S(2)}, u32[]{:S(2)}) async-start(s32[64,32,1]{1,2,0:T(1,128)} %bitcast.21), calls=%async_computation | async-start | bytes 65536 | tf_op jit(solution)/shard_map/all_to_all | solution.py:131
  48.6 11.0 %scatter_custom_fusion.1 = bf16[2048,512]{1,0:T(8,128)(2,1)} fusion(s32[2048]{0:T(1024)S(1)} %bitcast.196, bf16[1,2048,512]{2,1,0:T(8,128)(2,1)S(1)} %copy-done, bf16[]{:T(256)} %constant.141.clone.1), kind=kCustom, calls=%fused_computation.88 | custom fusion | bytes 4194306 | tf_op jit(solution)/shard_map/scatter | solution.py:124
  59.6 10.3 %all-to-all-start.1 = ((bf16[64,32,512]{2,1,0:T(8,128)(2,1)}), bf16[64,32,512]{2,1,0:T(8,128)(2,1)S(1)}, u32[]{:S(2)}, u32[]{:S(2)}) async-start(bf16[64,32,512]{2,1,0:T(8,128)(2,1)} %bitcast.182), calls=%async_computation.1 | async-start | bytes 4194304 | tf_op jit(solution)/shard_map/all_to_all | solution.py:130
  71.3 47.5 %all-to-all-done.1 = bf16[64,32,512]{2,1,0:T(8,128)(2,1)S(1)} async-done(((bf16[64,32,512]{2,1,0:T(8,128)(2,1)}), bf16[64,32,512]{2,1,0:T(8,128)(2,1)S(1)}, u32[]{:S(2)}, u32[]{:S(2)}) %all-to-all-start.1) | async-done | bytes 2097184 | tf_op jit(solution)/shard_map/all_to_all | solution.py:130
  118.8 22.3 %scatter_custom_fusion.2 = bf16[1024,512]{1,0:T(8,128)(2,1)S(1)} fusion(s32[2048]{0:T(1024)S(1)} %bitcast.194, bf16[2048,512]{1,0:T(8,128)(2,1)S(1)} %bitcast.184, bf16[]{:T(256)} %constant.141.clone.1), kind=kCustom, calls=%fused_computation.113 | custom fusion | bytes 1048578 | tf_op jit(solution)/shard_map/scatter | solution.py:134
  142.5 3.5 convolution_convert_fusion.2
  149.2 46.3 %collective-permute-done.2 = bf16[1024,512]{1,0:T(8,128)(2,1)} collective-permute-done((bf16[1024,512]{1,0:T(8,128)(2,1)S(1)}, bf16[1024,512]{1,0:T(8,128)(2,1)}, u32[]{:S(2)}, u32[]{:S(2)}) %collective-permute-start.2) | collective-permute-done | bytes 1048608 | tf_op jit(solution)/shard_map/ppermute | solution.py:18
  199.3 6.6 fusion.50
  206.0 4.6 copy.47
  210.6 3.7 slice_bitcast_fusion
  218.1 2.7 copy.48
  220.8 85.2 %while.23 = (s32[]{:T(128)}, bf16[8,3,1,1024,64]{3,4,0,1,2:T(8,128)(2,1)}, bf16[8,1,1024,64]{3,2,1,0:T(8,128)(2,1)}, bf16[8,1,1024,64]{3,2,1,0:T(8,128)(2,1)S(1)...) while((s32[]{:T(128)}, bf16[8,3,1,1024,64]{3,4,0,1,2:T(8,128)(2,1)}, ...), condition=%wide.region_16.17_spmd, body=%wide.region_12.16_spmd.sunk | while | flops 694481920 | bytes 38451300 | solution.py:92
  305.9 3.5 broadcast_in_dim.94
  309.4 32.0 %dynamic_update_slice.11 = bf16[2048,1536]{0,1:T(8,128)(2,1)} dynamic-update-slice(bf16[2048,1536]{0,1:T(8,128)(2,1)} %broadcast_in_dim.94, bf16[1024,1536]{0,1:T(8,128)(2,1)} %bitcast.183, s32[]{:T(128)S(6)} %select_n.180, s32[]{:T(128)} %constant.143.clone.1) | dynamic-update-slice | bytes 6291460 | tf_op jit(solution)/shard_map/dynamic_update_slice | solution.py:161
  341.4 3.9 slice.55
  345.3 40.1 %while.22 = (s32[]{:T(128)}, bf16[8,1,1024,64]{2,3,1,0:T(8,128)(2,1)}, bf16[8,1,1024,64]{3,2,1,0:T(8,128)(2,1)}, bf16[8,1,1024,64]{3,2,1,0:T(8,128)(2,1)S(1)}, bf16[8,1,1024,64]{3,2,1,0:T(8,128)(2,1)}, /*index=5*/s32[]{:T(128)}) while((s32[]{:T(128)}, bf16[8,1,1024,64]{2,3,1,0:T(8,128)(2,1)}, bf16[8,1,1024,64]{3,2,1,0:T(8,128)(2,1)}, ...), condition=%wide.region_11.12_spmd, body=%wide.region_8.11_spmd.sunk | while | flops 277936128 | bytes 13523021 | solution.py:56
  352.7 2.6 fusion.121
  357.7 2.6 fusion.121
  386.3 5.2 fusion.63
  392.5 9.2 %gather_fusion = bf16[2048,512]{1,0:T(8,128)(2,1)} fusion(bf16[1024,512]{1,0:T(8,128)(2,1)S(1)} %fusion.62, s32[2048]{0:T(1024)S(1)} %copy-done.6), kind=kCustom, calls=%fused_computation | custom fusion | bytes 4202496 | tf_op jit(solution)/shard_map/gather | solution.py:178
  401.7 2.7 broadcast_select_fusion
  404.5 8.9 %all-to-all-start.2 = ((bf16[64,32,512]{2,1,0:T(8,128)(2,1)}), bf16[64,32,512]{2,1,0:T(8,128)(2,1)}, u32[]{:S(2)}, u32[]{:S(2)}) async-start(bf16[64,32,512]{2,1,0:T(8,128)(2,1)} %broadcast_select_fusion), calls=%async_computation.2 | async-start | bytes 4194304 | tf_op jit(solution)/shard_map/all_to_all | solution.py:180
  413.5 3.1 fusion.71
  416.5 6.7 fusion.75
  424.6 3.5 fusion.68
  428.1 81.9 %psum.23 = f32[512]{0:T(512)S(1)} all-reduce(f32[512]{0:T(512)S(1)} %get-tuple-element.119), channel_id=1, replica_groups=mesh['pts'=64,'rep'=4] {'pts','rep'}, use_global_device_ids=true, to_apply=%region_22.23 | all-reduce | flops 512 | bytes 4096 | tf_op jit(solution)/shard_map/psum | solution.py:183
  510.6 193.6 %all-reduce.3.cloned.1.call-done = (f32[512,1536]{1,0:T(8,128)}, f32[512,512]{1,0:T(8,128)}) async-done(((f32[512,1536]{1,0:T(8,128)}, f32[512,512]{1,0:T(8,128)}), (f32[512,1536]{1,0:T(8,128)}, f32[512,512]{1,0:T(8,128)})) %all-reduce.3.cloned.1.call-update) | async-done | bytes 4194320 | tf_op jit(solution)/shard_map/psum | solution.py:183
  706.5 3.8 broadcast_multiply_fusion
  710.3 11.3 %gather_fusion.1 = bf16[2048,512]{1,0:T(8,128)(2,1)} fusion(bf16[2048,512]{1,0:T(8,128)(2,1)} %bitcast.44, s32[2048]{0:T(1024)S(1)} %broadcast_clamp_fusion), kind=kCustom, calls=%fused_computation.1 | custom fusion | bytes 4202496 | tf_op jit(solution)/shard_map/gather | solution.py:182
  721.6 2.7 bitcast_select_fusion
  (161 shorter events, 142.2 us)
Async XLA Ops:
  7.2 41.4 %copy-start = (bf16[1,2048,512]{2,1,0:T(8,128)(2,1)S(1)}, bf16[1,2048,512]{2,1,0:T(8,128)(2,1)}, u32[]{:S(2)}) copy-start(bf16[1,2048,512]{2,1,0:T(8,128)(2,1)} %param.16) | copy-start | bytes 6291460
  8.7 19.2 %copy-start.4 = (s32[1,2048]{1,0:T(1,128)S(1)}, s32[1,2048]{1,0:T(1,128)}, u32[]{:S(2)}) copy-start(s32[1,2048]{1,0:T(1,128)} %param.18) | copy-start | bytes 24580
  37.6 22.0 %all-to-all-start = ((s32[64,32,1]{1,2,0:T(1,128)}), s32[64,32,1]{1,2,0:T(1,128)S(1)}, u32[]{:S(2)}, u32[]{:S(2)}) async-start(s32[64,32,1]{1,2,0:T(1,128)} %bitcast.21), calls=%async_computation | async-start | bytes 65536 | tf_op jit(solution)/shard_map/all_to_all | solution.py:131
  59.6 59.2 %all-to-all-start.1 = ((bf16[64,32,512]{2,1,0:T(8,128)(2,1)}), bf16[64,32,512]{2,1,0:T(8,128)(2,1)S(1)}, u32[]{:S(2)}, u32[]{:S(2)}) async-start(bf16[64,32,512]{2,1,0:T(8,128)(2,1)} %bitcast.182), calls=%async_computation.1 | async-start | bytes 4194304 | tf_op jit(solution)/shard_map/all_to_all | solution.py:130
  69.9 72.0 %copy-start.8 = (f32[512]{0:T(512)S(1)}, f32[512]{0:T(512)}, u32[]{:S(2)}) copy-start(f32[512]{0:T(512)} %param.20) | copy-start | bytes 6148
  141.1 1.4 copy-start.9
  142.5 3.6 copy-start.2
  142.5 3.6 copy-start.12
  146.1 53.3 %collective-permute-start = (bf16[1024,1536]{1,0:T(8,128)(2,1)}, bf16[1024,1536]{1,0:T(8,128)(2,1)}, u32[]{:S(2)}, u32[]{:S(2)}) collective-permute-start(bf16[1024,1536]{1,0:T(8,128)(2,1)} %convolution_convert_fusion.2), channel_id=1, source_target_pairs={{0,252},{4,0},{8,4},{12,8},{16,12},{20,16},{24,20},{28,24},{32,28}... | collective-permute-start | bytes 9437192 | tf_op jit(solution)/shard_map/ppermute | solution.py:18
  146.8 48.7 %collective-permute-start.2 = (bf16[1024,512]{1,0:T(8,128)(2,1)S(1)}, bf16[1024,512]{1,0:T(8,128)(2,1)}, u32[]{:S(2)}, u32[]{:S(2)}) collective-permute-start(bf16[1024,512]{1,0:T(8,128)(2,1)S(1)} %convolution_convert_fusion.3), channel_id=1, source_target_pairs={{0,252},{4,0},{8,4},{12,8},{16,12},{20,16},{24,20},{28,24},{32,28}... | collective-permute-start | bytes 3145736 | tf_op jit(solution)/shard_map/ppermute | solution.py:18
  345.3 41.0 %collective-permute-start.3 = (bf16[1024,1536]{0,1:T(8,128)(2,1)}, bf16[1024,1536]{0,1:T(8,128)(2,1)}, u32[]{:S(2)}, u32[]{:S(2)}) collective-permute-start(bf16[1024,1536]{0,1:T(8,128)(2,1)} %slice.55), channel_id=1, source_target_pairs={{0,4},{4,8},{8,12},{12,16},{16,20},{20,24},{24,28},{28,32},{32,36}... | collective-permute-start | bytes 9437192 | tf_op jit(solution)/shard_map/ppermute | solution.py:18
  385.4 6.1 copy-start.3
  385.4 28.1 %collective-permute-start.1 = (bf16[1024,512]{0,1:T(8,128)(2,1)}, bf16[1024,512]{0,1:T(8,128)(2,1)}, u32[]{:S(2)}, u32[]{:S(2)}) collective-permute-start(bf16[1024,512]{0,1:T(8,128)(2,1)} %bitcast.197), channel_id=1, source_target_pairs={{0,4},{4,8},{8,12},{12,16},{16,20},{20,24},{24,28},{28,32},{32,36}... | collective-permute-start | bytes 3145736 | tf_op jit(solution)/shard_map/ppermute | solution.py:18
  391.5 1.0 copy-start.6
  392.5 9.2 %copy-start.5 = (pred[64,32]{1,0:T(8,128)(4,1)S(1)}, pred[64,32]{1,0:T(8,128)(4,1)}, u32[]{:S(2)}) copy-start(pred[64,32]{1,0:T(8,128)(4,1)} %copy.52) | copy-start | bytes 6148
  404.5 9.0 %copy-start.10 = (bf16[8,1,1024,64]{2,3,1,0:T(8,128)(2,1)S(1)}, bf16[8,1,1024,64]{2,3,1,0:T(8,128)(2,1)}, u32[]{:S(2)}) copy-start(bf16[8,1,1024,64]{2,3,1,0:T(8,128)(2,1)} %get-tuple-element.84) | copy-start | bytes 3145732
  404.5 305.9 %all-to-all-start.2 = ((bf16[64,32,512]{2,1,0:T(8,128)(2,1)}), bf16[64,32,512]{2,1,0:T(8,128)(2,1)}, u32[]{:S(2)}, u32[]{:S(2)}) async-start(bf16[64,32,512]{2,1,0:T(8,128)(2,1)} %broadcast_select_fusion), calls=%async_computation.2 | async-start | bytes 4194304 | tf_op jit(solution)/shard_map/all_to_all | solution.py:180
  413.4 290.9 %all-reduce.3.cloned.1.call-start = ((), (), s32[]{:S(2)}) async-start(), calls=%async_computation.3 | async-start | bytes 8388608 | tf_op jit(solution)/shard_map/psum | solution.py:183
  423.2 0.7 copy-start.7
  423.2 1.2 copy-start.11
  423.2 1.4 copy-start.13
  710.3 14.0 %copy-start.1 = (bf16[1,2048,512]{2,1,0:T(8,128)(2,1)S(1)}, bf16[1,2048,512]{2,1,0:T(8,128)(2,1)}, u32[]{:S(2)}) copy-start(bf16[1,2048,512]{2,1,0:T(8,128)(2,1)} %param.16) | copy-start | bytes 6291460
Sparse Core Ops, SparseCore 0:
  423.4 280.8 all-reduce.2
where the time goes:
time: 742 us; the launch traced here: 732 us
  waiting for transfers between devices  287 us (39%)
  local copies, waits for them, and re-layouts  122 us (16%)
  matrix products  120 us (16%)
  blocking collectives  81.9 us (11%)
  other arithmetic  72.6 us (10%)
  starting transfers between devices  31.5 us (4%)
  between operations  16.2 us (2%)
    psum x1, waiting for transfers between devices, on_device(): lax.psum((grad_in, grad_out, grad_scale), ('pts', 'rep'))  194 us
    psum x1, blocking collectives, on_device(): lax.psum((grad_in, grad_out, grad_scale), ('pts', 'rep'))  81.9 us
    all_to_all x1, waiting for transfers between devices, on_device(): lax.all_to_all(outgoing, 'pts', split_axis=0, concat_axis=0, tiled=True)  47.5 us
    ppermute x4, waiting for transfers between devices, shifted(): return lax.ppermute(value, axis, pairs)  46.3 us
    dynamic_update_slice x1, local copies, waits for them, and re-layouts, on_device(): lax.dynamic_update_slice(jnp.zeros((row_count + PATCH, 3 * width), jnp.bf...  32 us
    scatter x1, local copies, waits for them, and re-layouts, on_device(): jnp.zeros((row_count, width), jnp.bfloat16).at[placed]  22.3 us
    dot_general x8, matrix products, head_forward(): jnp.einsum('gqk,gkd->gqd', attention, value_rows, preferred_element_type=...  20.9 us
    another operation x2, other arithmetic  18.3 us
  transfers between devices with their start and end apart: 8, of which 3 were waited for; matrix products, arithmetic and copies ran while one was open for 13% of the time, Pallas kernels for 0%

commit v1 on v0

v1 whole, which is shorter than its diff:
```python
import functools
import math

import jax
import jax.numpy as jnp
from jax import lax
from jax.experimental import pallas as pl
from jax.experimental.pallas import tpu as pltpu
from jax.sharding import PartitionSpec as P

HEAD_DIM = 64
PATCH = 1024
EPSILON = 1e-05
MESH = pl.DeviceIdType.MESH
BF16 = jnp.bfloat16
F32 = jnp.float32
NT = (((1,), (1,)), ((), ()))
TN = (((0,), (0,)), ((), ()))


def params(**kw):
    return pltpu.CompilerParams(vmem_limit_bytes=56 << 20, **kw)


def shifted(value, axis, steps):
    count = lax.axis_size(axis)
    pairs = [(source, (source + steps) % count) for source in range(count)]
    return lax.ppermute(value, axis, pairs)


def place_kernel(dest_ref, src_ref, out_ref):
    block, depth = out_ref.shape[0], src_ref.shape[0]
    row = lax.broadcasted_iota(jnp.int32, (block, depth), 0) + pl.program_id(0) * block
    hot = jnp.where(row == dest_ref[...], 1.0, 0.0).astype(BF16)
    out_ref[...] = jnp.dot(hot, src_ref[...], preferred_element_type=F32).astype(BF16)


def place(dest, src, rows, block=256):
    depth, width = src.shape
    return pl.pallas_call(
        place_kernel,
        grid=(rows // block,),
        in_specs=[
            pl.BlockSpec((1, depth), lambda i: (0, 0)),
            pl.BlockSpec((depth, width), lambda i: (0, 0)),
        ],
        out_specs=pl.BlockSpec((block, width), lambda i: (i, 0)),
        out_shape=jax.ShapeDtypeStruct((rows, width), BF16),
        compiler_params=params(),
        name="place",
    )(dest.reshape(1, depth), src)


def fetch_kernel(index_ref, src_ref, out_ref):
    block, depth = out_ref.shape[0], src_ref.shape[0]
    column = lax.broadcasted_iota(jnp.int32, (block, depth), 1)
    hot = jnp.where(column == index_ref[...], 1.0, 0.0).astype(BF16)
    out_ref[...] = jnp.dot(hot, src_ref[...], preferred_element_type=F32).astype(BF16)


def fetch(index, src, block=256):
    depth, width = src.shape
    rows = index.shape[0]
    return pl.pallas_call(
        fetch_kernel,
        grid=(rows // block,),
        in_specs=[
            pl.BlockSpec((block, 1), lambda i: (i, 0)),
            pl.BlockSpec((depth, width), lambda i: (0, 0)),
        ],
        out_specs=pl.BlockSpec((block, width), lambda i: (i, 0)),
        out_shape=jax.ShapeDtypeStruct((rows, width), BF16),
        compiler_params=params(),
        name="fetch",
    )(index.reshape(rows, 1), src)


def unit_of(values):
    centre = jnp.mean(values, axis=-1, keepdims=True)
    deviation = values - centre
    inverse = lax.rsqrt(jnp.mean(deviation * deviation, axis=-1, keepdims=True) + EPSILON)
    return deviation * inverse, inverse


def project_kernel(limit_ref, own_ref, next_ref, gain_ref, weight_ref, win_ref, normed_ref, qkv_ref):
    block = own_ref.shape[0]
    row = lax.broadcasted_iota(jnp.int32, own_ref.shape, 0) + pl.program_id(0) * block
    values = jnp.where(
        row < limit_ref[0], own_ref[...].astype(F32), next_ref[...].astype(F32)
    )
    unit, _ = unit_of(values)
    normed = (unit * gain_ref[...]).astype(BF16)
    win_ref[...] = values.astype(BF16)
    normed_ref[...] = normed
    qkv_ref[...] = jnp.dot(normed, weight_ref[...], preferred_element_type=F32).astype(BF16)


def project(limit, own, following, gain, weight, block=256):
    rows, width = own.shape
    wide = weight.shape[1]
    tile = pl.BlockSpec((block, width), lambda i: (i, 0))
    return pl.pallas_call(
        project_kernel,
        grid=(rows // block,),
        in_specs=[
            pl.BlockSpec(memory_space=pltpu.SMEM),
            tile,
            tile,
            pl.BlockSpec((1, width), lambda i: (0, 0)),
            pl.BlockSpec((width, wide), lambda i: (0, 0)),
        ],
        out_specs=[tile, tile, pl.BlockSpec((block, wide), lambda i: (i, 0))],
        out_shape=[
            jax.ShapeDtypeStruct((rows, width), BF16),
            jax.ShapeDtypeStruct((rows, width), BF16),
            jax.ShapeDtypeStruct((rows, wide), BF16),
        ],
        compiler_params=params(),
        name="project",
    )(limit, own, following, gain.reshape(1, width), weight)


def attend_kernel(q_ref, k_ref, v_ref, g_ref, mixed_ref, d_ref, dk_ref, dv_ref, *, chunk):
    keys, values = k_ref[...], v_ref[...]
    lane = lax.broadcasted_iota(jnp.int32, (1, 128), 1)
    line = lax.broadcasted_iota(jnp.int32, (128, 1), 0)
    lanes = [jnp.where(lane < HEAD_DIM, 1.0, 0.0), jnp.where(lane < HEAD_DIM, 0.0, 1.0)]
    lines = [jnp.where(line < HEAD_DIM, 1.0, 0.0), jnp.where(line < HEAD_DIM, 0.0, 1.0)]
    keys_t = keys.astype(F32).T
    values_t = values.astype(F32).T
    keys_t = [(keys_t * m).astype(BF16) for m in lines]
    values_t = [(values_t * m).astype(BF16) for m in lines]
    dk_ref[...] = jnp.zeros_like(dk_ref)
    dv_ref[...] = jnp.zeros_like(dv_ref)

    def step(at, carry):
        window = pl.ds(pl.multiple_of(at * chunk, chunk), chunk)
        q_all = q_ref[window, :].astype(F32) * HEAD_DIM ** (-0.5)
        g_all = g_ref[window, :].astype(F32)
        mixed_t = jnp.zeros((128, chunk), F32)
        dq_t = jnp.zeros((128, chunk), F32)
        for head in range(2):
            q = (q_all * lanes[head]).astype(BF16)
            g = (g_all * lanes[head]).astype(BF16)
            logits = lax.dot_general(keys, q, NT, preferred_element_type=F32)
            power = jnp.exp(logits - jnp.max(logits, axis=0, keepdims=True))
            share = power * (1.0 / jnp.sum(power, axis=0, keepdims=True))
            share_b = share.astype(BF16)
            mixed_t += jnp.dot(values_t[head], share_b, preferred_element_type=F32)
            dv_ref[...] += jnp.dot(share_b, g, preferred_element_type=F32)
            dshare = lax.dot_general(values, g, NT, preferred_element_type=F32)
            dot = jnp.sum(dshare * share, axis=0, keepdims=True)
            dlogits = (share * (dshare - dot)).astype(BF16)
            dq_t += jnp.dot(keys_t[head], dlogits, preferred_element_type=F32)
            dk_ref[...] += jnp.dot(dlogits, q, preferred_element_type=F32)
        mixed_ref[window, :] = mixed_t.T.astype(BF16)
        d_ref[0, window, :] = (dq_t * HEAD_DIM ** (-0.5)).T.astype(BF16)
        return carry

    lax.fori_loop(0, q_ref.shape[0] // chunk, step, 0)
    d_ref[1] = dk_ref[...].astype(BF16)
    d_ref[2] = dv_ref[...].astype(BF16)


def attend(qkv, grads, chunk=256):
    rows, width = grads.shape
    pairs = width // 128
    return pl.pallas_call(
        functools.partial(attend_kernel, chunk=chunk),
        grid=(pairs,),
        in_specs=[
            pl.BlockSpec((rows, 128), lambda j: (0, j)),
            pl.BlockSpec((rows, 128), lambda j: (0, pairs + j)),
            pl.BlockSpec((rows, 128), lambda j: (0, 2 * pairs + j)),
            pl.BlockSpec((rows, 128), lambda j: (0, j)),
        ],
        out_specs=[
            pl.BlockSpec((rows, 128), lambda j: (0, j)),
            pl.BlockSpec((3, rows, 128), lambda j: (0, 0, j)),
        ],
        out_shape=[
            jax.ShapeDtypeStruct((rows, width), BF16),
            jax.ShapeDtypeStruct((3, rows, width), BF16),
        ],
        scratch_shapes=[pltpu.VMEM((rows, 128), F32), pltpu.VMEM((rows, 128), F32)],
        compiler_params=params(),
        name="attend",
    )(qkv, qkv, qkv, grads)


def input_grad_kernel(d_ref, weight_ref, win_ref, cot_ref, gain_ref, out_ref, scale_ref):
    width = win_ref.shape[1]
    grad = jnp.zeros(win_ref.shape, F32)
    for part in range(3):
        grad += lax.dot_general(
            d_ref[part],
            weight_ref[:, part * width : (part + 1) * width],
            NT,
            preferred_element_type=F32,
        )
    unit, inverse = unit_of(win_ref[...].astype(F32))
    product = grad * unit

    @pl.when(pl.program_id(0) == 0)
    def _():
        scale_ref[...] = jnp.zeros_like(scale_ref)

    scale_ref[...] += jnp.sum(product, axis=0, keepdims=True)
    weighted = grad * gain_ref[...]
    branch = inverse * (
        weighted
        - jnp.mean(weighted, axis=-1, keepdims=True)
        - unit * jnp.mean(product * gain_ref[...], axis=-1, keepdims=True)
    )
    out_ref[...] = (cot_ref[...].astype(F32) + branch).astype(BF16)


def input_grad(d, weight, win, cot, gain, block=256):
    rows, width = win.shape
    tile = pl.BlockSpec((block, width), lambda i: (i, 0))
    return pl.pallas_call(
        input_grad_kernel,
        grid=(rows // block,),
        in_specs=[
            pl.BlockSpec((3, block, width), lambda i: (0, i, 0)),
            pl.BlockSpec(weight.shape, lambda i: (0, 0)),
            tile,
            tile,
            pl.BlockSpec((1, width), lambda i: (0, 0)),
        ],
        out_specs=[tile, pl.BlockSpec((1, width), lambda i: (0, 0))],
        out_shape=[
            jax.ShapeDtypeStruct((rows, width), BF16),
            jax.ShapeDtypeStruct((1, width), F32),
        ],
        compiler_params=params(),
        name="input_grad",
    )(d, weight, win, cot, gain.reshape(1, width))


def weight_grad_kernel(normed_ref, d_ref, mixed_ref, cot_ref, out_ref):
    @pl.when(pl.program_id(0) < 3)
    def _():
        out_ref[...] = lax.dot_general(
            normed_ref[...], d_ref[0], TN, preferred_element_type=F32
        ).astype(BF16)

    @pl.when(pl.program_id(0) == 3)
    def _():
        out_ref[...] = lax.dot_general(
            mixed_ref[...], cot_ref[...], TN, preferred_element_type=F32
        ).astype(BF16)


def weight_grad(normed, d, mixed, cot):
    rows, width = normed.shape
    whole = pl.BlockSpec((rows, width), lambda j: (0, 0))
    return pl.pallas_call(
        weight_grad_kernel,
        grid=(4,),
        in_specs=[
            whole,
            pl.BlockSpec((1, rows, width), lambda j: (jnp.minimum(j, 2), 0, 0)),
            whole,
            whole,
        ],
        out_specs=pl.BlockSpec((width, width), lambda j: (0, j)),
        out_shape=jax.ShapeDtypeStruct((width, 4 * width), BF16),
        compiler_params=params(),
        name="weight_grad",
    )(normed, d, mixed, cot)


def reduce_kernel(
    sizes, g_ref, s_ref, out_ref, t_ref,
    half, in_core, quarter, in_y, band, in_z, piece, in_x,
    small, small_core, small_y, small_z, small_x, send_sem, recv_sem, small_send, small_recv,
):
    nx, ny, nz = sizes
    rows, wide = g_ref.shape
    half_w, part_w = wide // 2, wide // 2 // ny
    band_h, piece_h = rows // nz, rows // nz // nx
    me = lax.axis_index("pts")
    y = lax.axis_index("rep")
    core = lax.rem(me, 2)
    z = lax.rem(me // 2, nz)
    x = me // (2 * nz)

    def at(x_, y_, z_, core_):
        return {"pts": (x_ * nz + z_) * 2 + core_, "rep": y_}

    by_core = [(at(x, y, z, 1 - core), 1 - core)]
    by_y = [(at(x, lax.rem(y + k, ny), z, core), lax.rem(y + k, ny)) for k in range(1, ny)]
    by_z = [(at(x, y, lax.rem(z + k, nz), core), lax.rem(z + k, nz)) for k in range(1, nz)]
    by_x = [(at(lax.rem(x + k, nx), y, z, core), lax.rem(x + k, nx)) for k in range(1, nx)]
    everyone = by_core + by_y + by_z + by_x
    barrier = pltpu.get_barrier_semaphore()
    for device, _ in everyone:
        pl.semaphore_signal(barrier, inc=1, device_id=device, device_id_type=MESH)
    pl.semaphore_wait(barrier, len(everyone))

    def send(src, dst, slot, device, sems=(send_sem, recv_sem)):
        copy = pltpu.make_async_remote_copy(
            src_ref=src, dst_ref=dst, send_sem=sems[0].at[slot], recv_sem=sems[1].at[slot],
            device_id=device, device_id_type=MESH,
        )
        copy.start()
        return copy

    def columns(index, width, base=0):
        return pl.ds(pl.multiple_of(base + index * width, width), width)

    def lines(index, height):
        return pl.ds(pl.multiple_of(index * height, height), height)

    used = [0]

    def exchange(peers, pick, land, small_slots, mine):
        small_slots[mine] = small[...]
        copies = []
        for k, (device, index) in enumerate(peers):
            slot = used[0] + k
            copies.append(send(pick(index), land(k), slot, device))
            copies.append(send(small, small_slots.at[mine], slot, device, (small_send, small_recv)))
        used[0] += len(peers)
        for copy in copies:
            copy.wait()
        total = small_slots[0]
        for k in range(1, len(peers) + 1):
            total += small_slots[k]
        small[...] = total

    small[...] = s_ref[...]
    exchange(by_core, lambda i: g_ref.at[:, columns(i, half_w)], lambda k: in_core, small_core, core)
    own = g_ref[:, columns(core, half_w)]
    half[...] = (own.astype(F32) + in_core[...].astype(F32)).astype(BF16)
    exchange(by_y, lambda i: half.at[:, columns(i, part_w)], lambda k: in_y.at[k], small_y, y)
    total = half[:, columns(y, part_w)].astype(F32)
    for k in range(ny - 1):
        total += in_y[k].astype(F32)
    quarter[...] = total.astype(BF16)
    exchange(by_z, lambda i: quarter.at[lines(i, band_h), :], lambda k: in_z.at[k], small_z, z)
    total = quarter[lines(z, band_h), :].astype(F32)
    for k in range(nz - 1):
        total += in_z[k].astype(F32)
    band[...] = total.astype(BF16)
    exchange(by_x, lambda i: band.at[lines(i, piece_h), :], lambda k: in_x.at[k], small_x, x)
    total = band[lines(x, piece_h), :].astype(F32)
    for k in range(nx - 1):
        total += in_x[k].astype(F32)
    t_ref[...] = small[...]

    column = columns(core * ny + y, part_w)
    first = pl.multiple_of(z * band_h + x * piece_h, piece_h)
    out_ref[pl.ds(first, piece_h), column] = total.astype(BF16)

    def spread(peers, view):
        copies = [send(view, view, used[0] + k, device) for k, (device, _) in enumerate(peers)]
        used[0] += len(peers)
        for copy in copies:
            copy.wait()

    spread(by_x, out_ref.at[pl.ds(first, piece_h), column])
    spread(by_z, out_ref.at[lines(z, band_h), column])
    spread(by_y, out_ref.at[:, column])
    spread(by_core, out_ref.at[:, columns(core, half_w)])


def reduce_all(grads, small, sizes):
    nx, ny, nz = sizes
    rows, wide = grads.shape
    peers = 1 + (ny - 1) + (nz - 1) + (nx - 1)
    part = wide // 2 // ny
    vmem = pl.BlockSpec(memory_space=pltpu.VMEM)
    buffers = [
        (rows, wide // 2), (rows, wide // 2),
        (rows, part), (ny - 1, rows, part),
        (rows // nz, part), (nz - 1, rows // nz, part),
        (rows // nz // nx, part), (nx - 1, rows // nz // nx, part),
    ]
    return pl.pallas_call(
        functools.partial(reduce_kernel, sizes),
        in_specs=[vmem, vmem],
        out_specs=[vmem, vmem],
        out_shape=[
            jax.ShapeDtypeStruct(grads.shape, BF16),
            jax.ShapeDtypeStruct(small.shape, F32),
        ],
        scratch_shapes=[pltpu.VMEM(shape, BF16) for shape in buffers]
        + [pltpu.VMEM(small.shape, F32)]
        + [pltpu.VMEM((n,) + small.shape, F32) for n in (2, ny, nz, nx)]
        + [
            pltpu.SemaphoreType.DMA((2 * peers,)),
            pltpu.SemaphoreType.DMA((2 * peers,)),
            pltpu.SemaphoreType.DMA((peers,)),
            pltpu.SemaphoreType.DMA((peers,)),
        ],
        compiler_params=params(collective_id=0, has_side_effects=True),
        name="reduce_all",
    )(grads, small)


def route_slots(rank_row, point_count, total, row_count, shard_count, send_size, offset):
    slot_total = rank_row.shape[0]
    index = jnp.arange(slot_total, dtype=jnp.int32)
    live_slot = index < point_count
    moved = rank_row % total
    target_shard = jnp.where(live_slot, moved // row_count, shard_count)
    matches = target_shard[:, None] == jnp.arange(shard_count, dtype=jnp.int32)[None, :]
    earlier = (index[:, None] > index[None, :]).astype(BF16)
    before = jnp.dot(earlier, matches.astype(BF16), preferred_element_type=F32)
    ordinal = jnp.sum(jnp.where(matches, before, 0.0), axis=1).astype(jnp.int32)
    target = jnp.where(live_slot, target_shard * send_size + ordinal, shard_count * send_size)
    return target, (moved % row_count - offset) % row_count


def on_device(
    sizes, points, counts, hilbert_rank, patch_shift, norm_gain, project_in, project_out, cotangent
):
    shard_count = lax.axis_size("pts")
    row_count = cotangent.shape[1]
    width = points.shape[2]
    slot_total = points.shape[1]
    slot_size = slot_total // shard_count
    total = row_count * shard_count
    offset = patch_shift[0]
    limit = row_count - offset
    own_row = jnp.arange(row_count, dtype=jnp.int32)[:, None] < limit

    cot_rows = cotangent[0]
    cot_rolled = lax.dynamic_slice_in_dim(
        jnp.concatenate([cot_rows, cot_rows], axis=0), offset, row_count, 0
    )
    cot_next = shifted(cot_rolled, "pts", -1)

    target, position = route_slots(
        hilbert_rank[0], counts[0, 0], total, row_count, shard_count, slot_size, offset
    )
    slot = jnp.arange(slot_total, dtype=jnp.int32)
    out_position = jnp.max(
        jnp.where(target[:, None] == slot[None, :], position[:, None], -1), axis=0
    )
    outgoing = place(target, points[0], slot_total)
    in_position = lax.all_to_all(
        out_position.reshape(shard_count, slot_size), "pts", split_axis=0, concat_axis=0, tiled=True
    ).reshape(slot_total)
    incoming = lax.all_to_all(
        outgoing.reshape(shard_count, slot_size, width), "pts", split_axis=0, concat_axis=0, tiled=True
    ).reshape(slot_total, width)

    cot_window = jnp.where(own_row, cot_rolled, cot_next)
    grad_mixed = jnp.dot(cot_window, project_out.T, preferred_element_type=F32).astype(BF16)

    rolled = place(in_position, incoming, row_count)
    rolled_next = shifted(rolled, "pts", -1)
    window, normed, qkv = project(limit.reshape(1), rolled, rolled_next, norm_gain, project_in)
    mixed, d_qkv = attend(qkv, grad_mixed)
    grad_window, scale = input_grad(d_qkv, project_in, window, cot_window, norm_gain)
    grad_back = shifted(grad_window, "pts", 1)

    partial = weight_grad(normed, d_qkv, mixed, cot_window)
    block_window = (
        window.astype(F32) + jnp.dot(mixed, project_out, preferred_element_type=F32)
    ).astype(BF16)

    grad_rolled = jnp.where(own_row, grad_window, grad_back)
    returning = fetch(in_position, grad_rolled)
    returning, partial, scale, block_window = lax.optimization_barrier(
        (returning, partial, scale, block_window)
    )
    arrived = lax.all_to_all(
        returning.reshape(shard_count, slot_size, width), "pts", split_axis=0, concat_axis=0, tiled=True
    ).reshape(slot_total, width)
    block_back = shifted(block_window, "pts", 1)

    small = jnp.zeros((8, 128), F32).at[: width // 128].set(scale.reshape(width // 128, 128))
    summed, small = reduce_all(partial, small, sizes)

    block_rolled = jnp.where(own_row, block_window, block_back)
    block_rows = lax.dynamic_slice_in_dim(
        jnp.concatenate([block_rolled, block_rolled], axis=0), limit, row_count, 0
    )
    grad_points = fetch(target, arrived)
    factor = 1.0 / math.sqrt(total * lax.axis_size("rep"))
    return (
        block_rows[None],
        grad_points[None],
        summed[:, : 3 * width].astype(F32) * factor,
        summed[:, 3 * width :].astype(F32) * factor,
        small[: width // 128].reshape(width) * factor,
    )


def solution(mesh):
    spread = mesh.shape["pts"]
    sizes = {64: (4, 4, 8), 8: (2, 2, 2)}[spread]
    return jax.shard_map(
        functools.partial(on_device, sizes),
        mesh=mesh,
        in_specs=(
            P("rep", "pts", None),
            P("rep", "pts"),
            P("rep", "pts"),
            P("rep"),
            P(),
            P(),
            P(),
            P("rep", "pts", None),
        ),
        out_specs=(P("rep", "pts", None), P("rep", "pts", None), P(), P(), P()),
        check_vma=False,
    )
```

time: 742 us -> 317 us (0.43)
  waiting for transfers between devices: 287 us -> 56.4 us
  Pallas kernels: 0 us -> 178 us
  matrix products: 120 us -> 5.1 us
  local copies, waits for them, and re-layouts: 122 us -> 10.9 us
  blocking collectives: 81.9 us -> 0 us
  other arithmetic: 72.6 us -> 26.1 us
  between operations: 16.2 us -> 2.15 us
    psum x1 -> x0, waiting for transfers between devices: 194 us -> none  [on_device(): lax.psum((grad_in, grad_out, grad_scale), ('pts', 'rep'))]
    pallas_call x0 -> x9, Pallas kernels: none -> 178 us  [the longest x1 83.5 us: reduce_all(): pl.pallas_call(functools.partial(reduce_kernel, sizes), in_specs=[vmem, v...]
    dot_general x62 -> x3, matrix products: 120 us -> 5.1 us  [the longest x1 1.75 us: on_device(): jnp.dot(cot_window, project_out.T, preferred_element_type=F32).astype(BF16)]
    psum x1 -> x0, blocking collectives: 81.9 us -> none  [on_device(): lax.psum((grad_in, grad_out, grad_scale), ('pts', 'rep'))]
    scatter x3 -> x1, local copies, waits for them, and re-layouts: 41.3 us -> 0.6 us  [on_device(): jnp.zeros((8, 128), F32).at[:width // 128]]
    ppermute x4, waiting for transfers between devices: 46.3 us -> 11.7 us  [shifted(): return lax.ppermute(value, axis, pairs)]
    dynamic_update_slice x1 -> x0, local copies, waits for them, and re-layouts: 32 us -> none  [on_device(): lax.dynamic_update_slice(jnp.zeros((row_count + PATCH, 3 * width), jnp.bf...]
    gather x2 -> x0, local copies, waits for them, and re-layouts: 20.5 us -> none  [the longest x1 11.3 us: on_device(): arrived[safe_target]]
  transfers between devices with their start and end apart: 8 -> 7, of which waited for: 3 -> 4; matrix products, arithmetic and copies ran while one was open for 13% -> 10% of each run, Pallas kernels for 0% -> 33%
where the time goes in v1:
time: 317 us; the launch traced here: 314 us
  Pallas kernels  178 us (56%)
  waiting for transfers between devices  56.4 us (18%)
  starting transfers between devices  35.2 us (11%)
  other arithmetic  26.1 us (8%)
  local copies, waits for them, and re-layouts  10.9 us (3%)
  matrix products  5.1 us (2%)
    pallas_call x1, Pallas kernels, reduce_all(): pl.pallas_call(functools.partial(reduce_kernel, sizes), in_specs=[vmem, v...  83.5 us
    pallas_call x1, Pallas kernels, attend(): pl.pallas_call(functools.partial(attend_kernel, chunk=chunk), grid=(pairs...  44.8 us
    all_to_all x1, waiting for transfers between devices, on_device(): lax.all_to_all(outgoing.reshape(shard_count, slot_size, width), 'pts', sp...  44.6 us
    pallas_call x2, Pallas kernels, fetch(): pl.pallas_call(fetch_kernel, grid=(rows // block,), in_specs=[pl.BlockSpe...  17 us
    pallas_call x2, Pallas kernels, place(): pl.pallas_call(place_kernel, grid=(rows // block,), in_specs=[pl.BlockSpe...  13.2 us
    ppermute x4, waiting for transfers between devices, shifted(): return lax.ppermute(value, axis, pairs)  11.7 us
    all_to_all x1, starting transfers between devices, on_device(): lax.all_to_all(out_position.reshape(shard_count, slot_size), 'pts', split...  11 us
    all_to_all x1, starting transfers between devices, on_device(): lax.all_to_all(returning.reshape(shard_count, slot_size, width), 'pts', s...  10.8 us
  transfers between devices with their start and end apart: 7, of which 4 were waited for; matrix products, arithmetic and copies ran while one was open for 10% of the time, Pallas kernels for 33%

profile of v1, /device:TPU:97, one launch (start us, length us, event | category | flops | bytes accessed | tf_op | source)
XLA Modules:
  0.0 314.0 jit_solution(17092806844429405073)
XLA Ops:
  2.7 1.7 fusion.2
  4.4 3.3 %select_reduce_fusion = s32[2048]{0:T(1024)S(1)} fusion(s32[2048]{0:T(1024)S(1)} %get-tuple-element.44, s32[2048]{0:T(1024)S(1)} %add_select_fusion.6), kind=kLoop, calls=%fused_computation | loop fusion | flops 12580864 | bytes 24576 | tf_op jit(solution)/shard_map/reduce_max | solution.py:440
  8.4 11.0 %all-to-all-start = ((s32[64,1,32]{2,1,0:T(1,128)}), s32[64,1,32]{2,1,0:T(1,128)S(1)}, u32[]{:S(2)}, u32[]{:S(2)}) async-start(s32[64,1,32]{2,1,0:T(1,128)} %bitcast.3), calls=%async_computation | async-start | bytes 65536 | tf_op jit(solution)/shard_map/all_to_all | solution.py:444
  20.0 8.0 %place.2 = bf16[2048,512]{1,0:T(8,128)(2,1)} custom-call(s32[1,2048]{1,0:T(1,128)} %compare_select_fusion.5.dest_ref, bf16[2048,512]{1,0:T(8,128)(2,1)} %bitcast.42), custom_call_target="tpu_custom_call" | custom-call | tf_op jit(solution)/shard_map/place/pallas_call | solution.py:40
  28.1 10.3 %all-to-all-start.1 = ((bf16[64,32,512]{2,1,0:T(8,128)(2,1)}), bf16[64,32,512]{2,1,0:T(8,128)(2,1)S(1)}, u32[]{:S(2)}, u32[]{:S(2)}) async-start(bf16[64,32,512]{2,1,0:T(8,128)(2,1)} %bitcast.38), calls=%async_computation.1 | async-start | bytes 4194304 | tf_op jit(solution)/shard_map/all_to_all | solution.py:447
  38.4 3.2 %fusion.11 = bf16[1024,512]{1,0:T(8,128)(2,1)} fusion(s32[]{:T(128)S(6)} %select_n.135, bf16[1024,512]{1,0:T(8,128)(2,1)} %bitcast.40), kind=kLoop, calls=%fused_computation.28 | loop fusion | flops 2097152 | bytes 2097156 | tf_op jit(solution)/shard_map/concatenate | solution.py:432
  42.7 44.6 %all-to-all-done.1 = bf16[64,32,512]{2,1,0:T(8,128)(2,1)S(1)} async-done(((bf16[64,32,512]{2,1,0:T(8,128)(2,1)}), bf16[64,32,512]{2,1,0:T(8,128)(2,1)S(1)}, u32[]{:S(2)}, u32[]{:S(2)}) %all-to-all-start.1) | async-done | bytes 2097184 | tf_op jit(solution)/shard_map/all_to_all | solution.py:447
  87.3 1.3 copy-done.3
  88.6 5.2 %place.3.own_ref = bf16[1024,512]{1,0:T(8,128)(2,1)} custom-call(s32[1,2048]{1,0:T(1,128)} %reshape_reshape.7.dest_ref, bf16[2048,512]{1,0:T(8,128)(2,1)} %bitcast.39), custom_call_target="tpu_custom_call" | custom-call | tf_op jit(solution)/shard_map/place/pallas_call | solution.py:40
  93.8 4.1 %collective-permute-done.1 = bf16[1024,512]{1,0:T(8,128)(2,1)} collective-permute-done((bf16[1024,512]{1,0:T(8,128)(2,1)}, bf16[1024,512]{1,0:T(8,128)(2,1)}, u32[]{:S(2)}, u32[]{:S(2)}) %collective-permute-start.1) | collective-permute-done | bytes 1048608 | tf_op jit(solution)/shard_map/ppermute | solution.py:28
  97.9 2.4 broadcast_select_fusion.2.cot_ref
  100.3 1.8 convolution_convert_fusion.g_ref
  102.1 7.4 %collective-permute-done.next_ref = bf16[1024,512]{1,0:T(8,128)(2,1)S(1)} collective-permute-done((bf16[1024,512]{1,0:T(8,128)(2,1)}, bf16[1024,512]{1,0:T(8,128)(2,1)S(1)}, u32[]{:S(2)}, u32[]{:S(2)}) %collective-permute-start) | collective-permute-done | bytes 1048608 | tf_op jit(solution)/shard_map/ppermute | solution.py:28
  110.4 6.2 %project.1 = (bf16[1024,512]{1,0:T(8,128)(2,1)}, bf16[1024,512]{1,0:T(8,128)(2,1)}, bf16[1024,1536]{1,0:T(8,128)(2,1)}) custom-call(s32[1]{0:T(128)} %bitcast.4.limit_ref, bf16[1024,512]{1,0:T(8,128)(2,1)} %place.3.own_ref, bf16[1024,512]{1,0:T(8,128)(2,1)} %copy-done.5, f32[1,512]{1,0:T(1,128)} %bitcast.49, bf16[512,1536]{1,0:T(8,128)(2,1)} %weight_ref.3), custom_call_target="tpu_custom_call" | custom-call | tf_op jit(solution)/shard_map/project/pallas_call | solution.py:102
  116.6 44.8 %attend.1 = (bf16[1024,512]{1,0:T(8,128)(2,1)}, bf16[3,1024,512]{2,1,0:T(8,128)(2,1)}) custom-call(bf16[1024,1536]{1,0:T(8,128)(2,1)} %get-tuple-element.30.q_ref.k_ref.v_ref, bf16[1024,1536]{1,0:T(8,128)(2,1)} %get-tuple-element.30.q_ref.k_ref.v_ref, bf16[1024,1536]{1,0:T(8,128)(2,1)} %get-tuple-element.30.q_ref.k_ref.v_ref, ...), custom_call_target="tpu_custom_call" | custom-call | tf_op jit(solution)/shard_map/attend/pallas_call | solution.py:168
  161.4 6.7 %input_grad.1 = (bf16[1024,512]{1,0:T(8,128)(2,1)}, f32[1,512]{1,0:T(1,128)}) custom-call(bf16[3,1024,512]{2,1,0:T(8,128)(2,1)} %get-tuple-element.31.d_ref, bf16[512,1536]{1,0:T(8,128)(2,1)} %weight_ref.3, bf16[1024,512]{1,0:T(8,128)(2,1)} %get-tuple-element.32.win_ref, bf16[1024,512]{1,0:T(8,128)(2,1)} %copy-done.1, f32[1,512]{1,0:T(1,128)} %bitcast.50), custom_call_target="tpu_custom_call" | custom-call | tf_op jit(solution)/shard_map/input_grad/pallas_call | solution.py:221
  169.4 2.1 reshape_reshape.8.index_ref
  171.4 6.8 %weight_grad.1.g_ref = bf16[512,2048]{1,0:T(8,128)(2,1)} custom-call(bf16[1024,512]{1,0:T(8,128)(2,1)} %get-tuple-element.34.normed_ref, bf16[3,1024,512]{2,1,0:T(8,128)(2,1)} %get-tuple-element.31.d_ref, bf16[1024,512]{1,0:T(8,128)(2,1)} %get-tuple-element.35.mixed_ref, bf16[1024,512]{1,0:T(8,128)(2,1)} %copy-done.1), custom_call_target="tpu_custom_call" | custom-call | tf_op jit(solution)/shard_map/weight_grad/pallas_call | solution.py:258
  178.2 1.7 add_convert_fusion
  181.4 7.8 %fetch.2 = bf16[2048,512]{1,0:T(8,128)(2,1)} custom-call(s32[2048,1]{1,0:T(8,128)} %reshape_reshape.8.index_ref, bf16[1024,512]{1,0:T(8,128)(2,1)} %broadcast_select_fusion.1.src_ref), custom_call_target="tpu_custom_call" | custom-call | tf_op jit(solution)/shard_map/fetch/pallas_call | solution.py:64
  189.2 10.8 %all-to-all-start.2 = ((bf16[64,32,512]{2,1,0:T(8,128)(2,1)}), bf16[64,32,512]{2,1,0:T(8,128)(2,1)S(1)}, u32[]{:S(2)}, u32[]{:S(2)}) async-start(bf16[64,32,512]{2,1,0:T(8,128)(2,1)} %bitcast.37), calls=%async_computation.2 | async-start | bytes 4194304 | tf_op jit(solution)/shard_map/all_to_all | solution.py:471
  200.0 1.3 copy.29
  201.4 1.3 copy.26
  202.7 3.7 %fusion.8.index_ref = s32[2048,1]{1,0:T(8,128)} fusion(s32[2048,1]{1,0:T(8,128)} %copy.29, s32[2048,1]{1,0:T(8,128)} %copy.26, s32[]{:T(128)} %bitcast.28), kind=kLoop, calls=%fused_computation.25 | loop fusion | flops 63488 | bytes 24580 | tf_op jit(solution)/shard_map/jit(_where)/select_n | solution.py:413
  206.5 2.7 collective-permute-start.3
  209.7 83.5 %reduce_all.1 = (bf16[512,2048]{1,0:T(8,128)(2,1)}, f32[8,128]{1,0:T(8,128)}) custom-call(bf16[512,2048]{1,0:T(8,128)(2,1)} %weight_grad.1.g_ref, f32[8,128]{1,0:T(8,128)} %scatter.4.s_ref), custom_call_target="tpu_custom_call" | custom-call | tf_op jit(solution)/shard_map/reduce_all/pallas_call | solution.py:381
  293.3 1.3 multiply_bitcast_fusion
  294.5 2.2 convert_multiply_fusion.1
  296.7 3.5 %convert_multiply_fusion = f32[512,1536]{1,0:T(8,128)} fusion(bf16[512,2048]{1,0:T(8,128)(2,1)} %get-tuple-element.41), kind=kLoop, calls=%fused_computation.4 | loop fusion | flops 1572864 | bytes 4718592 | tf_op jit(solution)/shard_map/mul | solution.py:488
  300.4 3.0 fusion.10
  303.4 1.3 copy-done.2
  304.8 9.2 %fetch.3 = bf16[2048,512]{1,0:T(8,128)(2,1)} custom-call(s32[2048,1]{1,0:T(8,128)} %fusion.8.index_ref, bf16[2048,512]{1,0:T(8,128)(2,1)} %bitcast.36), custom_call_target="tpu_custom_call" | custom-call | tf_op jit(solution)/shard_map/fetch/pallas_call | solution.py:64
  (39 shorter events, 7.8 us)
Async XLA Ops:
  0.6 99.7 %copy-start = (bf16[512,512]{1,0:T(8,128)(2,1)S(1)}, bf16[512,512]{1,0:T(8,128)(2,1)}, u32[]{:S(2)}) copy-start(bf16[512,512]{1,0:T(8,128)(2,1)} %param.16) | copy-start | bytes 1572868
  2.7 16.6 %copy-start.9 = (s32[1,2048]{1,0:T(1,128)S(1)}, s32[1,2048]{1,0:T(1,128)}, u32[]{:S(2)}) copy-start(s32[1,2048]{1,0:T(1,128)} %param.12) | copy-start | bytes 24580
  8.4 19.7 %all-to-all-start = ((s32[64,1,32]{2,1,0:T(1,128)}), s32[64,1,32]{2,1,0:T(1,128)S(1)}, u32[]{:S(2)}, u32[]{:S(2)}) async-start(s32[64,1,32]{2,1,0:T(1,128)} %bitcast.3), calls=%async_computation | async-start | bytes 65536 | tf_op jit(solution)/shard_map/all_to_all | solution.py:444
  28.1 59.2 %all-to-all-start.1 = ((bf16[64,32,512]{2,1,0:T(8,128)(2,1)}), bf16[64,32,512]{2,1,0:T(8,128)(2,1)S(1)}, u32[]{:S(2)}, u32[]{:S(2)}) async-start(bf16[64,32,512]{2,1,0:T(8,128)(2,1)} %bitcast.38), calls=%async_computation.1 | async-start | bytes 4194304 | tf_op jit(solution)/shard_map/all_to_all | solution.py:447
  41.6 56.3 %collective-permute-start.1 = (bf16[1024,512]{1,0:T(8,128)(2,1)}, bf16[1024,512]{1,0:T(8,128)(2,1)}, u32[]{:S(2)}, u32[]{:S(2)}) collective-permute-start(bf16[1024,512]{1,0:T(8,128)(2,1)} %fusion.11), channel_id=1, source_target_pairs={{0,252},{4,0},{8,4},{12,8},{16,12},{20,16},{24,20},{28,24},{32,28}... | collective-permute-start | bytes 3145736 | tf_op jit(solution)/shard_map/ppermute | solution.py:28
  87.3 1.3 copy-start.3
  93.8 15.6 %collective-permute-start = (bf16[1024,512]{1,0:T(8,128)(2,1)}, bf16[1024,512]{1,0:T(8,128)(2,1)S(1)}, u32[]{:S(2)}, u32[]{:S(2)}) collective-permute-start(bf16[1024,512]{1,0:T(8,128)(2,1)} %place.3.own_ref), channel_id=1, source_target_pairs={{0,252},{4,0},{8,4},{12,8},{16,12},{20,16},{24,20},{28,24},{32,28}... | collective-permute-start | bytes 3145736 | tf_op jit(solution)/shard_map/ppermute | solution.py:28
  100.3 16.3 %copy-start.1 = (bf16[1024,512]{1,0:T(8,128)(2,1)}, bf16[1024,512]{1,0:T(8,128)(2,1)S(1)}, u32[]{:S(2)}) copy-start(bf16[1024,512]{1,0:T(8,128)(2,1)S(1)} %broadcast_select_fusion.2.cot_ref) | copy-start | bytes 3145732
  109.4 1.0 copy-start.5
  168.1 12.1 %collective-permute-start.2 = (bf16[1024,512]{1,0:T(8,128)(2,1)}, bf16[1024,512]{1,0:T(8,128)(2,1)S(1)}, u32[]{:S(2)}, u32[]{:S(2)}) collective-permute-start(bf16[1024,512]{1,0:T(8,128)(2,1)} %get-tuple-element.33), channel_id=1, source_target_pairs={{0,4},{4,8},{8,12},{12,16},{16,20},{20,24},{24,28},{28,32},{32,36}... | collective-permute-start | bytes 3145736 | tf_op jit(solution)/shard_map/ppermute | solution.py:28
  171.4 6.8 %copy-start.4 = (bf16[1024,512]{1,0:T(8,128)(2,1)S(1)}, bf16[1024,512]{1,0:T(8,128)(2,1)}, u32[]{:S(2)}) copy-start(bf16[1024,512]{1,0:T(8,128)(2,1)} %get-tuple-element.32.win_ref) | copy-start | bytes 3145732
  171.4 6.8 %copy-start.8 = (bf16[1024,512]{1,0:T(8,128)(2,1)S(1)}, bf16[1024,512]{1,0:T(8,128)(2,1)}, u32[]{:S(2)}) copy-start(bf16[1024,512]{1,0:T(8,128)(2,1)} %get-tuple-element.35.mixed_ref) | copy-start | bytes 3145732
  178.2 2.0 copy-start.7
  189.2 114.2 %all-to-all-start.2 = ((bf16[64,32,512]{2,1,0:T(8,128)(2,1)}), bf16[64,32,512]{2,1,0:T(8,128)(2,1)S(1)}, u32[]{:S(2)}, u32[]{:S(2)}) async-start(bf16[64,32,512]{2,1,0:T(8,128)(2,1)} %bitcast.37), calls=%async_computation.2 | async-start | bytes 4194304 | tf_op jit(solution)/shard_map/all_to_all | solution.py:471
  201.4 7.8 %copy-start.10 = (f32[1,512]{1,0:T(1,128)S(1)}, f32[1,512]{1,0:T(1,128)}, u32[]{:S(2)}) copy-start(f32[1,512]{1,0:T(1,128)} %get-tuple-element.40) | copy-start | bytes 6148
  202.7 3.7 %copy-start.6 = (bf16[1024,512]{1,0:T(8,128)(2,1)S(1)}, bf16[1024,512]{1,0:T(8,128)(2,1)}, u32[]{:S(2)}) copy-start(bf16[1024,512]{1,0:T(8,128)(2,1)} %add_convert_fusion) | copy-start | bytes 3145732
  206.5 93.7 %collective-permute-start.3 = (bf16[1024,512]{1,0:T(8,128)(2,1)S(1)}, bf16[1024,512]{1,0:T(8,128)(2,1)S(1)}, u32[]{:S(2)}, u32[]{:S(2)}) collective-permute-start(bf16[1024,512]{1,0:T(8,128)(2,1)S(1)} %copy-done.6), channel_id=1, source_target_pairs={{0,4},{4,8},{8,12},{12,16},{16,20},{20,24},{24,28},{28,32},{32,36}... | collective-permute-start | bytes 3145736 | tf_op jit(solution)/shard_map/ppermute | solution.py:28
  303.4 1.3 copy-start.2

commit v2 on v1

--- a/solution.py
+++ b/solution.py
@@ -8,8 +8,8 @@
 from jax.experimental.pallas import tpu as pltpu
 from jax.sharding import PartitionSpec as P
 
+
 HEAD_DIM = 64
-PATCH = 1024
 EPSILON = 1e-05
 MESH = pl.DeviceIdType.MESH
 BF16 = jnp.bfloat16
@@ -35,7 +35,7 @@
     out_ref[...] = jnp.dot(hot, src_ref[...], preferred_element_type=F32).astype(BF16)
 
 
-def place(dest, src, rows, block=256):
+def place(dest, src, rows, block=512):
     depth, width = src.shape
     return pl.pallas_call(
         place_kernel,
@@ -58,7 +58,7 @@
     out_ref[...] = jnp.dot(hot, src_ref[...], preferred_element_type=F32).astype(BF16)
 
 
-def fetch(index, src, block=256):
+def fetch(index, src, block=512):
     depth, width = src.shape
     rows = index.shape[0]
     return pl.pallas_call(
@@ -95,7 +95,7 @@
     qkv_ref[...] = jnp.dot(normed, weight_ref[...], preferred_element_type=F32).astype(BF16)
 
 
-def project(limit, own, following, gain, weight, block=256):
+def project(limit, own, following, gain, weight, block=512):
     rows, width = own.shape
     wide = weight.shape[1]
     tile = pl.BlockSpec((block, width), lambda i: (i, 0))
@@ -121,6 +121,7 @@
 
 
 def attend_kernel(q_ref, k_ref, v_ref, g_ref, mixed_ref, d_ref, dk_ref, dv_ref, *, chunk):
+    rows = q_ref.shape[0]
     keys, values = k_ref[...], v_ref[...]
     lane = lax.broadcasted_iota(jnp.int32, (1, 128), 1)
     line = lax.broadcasted_iota(jnp.int32, (128, 1), 0)
@@ -130,39 +131,42 @@
     values_t = values.astype(F32).T
     keys_t = [(keys_t * m).astype(BF16) for m in lines]
     values_t = [(values_t * m).astype(BF16) for m in lines]
-    dk_ref[...] = jnp.zeros_like(dk_ref)
-    dv_ref[...] = jnp.zeros_like(dv_ref)
-
-    def step(at, carry):
-        window = pl.ds(pl.multiple_of(at * chunk, chunk), chunk)
+    steps = rows // chunk
+    for at in range(steps):
+        window = slice(at * chunk, (at + 1) * chunk)
         q_all = q_ref[window, :].astype(F32) * HEAD_DIM ** (-0.5)
         g_all = g_ref[window, :].astype(F32)
+        q = jnp.concatenate([(q_all * m).astype(BF16) for m in lanes], axis=0)
+        g = jnp.concatenate([(g_all * m).astype(BF16) for m in lanes], axis=0)
+        logits = lax.dot_general(keys, q, NT, preferred_element_type=F32)
+        power = jnp.exp(logits - jnp.max(logits, axis=0, keepdims=True))
+        share = power * (1.0 / jnp.sum(power, axis=0, keepdims=True))
+        share_b = share.astype(BF16)
+        dshare = lax.dot_general(values, g, NT, preferred_element_type=F32)
+        dot = jnp.sum(dshare * share, axis=0, keepdims=True)
+        dlogits = (share * (dshare - dot)).astype(BF16)
         mixed_t = jnp.zeros((128, chunk), F32)
         dq_t = jnp.zeros((128, chunk), F32)
         for head in range(2):
-            q = (q_all * lanes[head]).astype(BF16)
-            g = (g_all * lanes[head]).astype(BF16)
-            logits = lax.dot_general(keys, q, NT, preferred_element_type=F32)
-            power = jnp.exp(logits - jnp.max(logits, axis=0, keepdims=True))
-            share = power * (1.0 / jnp.sum(power, axis=0, keepdims=True))
-            share_b = share.astype(BF16)
-            mixed_t += jnp.dot(values_t[head], share_b, preferred_element_type=F32)
-            dv_ref[...] += jnp.dot(share_b, g, preferred_element_type=F32)
-            dshare = lax.dot_general(values, g, NT, preferred_element_type=F32)
-            dot = jnp.sum(dshare * share, axis=0, keepdims=True)
-            dlogits = (share * (dshare - dot)).astype(BF16)
-            dq_t += jnp.dot(keys_t[head], dlogits, preferred_element_type=F32)
-            dk_ref[...] += jnp.dot(dlogits, q, preferred_element_type=F32)
+            part = slice(head * chunk, (head + 1) * chunk)
+            mixed_t += jnp.dot(values_t[head], share_b[:, part], preferred_element_type=F32)
+            dq_t += jnp.dot(keys_t[head], dlogits[:, part], preferred_element_type=F32)
+        dv = jnp.dot(share_b, g, preferred_element_type=F32)
+        dk = jnp.dot(dlogits, q, preferred_element_type=F32)
+        if at > 0:
+            dv += dv_ref[...]
+            dk += dk_ref[...]
+        if at < steps - 1:
+            dv_ref[...] = dv
+            dk_ref[...] = dk
+        else:
+            d_ref[1] = dk.astype(BF16)
+            d_ref[2] = dv.astype(BF16)
         mixed_ref[window, :] = mixed_t.T.astype(BF16)
         d_ref[0, window, :] = (dq_t * HEAD_DIM ** (-0.5)).T.astype(BF16)
-        return carry
-
-    lax.fori_loop(0, q_ref.shape[0] // chunk, step, 0)
-    d_ref[1] = dk_ref[...].astype(BF16)
-    d_ref[2] = dv_ref[...].astype(BF16)
-
-
-def attend(qkv, grads, chunk=256):
+
+
+def attend(qkv, grads, chunk=512):
     rows, width = grads.shape
     pairs = width // 128
     return pl.pallas_call(
@@ -215,7 +219,7 @@
     out_ref[...] = (cot_ref[...].astype(F32) + branch).astype(BF16)
 
 
-def input_grad(d, weight, win, cot, gain, block=256):
+def input_grad(d, weight, win, cot, gain, block=512):
     rows, width = win.shape
     tile = pl.BlockSpec((block, width), lambda i: (i, 0))
     return pl.pallas_call(
@@ -238,47 +242,56 @@
     )(d, weight, win, cot, gain.reshape(1, width))
 
 
-def weight_grad_kernel(normed_ref, d_ref, mixed_ref, cot_ref, out_ref):
-    @pl.when(pl.program_id(0) < 3)
+def weight_grad_kernel(half_ref, normed_ref, d_ref, mixed_ref, cot_ref, out_ref):
+    part = half_ref[0] * 2 + pl.program_id(0)
+    middle = out_ref.shape[2]
+
+    def emit(left, right):
+        grad = lax.dot_general(left, right, TN, preferred_element_type=F32).astype(BF16)
+        out_ref[0] = grad[:, :middle]
+        out_ref[1] = grad[:, middle:]
+
+    @pl.when(part < 3)
     def _():
-        out_ref[...] = lax.dot_general(
-            normed_ref[...], d_ref[0], TN, preferred_element_type=F32
-        ).astype(BF16)
-
-    @pl.when(pl.program_id(0) == 3)
+        emit(normed_ref[...], d_ref[0])
+
+    @pl.when(part == 3)
     def _():
-        out_ref[...] = lax.dot_general(
-            mixed_ref[...], cot_ref[...], TN, preferred_element_type=F32
-        ).astype(BF16)
-
-
-def weight_grad(normed, d, mixed, cot):
+        emit(mixed_ref[...], cot_ref[...])
+
+
+def weight_grad(half, normed, d, mixed, cot):
     rows, width = normed.shape
-    whole = pl.BlockSpec((rows, width), lambda j: (0, 0))
+    whole = pl.BlockSpec((rows, width), lambda j, half: (0, 0))
     return pl.pallas_call(
         weight_grad_kernel,
-        grid=(4,),
-        in_specs=[
-            whole,
-            pl.BlockSpec((1, rows, width), lambda j: (jnp.minimum(j, 2), 0, 0)),
-            whole,
-            whole,
-        ],
-        out_specs=pl.BlockSpec((width, width), lambda j: (0, j)),
-        out_shape=jax.ShapeDtypeStruct((width, 4 * width), BF16),
+        grid_spec=pltpu.PrefetchScalarGridSpec(
+            num_scalar_prefetch=1,
+            grid=(2,),
+            in_specs=[
+                whole,
+                pl.BlockSpec(
+                    (1, rows, width), lambda j, half: (jnp.minimum(half[0] * 2 + j, 2), 0, 0)
+                ),
+                whole,
+                whole,
+            ],
+            out_specs=pl.BlockSpec((2, width, width // 2), lambda j, half: (j, 0, 0)),
+        ),
+        out_shape=jax.ShapeDtypeStruct((4, width, width // 2), BF16),
         compiler_params=params(),
         name="weight_grad",
-    )(normed, d, mixed, cot)
+    )(half.reshape(1), normed, d, mixed, cot)
 
 
 def reduce_kernel(
-    sizes, g_ref, s_ref, out_ref, t_ref,
-    half, in_core, quarter, in_y, band, in_z, piece, in_x,
-    small, small_core, small_y, small_z, small_x, send_sem, recv_sem, small_send, small_recv,
+    sizes, q_ref, s_ref, out_ref, t_ref,
+    band, in_z, in_x, small, small_core, small_y, small_z, small_x,
+    send_sem, recv_sem, small_send, small_recv,
 ):
     nx, ny, nz = sizes
-    rows, wide = g_ref.shape
-    half_w, part_w = wide // 2, wide // 2 // ny
+    rows, part_w = q_ref.shape
+    half_w = part_w * ny
     band_h, piece_h = rows // nz, rows // nz // nx
     me = lax.axis_index("pts")
     y = lax.axis_index("rep")
@@ -299,91 +312,123 @@
         pl.semaphore_signal(barrier, inc=1, device_id=device, device_id_type=MESH)
     pl.semaphore_wait(barrier, len(everyone))
 
-    def send(src, dst, slot, device, sems=(send_sem, recv_sem)):
+    used = [0]
+    small_used = [0]
+
+    def send(src, dst, device):
+        slot = used[0]
+        used[0] += 1
         copy = pltpu.make_async_remote_copy(
-            src_ref=src, dst_ref=dst, send_sem=sems[0].at[slot], recv_sem=sems[1].at[slot],
+            src_ref=src, dst_ref=dst, send_sem=send_sem.at[slot], recv_sem=recv_sem.at[slot],
             device_id=device, device_id_type=MESH,
         )
         copy.start()
         return copy
 
-    def columns(index, width, base=0):
-        return pl.ds(pl.multiple_of(base + index * width, width), width)
+    def send_small(peers, slots, mine):
+        slots[mine] = small[...]
+        copies = []
+        for device, _ in peers:
+            slot = small_used[0]
+            small_used[0] += 1
+            copy = pltpu.make_async_remote_copy(
+                src_ref=small, dst_ref=slots.at[mine],
+                send_sem=small_send.at[slot], recv_sem=small_recv.at[slot],
+                device_id=device, device_id_type=MESH,
+            )
+            copy.start()
+            copies.append(copy)
+        return copies
+
+    def add_small(copies, slots):
+        for copy in copies:
+            copy.wait()
+        total = slots[0]
+        for k in range(1, slots.shape[0]):
+            total += slots[k]
+        small[...] = total
+
+    def columns(index, width):
+        return pl.ds(pl.multiple_of(index * width, width), width)
 
     def lines(index, height):
         return pl.ds(pl.multiple_of(index * height, height), height)
 
-    used = [0]
-
-    def exchange(peers, pick, land, small_slots, mine):
-        small_slots[mine] = small[...]
-        copies = []
-        for k, (device, index) in enumerate(peers):
-            slot = used[0] + k
-            copies.append(send(pick(index), land(k), slot, device))
-            copies.append(send(small, small_slots.at[mine], slot, device, (small_send, small_recv)))
-        used[0] += len(peers)
-        for copy in copies:
-            copy.wait()
-        total = small_slots[0]
-        for k in range(1, len(peers) + 1):
-            total += small_slots[k]
-        small[...] = total
-
     small[...] = s_ref[...]
-    exchange(by_core, lambda i: g_ref.at[:, columns(i, half_w)], lambda k: in_core, small_core, core)
-    own = g_ref[:, columns(core, half_w)]
-    half[...] = (own.astype(F32) + in_core[...].astype(F32)).astype(BF16)
-    exchange(by_y, lambda i: half.at[:, columns(i, part_w)], lambda k: in_y.at[k], small_y, y)
-    total = half[:, columns(y, part_w)].astype(F32)
-    for k in range(ny - 1):
-        total += in_y[k].astype(F32)
-    quarter[...] = total.astype(BF16)
-    exchange(by_z, lambda i: quarter.at[lines(i, band_h), :], lambda k: in_z.at[k], small_z, z)
-    total = quarter[lines(z, band_h), :].astype(F32)
+    copies = [
+        send(q_ref.at[lines(i, band_h), :], in_z.at[k], device) for k, (device, i) in enumerate(by_z)
+    ]
+    small_copies = send_small(by_z, small_z, z)
+    for copy in copies:
+        copy.wait()
+    total = q_ref[lines(z, band_h), :].astype(F32)
     for k in range(nz - 1):
         total += in_z[k].astype(F32)
     band[...] = total.astype(BF16)
-    exchange(by_x, lambda i: band.at[lines(i, piece_h), :], lambda k: in_x.at[k], small_x, x)
+    copies = [
+        send(band.at[lines(i, piece_h), :], in_x.at[k], device) for k, (device, i) in enumerate(by_x)
+    ]
+    add_small(small_copies, small_z)
+    small_copies = send_small(by_x, small_x, x)
+    for copy in copies:
+        copy.wait()
     total = band[lines(x, piece_h), :].astype(F32)
     for k in range(nx - 1):
         total += in_x[k].astype(F32)
-    t_ref[...] = small[...]
 
     column = columns(core * ny + y, part_w)
     first = pl.multiple_of(z * band_h + x * piece_h, piece_h)
     out_ref[pl.ds(first, piece_h), column] = total.astype(BF16)
 
     def spread(peers, view):
-        copies = [send(view, view, used[0] + k, device) for k, (device, _) in enumerate(peers)]
-        used[0] += len(peers)
+        return [send(view, view, device) for device, _ in peers]
+
+    copies = spread(by_x, out_ref.at[pl.ds(first, piece_h), column])
+    add_small(small_copies, small_x)
+    small_copies = send_small(by_y, small_y, y)
+    for copy in copies:
+        copy.wait()
+    copies = spread(by_z, out_ref.at[lines(z, band_h), column])
+    add_small(small_copies, small_y)
+    small_copies = send_small(by_core, small_core, core)
+    for copy in copies:
+        copy.wait()
+    own = out_ref.at[:, column]
+    if ny == 4:
+        turn = 1 - 2 * core
+        ahead = at(x, lax.rem(y + turn + ny, ny), z, core)
+        behind = at(x, lax.rem(y - turn + ny, ny), z, core)
+        forth, back = send(own, own, ahead), send(own, own, behind)
+        forth.wait()
+        came = out_ref.at[:, columns(core * ny + lax.rem(y - turn + ny, ny), part_w)]
+        passed = send(came, came, ahead)
+        add_small(small_copies, small_core)
+        back.wait()
+        passed.wait()
+    else:
+        copies = spread(by_y, own)
+        add_small(small_copies, small_core)
         for copy in copies:
             copy.wait()
-
-    spread(by_x, out_ref.at[pl.ds(first, piece_h), column])
-    spread(by_z, out_ref.at[lines(z, band_h), column])
-    spread(by_y, out_ref.at[:, column])
-    spread(by_core, out_ref.at[:, columns(core, half_w)])
-
-
-def reduce_all(grads, small, sizes):
+    t_ref[...] = small[...]
+    for copy in spread(by_core, out_ref.at[:, columns(core, half_w)]):
+        copy.wait()
+
+
+def reduce_all(quarter, small, sizes):
     nx, ny, nz = sizes
-    rows, wide = grads.shape
+    rows, part = quarter.shape
     peers = 1 + (ny - 1) + (nz - 1) + (nx - 1)
-    part = wide // 2 // ny
     vmem = pl.BlockSpec(memory_space=pltpu.VMEM)
     buffers = [
-        (rows, wide // 2), (rows, wide // 2),
-        (rows, part), (ny - 1, rows, part),
-        (rows // nz, part), (nz - 1, rows // nz, part),
-        (rows // nz // nx, part), (nx - 1, rows // nz // nx, part),
+        (rows // nz, part), (nz - 1, rows // nz, part), (max(nx - 1, 1), rows // nz // nx, part),
     ]
     return pl.pallas_call(
         functools.partial(reduce_kernel, sizes),
         in_specs=[vmem, vmem],
         out_specs=[vmem, vmem],
         out_shape=[
-            jax.ShapeDtypeStruct(grads.shape, BF16),
+            jax.ShapeDtypeStruct((rows, part * ny * 2), BF16),
             jax.ShapeDtypeStruct(small.shape, F32),
         ],
         scratch_shapes=[pltpu.VMEM(shape, BF16) for shape in buffers]
@@ -397,7 +442,30 @@
         ],
         compiler_params=params(collective_id=0, has_side_effects=True),
         name="reduce_all",
-    )(grads, small)
+    )(quarter, small)
+
+
+def scatter_core(normed, d, mixed, cot):
+    pts = lax.axis_size("pts")
+    core = lax.rem(lax.axis_index("pts"), 2)
+    swap = [(source, source ^ 1) for source in range(pts)]
+    theirs = lax.ppermute(weight_grad(1 - core, normed, d, mixed, cot), "pts", swap)
+    return (
+        weight_grad(core, normed, d, mixed, cot).astype(F32) + theirs.astype(F32)
+    ).astype(BF16)
+
+
+def scatter_rep(half):
+    reps = lax.axis_size("rep")
+    y = lax.axis_index("rep")
+
+    def piece(step):
+        return lax.dynamic_index_in_dim(half, lax.rem(y + step, reps), 0, keepdims=False)
+
+    total = piece(0).astype(F32)
+    for step in range(1, reps):
+        total += shifted(piece(step), "rep", step).astype(F32)
+    return total.astype(BF16)
 
 
 def route_slots(rank_row, point_count, total, row_count, shard_count, send_size, offset):
@@ -428,10 +496,7 @@
     own_row = jnp.arange(row_count, dtype=jnp.int32)[:, None] < limit
 
     cot_rows = cotangent[0]
-    cot_rolled = lax.dynamic_slice_in_dim(
-        jnp.concatenate([cot_rows, cot_rows], axis=0), offset, row_count, 0
-    )
-    cot_next = shifted(cot_rolled, "pts", -1)
+    cot_next = shifted(cot_rows, "pts", -1)
 
     target, position = route_slots(
         hilbert_rank[0], counts[0, 0], total, row_count, shard_count, slot_size, offset
@@ -441,6 +506,7 @@
         jnp.where(target[:, None] == slot[None, :], position[:, None], -1), axis=0
     )
     outgoing = place(target, points[0], slot_total)
+    outgoing, cot_next = lax.optimization_barrier((outgoing, cot_next))
     in_position = lax.all_to_all(
         out_position.reshape(shard_count, slot_size), "pts", split_axis=0, concat_axis=0, tiled=True
     ).reshape(slot_total)
@@ -448,7 +514,9 @@
         outgoing.reshape(shard_count, slot_size, width), "pts", split_axis=0, concat_axis=0, tiled=True
     ).reshape(slot_total, width)
 
-    cot_window = jnp.where(own_row, cot_rolled, cot_next)
+    cot_window = lax.dynamic_slice_in_dim(
+        jnp.concatenate([cot_rows, cot_next], axis=0), offset, row_count, 0
+    )
     grad_mixed = jnp.dot(cot_window, project_out.T, preferred_element_type=F32).astype(BF16)
 
     rolled = place(in_position, incoming, row_count)
@@ -458,15 +526,17 @@
     grad_window, scale = input_grad(d_qkv, project_in, window, cot_window, norm_gain)
     grad_back = shifted(grad_window, "pts", 1)
 
-    partial = weight_grad(normed, d_qkv, mixed, cot_window)
+    half = scatter_core(normed, d_qkv, mixed, cot_window)
+    grad_back, half = lax.optimization_barrier((grad_back, half))
+    quarter = scatter_rep(half)
     block_window = (
         window.astype(F32) + jnp.dot(mixed, project_out, preferred_element_type=F32)
     ).astype(BF16)
 
     grad_rolled = jnp.where(own_row, grad_window, grad_back)
     returning = fetch(in_position, grad_rolled)
-    returning, partial, scale, block_window = lax.optimization_barrier(
-        (returning, partial, scale, block_window)
+    quarter, scale, block_window, _ = lax.optimization_barrier(
+        (quarter, scale, block_window, returning)
     )
     arrived = lax.all_to_all(
         returning.reshape(shard_count, slot_size, width), "pts", split_axis=0, concat_axis=0, tiled=True
@@ -474,11 +544,10 @@
     block_back = shifted(block_window, "pts", 1)
 
     small = jnp.zeros((8, 128), F32).at[: width // 128].set(scale.reshape(width // 128, 128))
-    summed, small = reduce_all(partial, small, sizes)
-
-    block_rolled = jnp.where(own_row, block_window, block_back)
+    summed, small = reduce_all(quarter, small, sizes)
+
     block_rows = lax.dynamic_slice_in_dim(
-        jnp.concatenate([block_rolled, block_rolled], axis=0), limit, row_count, 0
+        jnp.concatenate([block_back, block_window], axis=0), limit, row_count, 0
     )
     grad_points = fetch(target, arrived)
     factor = 1.0 / math.sqrt(total * lax.axis_size("rep"))
@@ -493,7 +562,7 @@
 
 def solution(mesh):
     spread = mesh.shape["pts"]
-    sizes = {64: (4, 4, 8), 8: (2, 2, 2)}[spread]
+    sizes = {64: (4, 4, 8), 8: (2, 2, 2), 4: (1, 4, 2)}[spread]
     return jax.shard_map(
         functools.partial(on_device, sizes),
         mesh=mesh,

time: 317 us -> 307 us (0.968)
  Pallas kernels: 178 us -> 146 us
  waiting for transfers between devices: 56.4 us -> 71.5 us
  starting transfers between devices: 35.2 us -> 41.6 us
    pallas_call x1, Pallas kernels: 83.5 us -> 65.4 us  [reduce_all(): pl.pallas_call(functools.partial(reduce_kernel, sizes), in_specs=[vmem, v...]
    ppermute x4 -> x7, waiting for transfers between devices: 11.7 us -> 24.5 us  [shifted(): return lax.ppermute(value, axis, pairs)]
    pallas_call x1, Pallas kernels: 44.8 us -> 34.8 us  [attend(): pl.pallas_call(functools.partial(attend_kernel, chunk=chunk), grid=(pairs...]
    ppermute x4 -> x7, starting transfers between devices: 3.07 us -> 10.2 us  [shifted(): return lax.ppermute(value, axis, pairs)]
    pallas_call x2, Pallas kernels: 17 us -> 13.3 us  [fetch(): pl.pallas_call(fetch_kernel, grid=(rows // block,), in_specs=[pl.BlockSpe...]
    convert_element_type x0 -> x2, other arithmetic: none -> 3.35 us  [the longest x1 2.52 us: scatter_core(): return (weight_grad(core, normed, d, mixed, cot).astype(F32) + theirs.ast...]
    pallas_call x1 -> x2, Pallas kernels: 6.78 us -> 8.99 us  [weight_grad(): pl.pallas_call(weight_grad_kernel, grid_spec=pltpu.PrefetchScalarGridSpec...]
  transfers between devices with their start and end apart: 7 -> 11, of which waited for: 4 -> 5; matrix products, arithmetic and copies ran while one was open for 10% -> 12% of each run, Pallas kernels for 33% -> 27%
where the time goes in v2:
time: 307 us; the launch traced here: 303 us
  Pallas kernels  146 us (48%)
  waiting for transfers between devices  71.5 us (23%)
  starting transfers between devices  41.6 us (14%)
  other arithmetic  25.9 us (8%)
  local copies, waits for them, and re-layouts  11.9 us (4%)
  matrix products  4.08 us (1%)
    pallas_call x1, Pallas kernels, reduce_all(): pl.pallas_call(functools.partial(reduce_kernel, sizes), in_specs=[vmem, v...  65.4 us
    all_to_all x1, waiting for transfers between devices, on_device(): lax.all_to_all(outgoing.reshape(shard_count, slot_size, width), 'pts', sp...  47 us
    pallas_call x1, Pallas kernels, attend(): pl.pallas_call(functools.partial(attend_kernel, chunk=chunk), grid=(pairs...  34.8 us
    ppermute x7, waiting for transfers between devices, shifted(): return lax.ppermute(value, axis, pairs)  24.5 us
    pallas_call x2, Pallas kernels, fetch(): pl.pallas_call(fetch_kernel, grid=(rows // block,), in_specs=[pl.BlockSpe...  13.3 us
    pallas_call x2, Pallas kernels, place(): pl.pallas_call(place_kernel, grid=(rows // block,), in_specs=[pl.BlockSpe...  12.3 us
    all_to_all x1, starting transfers between devices, on_device(): lax.all_to_all(returning.reshape(shard_count, slot_size, width), 'pts', s...  10.6 us
    all_to_all x1, starting transfers between devices, on_device(): lax.all_to_all(out_position.reshape(shard_count, slot_size), 'pts', split...  10.4 us
  transfers between devices with their start and end apart: 11, of which 5 were waited for; matrix products, arithmetic and copies ran while one was open for 12% of the time, Pallas kernels for 27%

profile of v2, /device:TPU:97, one launch (start us, length us, event | category | flops | bytes accessed | tf_op | source)
XLA Modules:
  0.0 303.5 jit_solution(5831700638758753689)
XLA Ops:
  3.4 1.7 fusion.2
  5.1 3.3 %select_reduce_fusion = s32[2048]{0:T(1024)S(1)} fusion(s32[2048]{0:T(1024)S(1)} %get-tuple-element.53, s32[2048]{0:T(1024)S(1)} %add_select_fusion.6), kind=kLoop, calls=%fused_computation | loop fusion | flops 12580864 | bytes 24576 | tf_op jit(solution)/shard_map/reduce_max | solution.py:505
  9.1 10.4 %all-to-all-start = ((s32[64,1,32]{2,1,0:T(1,128)}), s32[64,1,32]{2,1,0:T(1,128)S(1)}, u32[]{:S(2)}, u32[]{:S(2)}) async-start(s32[64,1,32]{2,1,0:T(1,128)} %bitcast.4), calls=%async_computation | async-start | bytes 65536 | tf_op jit(solution)/shard_map/all_to_all | solution.py:510
  20.2 7.4 %place.2 = bf16[2048,512]{1,0:T(8,128)(2,1)} custom-call(s32[1,2048]{1,0:T(1,128)} %compare_select_fusion.5.dest_ref, bf16[2048,512]{1,0:T(8,128)(2,1)} %bitcast.51), custom_call_target="tpu_custom_call" | custom-call | tf_op jit(solution)/shard_map/place/pallas_call | solution.py:40
  28.6 10.3 %all-to-all-start.1 = ((bf16[64,32,512]{2,1,0:T(8,128)(2,1)}), bf16[64,32,512]{2,1,0:T(8,128)(2,1)S(1)}, u32[]{:S(2)}, u32[]{:S(2)}) async-start(bf16[64,32,512]{2,1,0:T(8,128)(2,1)} %bitcast.49), calls=%async_computation.1 | async-start | bytes 4194304 | tf_op jit(solution)/shard_map/all_to_all | solution.py:513
  40.9 47.0 %all-to-all-done.1 = bf16[64,32,512]{2,1,0:T(8,128)(2,1)S(1)} async-done(((bf16[64,32,512]{2,1,0:T(8,128)(2,1)}), bf16[64,32,512]{2,1,0:T(8,128)(2,1)S(1)}, u32[]{:S(2)}, u32[]{:S(2)}) %all-to-all-start.1) | async-done | bytes 2097184 | tf_op jit(solution)/shard_map/all_to_all | solution.py:513
  89.1 4.9 %place.3.own_ref = bf16[1024,512]{1,0:T(8,128)(2,1)} custom-call(s32[1,2048]{1,0:T(1,128)} %reshape_reshape.6.dest_ref, bf16[2048,512]{1,0:T(8,128)(2,1)} %bitcast.50), custom_call_target="tpu_custom_call" | custom-call | tf_op jit(solution)/shard_map/place/pallas_call | solution.py:40
  94.1 2.2 fusion.11.cot_ref
  96.3 1.7 convolution_convert_fusion.g_ref
  98.0 11.7 %collective-permute-done.1.next_ref = bf16[1024,512]{1,0:T(8,128)(2,1)S(1)} collective-permute-done((bf16[1024,512]{1,0:T(8,128)(2,1)}, bf16[1024,512]{1,0:T(8,128)(2,1)S(1)}, u32[]{:S(2)}, u32[]{:S(2)}) %collective-permute-start.1) | collective-permute-done | bytes 1048608 | tf_op jit(solution)/shard_map/ppermute | solution.py:28
  110.7 5.5 %project.1 = (bf16[1024,512]{1,0:T(8,128)(2,1)}, bf16[1024,512]{1,0:T(8,128)(2,1)}, bf16[1024,1536]{1,0:T(8,128)(2,1)}) custom-call(s32[1]{0:T(128)} %bitcast.1.limit_ref, bf16[1024,512]{1,0:T(8,128)(2,1)} %place.3.own_ref, bf16[1024,512]{1,0:T(8,128)(2,1)} %copy-done.7, f32[1,512]{1,0:T(1,128)} %bitcast.60, bf16[512,1536]{1,0:T(8,128)(2,1)} %weight_ref.3), custom_call_target="tpu_custom_call" | custom-call | tf_op jit(solution)/shard_map/project/pallas_call | solution.py:102
  116.1 34.8 %attend.1 = (bf16[1024,512]{1,0:T(8,128)(2,1)}, bf16[3,1024,512]{2,1,0:T(8,128)(2,1)}) custom-call(bf16[1024,1536]{1,0:T(8,128)(2,1)} %get-tuple-element.34.q_ref.k_ref.v_ref, bf16[1024,1536]{1,0:T(8,128)(2,1)} %get-tuple-element.34.q_ref.k_ref.v_ref, bf16[1024,1536]{1,0:T(8,128)(2,1)} %get-tuple-element.34.q_ref.k_ref.v_ref, ...), custom_call_target="tpu_custom_call" | custom-call | tf_op jit(solution)/shard_map/attend/pallas_call | solution.py:172
  150.9 4.5 %weight_grad.3 = bf16[4,512,256]{2,1,0:T(8,128)(2,1)} custom-call(s32[1]{0:T(128)} %bitcast.12.half_ref, bf16[1024,512]{1,0:T(8,128)(2,1)} %get-tuple-element.39.normed_ref, bf16[3,1024,512]{2,1,0:T(8,128)(2,1)} %get-tuple-element.36.d_ref, bf16[1024,512]{1,0:T(8,128)(2,1)} %get-tuple-element.40.mixed_ref, bf16[1024,512]{1,0:T(8,128)(2,1)} %copy-done.1), custom_call_target="tpu_custom_call" | custom-call | tf_op jit(solution)/shard_map/weight_grad/pallas_call | solution.py:266
  155.5 6.1 %input_grad.1 = (bf16[1024,512]{1,0:T(8,128)(2,1)}, f32[1,512]{1,0:T(1,128)}) custom-call(bf16[3,1024,512]{2,1,0:T(8,128)(2,1)} %get-tuple-element.36.d_ref, bf16[512,1536]{1,0:T(8,128)(2,1)} %weight_ref.3, bf16[1024,512]{1,0:T(8,128)(2,1)} %get-tuple-element.37.win_ref, bf16[1024,512]{1,0:T(8,128)(2,1)} %copy-done.1, f32[1,512]{1,0:T(1,128)} %bitcast.61), custom_call_target="tpu_custom_call" | custom-call | tf_op jit(solution)/shard_map/input_grad/pallas_call | solution.py:225
  162.4 2.0 reshape_reshape.8.index_ref
  164.5 4.5 %weight_grad.2 = bf16[4,512,256]{2,1,0:T(8,128)(2,1)} custom-call(s32[1]{0:T(128)} %bitcast.11.half_ref, bf16[1024,512]{1,0:T(8,128)(2,1)} %get-tuple-element.39.normed_ref, bf16[3,1024,512]{2,1,0:T(8,128)(2,1)} %get-tuple-element.36.d_ref, bf16[1024,512]{1,0:T(8,128)(2,1)} %get-tuple-element.40.mixed_ref, bf16[1024,512]{1,0:T(8,128)(2,1)} %copy-done.1), custom_call_target="tpu_custom_call" | custom-call | tf_op jit(solution)/shard_map/weight_grad/pallas_call | solution.py:266
  169.0 2.5 add_convert_fusion.1
  171.5 3.0 collective-permute-done.2
  175.7 5.6 %fetch.2 = bf16[2048,512]{1,0:T(8,128)(2,1)} custom-call(s32[2048,1]{1,0:T(8,128)} %reshape_reshape.8.index_ref, bf16[1024,512]{1,0:T(8,128)(2,1)} %broadcast_select_fusion.src_ref), custom_call_target="tpu_custom_call" | custom-call | tf_op jit(solution)/shard_map/fetch/pallas_call | solution.py:64
  181.3 10.6 %all-to-all-start.2 = ((bf16[64,32,512]{2,1,0:T(8,128)(2,1)}), bf16[64,32,512]{2,1,0:T(8,128)(2,1)S(1)}, u32[]{:S(2)}, u32[]{:S(2)}) async-start(bf16[64,32,512]{2,1,0:T(8,128)(2,1)} %bitcast.48), calls=%async_computation.2 | async-start | bytes 4194304 | tf_op jit(solution)/shard_map/all_to_all | solution.py:541
  191.9 1.3 copy.29
  194.6 3.8 %fusion.8.index_ref = s32[2048,1]{1,0:T(8,128)} fusion(s32[2048,1]{1,0:T(8,128)} %copy.29, s32[2048,1]{1,0:T(8,128)} %copy.26, s32[]{:T(128)} %bitcast.39), kind=kLoop, calls=%fused_computation.26 | loop fusion | flops 63488 | bytes 24580 | tf_op jit(solution)/shard_map/jit(_where)/select_n | solution.py:481
  198.5 1.4 collective-permute-start.4
  199.8 2.6 collective-permute-start.5
  204.2 3.1 %collective-permute-done.4 = bf16[512,256]{1,0:T(8,128)(2,1)S(1)} collective-permute-done((bf16[512,256]{1,0:T(8,128)(2,1)S(1)}, bf16[512,256]{1,0:T(8,128)(2,1)S(1)}, u32[]{:S(2)}, u32[]{:S(2)}) %collective-permute-start.4) | collective-permute-done | bytes 262176 | tf_op jit(solution)/shard_map/ppermute | solution.py:28
  207.4 6.7 %collective-permute-done.5 = bf16[512,256]{1,0:T(8,128)(2,1)S(1)} collective-permute-done((bf16[512,256]{1,0:T(8,128)(2,1)S(1)}, bf16[512,256]{1,0:T(8,128)(2,1)S(1)}, u32[]{:S(2)}, u32[]{:S(2)}) %collective-permute-start.5) | collective-permute-done | bytes 262176 | tf_op jit(solution)/shard_map/ppermute | solution.py:28
  214.9 3.5 %collective-permute-start.7 = (bf16[1024,512]{1,0:T(8,128)(2,1)S(1)}, bf16[1024,512]{1,0:T(8,128)(2,1)S(1)}, u32[]{:S(2)}, u32[]{:S(2)}) collective-permute-start(bf16[1024,512]{1,0:T(8,128)(2,1)S(1)} %add_convert_fusion), channel_id=1, source_target_pairs={{0,4},{4,8},{8,12},{12,16},{16,20},{20,24},{24,28},{28,32},{32,36}... | collective-permute-start | bytes 3145736 | tf_op jit(solution)/shard_map/ppermute | solution.py:28
  219.1 65.4 %reduce_all.1 = (bf16[512,2048]{1,0:T(8,128)(2,1)}, f32[8,128]{1,0:T(8,128)}) custom-call(bf16[512,256]{1,0:T(8,128)(2,1)} %fusion.15.q_ref, f32[8,128]{1,0:T(8,128)} %scatter.4.s_ref), custom_call_target="tpu_custom_call" | custom-call | tf_op jit(solution)/shard_map/reduce_all/pallas_call | solution.py:426
  285.8 2.2 convert_multiply_fusion.1
  287.9 3.5 %convert_multiply_fusion = f32[512,1536]{1,0:T(8,128)} fusion(bf16[512,2048]{1,0:T(8,128)(2,1)} %get-tuple-element.47), kind=kLoop, calls=%fused_computation.4 | loop fusion | flops 1572864 | bytes 4718592 | tf_op jit(solution)/shard_map/mul | solution.py:557
  291.4 3.0 fusion.10
  295.8 7.7 %fetch.3 = bf16[2048,512]{1,0:T(8,128)(2,1)} custom-call(s32[2048,1]{1,0:T(8,128)} %fusion.8.index_ref, bf16[2048,512]{1,0:T(8,128)(2,1)} %bitcast.47), custom_call_target="tpu_custom_call" | custom-call | tf_op jit(solution)/shard_map/fetch/pallas_call | solution.py:64
  (51 shorter events, 17.4 us)
Async XLA Ops:
  0.6 95.7 %copy-start = (bf16[512,512]{1,0:T(8,128)(2,1)S(1)}, bf16[512,512]{1,0:T(8,128)(2,1)}, u32[]{:S(2)}) copy-start(bf16[512,512]{1,0:T(8,128)(2,1)} %param.16) | copy-start | bytes 1572868
  0.6 27.0 %collective-permute-start = (bf16[1024,512]{1,0:T(8,128)(2,1)}, bf16[1024,512]{1,0:T(8,128)(2,1)S(1)}, u32[]{:S(2)}, u32[]{:S(2)}) collective-permute-start(bf16[1024,512]{1,0:T(8,128)(2,1)} %bitcast.53), channel_id=1, source_target_pairs={{0,252},{4,0},{8,4},{12,8},{16,12},{20,16},{24,20},{28,24},{32,28}... | collective-permute-start | bytes 3145736 | tf_op jit(solution)/shard_map/ppermute | solution.py:28
  3.4 16.1 %copy-start.10 = (s32[1,2048]{1,0:T(1,128)S(1)}, s32[1,2048]{1,0:T(1,128)}, u32[]{:S(2)}) copy-start(s32[1,2048]{1,0:T(1,128)} %param.12) | copy-start | bytes 24580
  9.1 18.5 %all-to-all-start = ((s32[64,1,32]{2,1,0:T(1,128)}), s32[64,1,32]{2,1,0:T(1,128)S(1)}, u32[]{:S(2)}, u32[]{:S(2)}) async-start(s32[64,1,32]{2,1,0:T(1,128)} %bitcast.4), calls=%async_computation | async-start | bytes 65536 | tf_op jit(solution)/shard_map/all_to_all | solution.py:510
  27.6 1.0 copy-start.8
  28.6 59.2 %all-to-all-start.1 = ((bf16[64,32,512]{2,1,0:T(8,128)(2,1)}), bf16[64,32,512]{2,1,0:T(8,128)(2,1)S(1)}, u32[]{:S(2)}, u32[]{:S(2)}) async-start(bf16[64,32,512]{2,1,0:T(8,128)(2,1)} %bitcast.49), calls=%async_computation.1 | async-start | bytes 4194304 | tf_op jit(solution)/shard_map/all_to_all | solution.py:513
  87.8 1.3 copy-start.3
  94.1 15.6 %collective-permute-start.1 = (bf16[1024,512]{1,0:T(8,128)(2,1)}, bf16[1024,512]{1,0:T(8,128)(2,1)S(1)}, u32[]{:S(2)}, u32[]{:S(2)}) collective-permute-start(bf16[1024,512]{1,0:T(8,128)(2,1)} %place.3.own_ref), channel_id=1, source_target_pairs={{0,252},{4,0},{8,4},{12,8},{16,12},{20,16},{24,20},{28,24},{32,28}... | collective-permute-start | bytes 3145736 | tf_op jit(solution)/shard_map/ppermute | solution.py:28
  96.3 19.8 %copy-start.1 = (bf16[1024,512]{1,0:T(8,128)(2,1)}, bf16[1024,512]{1,0:T(8,128)(2,1)S(1)}, u32[]{:S(2)}) copy-start(bf16[1024,512]{1,0:T(8,128)(2,1)S(1)} %fusion.11.cot_ref) | copy-start | bytes 3145732
  109.7 1.0 copy-start.7
  155.4 13.5 %collective-permute-start.3 = (bf16[4,512,256]{2,1,0:T(8,128)(2,1)}, bf16[4,512,256]{2,1,0:T(8,128)(2,1)S(1)}, u32[]{:S(2)}, u32[]{:S(2)}) collective-permute-start(bf16[4,512,256]{2,1,0:T(8,128)(2,1)} %weight_grad.3), channel_id=1, source_target_pairs={{0,4},{4,0},{8,12},{12,8},{16,20},{20,16},{24,28},{28,24},{32,36},... | collective-permute-start | bytes 3145736 | tf_op jit(solution)/shard_map/ppermute | solution.py:452
  161.6 12.9 %collective-permute-start.2 = (bf16[1024,512]{1,0:T(8,128)(2,1)}, bf16[1024,512]{1,0:T(8,128)(2,1)S(1)}, u32[]{:S(2)}, u32[]{:S(2)}) collective-permute-start(bf16[1024,512]{1,0:T(8,128)(2,1)} %get-tuple-element.38), channel_id=1, source_target_pairs={{0,4},{4,8},{8,12},{12,16},{16,20},{20,24},{24,28},{28,32},{32,36}... | collective-permute-start | bytes 3145736 | tf_op jit(solution)/shard_map/ppermute | solution.py:28
  169.0 5.5 %copy-start.9 = (bf16[1024,512]{1,0:T(8,128)(2,1)S(1)}, bf16[1024,512]{1,0:T(8,128)(2,1)}, u32[]{:S(2)}) copy-start(bf16[1024,512]{1,0:T(8,128)(2,1)} %get-tuple-element.38) | copy-start | bytes 3145732
  181.3 113.2 %all-to-all-start.2 = ((bf16[64,32,512]{2,1,0:T(8,128)(2,1)}), bf16[64,32,512]{2,1,0:T(8,128)(2,1)S(1)}, u32[]{:S(2)}, u32[]{:S(2)}) async-start(bf16[64,32,512]{2,1,0:T(8,128)(2,1)} %bitcast.48), calls=%async_computation.2 | async-start | bytes 4194304 | tf_op jit(solution)/shard_map/all_to_all | solution.py:541
  194.6 3.8 %copy-start.4 = (bf16[4,512,256]{2,1,0:T(8,128)(2,1)S(1)}, bf16[4,512,256]{2,1,0:T(8,128)(2,1)}, u32[]{:S(2)}) copy-start(bf16[4,512,256]{2,1,0:T(8,128)(2,1)} %add_convert_fusion.1) | copy-start | bytes 3145732
  194.6 9.0 %copy-start.5 = (bf16[1024,512]{1,0:T(8,128)(2,1)S(1)}, bf16[1024,512]{1,0:T(8,128)(2,1)}, u32[]{:S(2)}) copy-start(bf16[1024,512]{1,0:T(8,128)(2,1)} %get-tuple-element.40.mixed_ref) | copy-start | bytes 3145732
  194.6 9.0 %copy-start.6 = (bf16[1024,512]{1,0:T(8,128)(2,1)S(1)}, bf16[1024,512]{1,0:T(8,128)(2,1)}, u32[]{:S(2)}) copy-start(bf16[1024,512]{1,0:T(8,128)(2,1)} %get-tuple-element.37.win_ref) | copy-start | bytes 3145732
  198.5 8.9 %collective-permute-start.4 = (bf16[512,256]{1,0:T(8,128)(2,1)S(1)}, bf16[512,256]{1,0:T(8,128)(2,1)S(1)}, u32[]{:S(2)}, u32[]{:S(2)}) collective-permute-start(bf16[512,256]{1,0:T(8,128)(2,1)S(1)} %get-tuple-element.49), channel_id=1, source_target_pairs={{0,1},{1,2},{2,3},{3,0},{4,5},{5,6},{6,7},{7,4},{8,9},{9,10},{10,1... | collective-permute-start | bytes 786440 | tf_op jit(solution)/shard_map/ppermute | solution.py:28
  199.8 14.2 %collective-permute-start.5 = (bf16[512,256]{1,0:T(8,128)(2,1)S(1)}, bf16[512,256]{1,0:T(8,128)(2,1)S(1)}, u32[]{:S(2)}, u32[]{:S(2)}) collective-permute-start(bf16[512,256]{1,0:T(8,128)(2,1)S(1)} %get-tuple-element.51), channel_id=1, source_target_pairs={{0,2},{1,3},{2,0},{3,1},{4,6},{5,7},{6,4},{7,5},{8,10},{9,11},{10,... | collective-permute-start | bytes 786440 | tf_op jit(solution)/shard_map/ppermute | solution.py:28
  202.5 16.0 %copy-start.11 = (f32[1,512]{1,0:T(1,128)S(1)}, f32[1,512]{1,0:T(1,128)}, u32[]{:S(2)}) copy-start(f32[1,512]{1,0:T(1,128)} %get-tuple-element.46) | copy-start | bytes 6148
  202.5 11.6 %collective-permute-start.6 = (bf16[512,256]{1,0:T(8,128)(2,1)S(1)}, bf16[512,256]{1,0:T(8,128)(2,1)S(1)}, u32[]{:S(2)}, u32[]{:S(2)}) collective-permute-start(bf16[512,256]{1,0:T(8,128)(2,1)S(1)} %get-tuple-element.50), channel_id=1, source_target_pairs={{0,3},{1,0},{2,1},{3,2},{4,7},{5,4},{6,5},{7,6},{8,11},{9,8},{10,9... | collective-permute-start | bytes 786440 | tf_op jit(solution)/shard_map/ppermute | solution.py:28
  214.9 76.5 %collective-permute-start.7 = (bf16[1024,512]{1,0:T(8,128)(2,1)S(1)}, bf16[1024,512]{1,0:T(8,128)(2,1)S(1)}, u32[]{:S(2)}, u32[]{:S(2)}) collective-permute-start(bf16[1024,512]{1,0:T(8,128)(2,1)S(1)} %add_convert_fusion), channel_id=1, source_target_pairs={{0,4},{4,8},{8,12},{12,16},{16,20},{20,24},{24,28},{28,32},{32,36}... | collective-permute-start | bytes 3145736 | tf_op jit(solution)/shard_map/ppermute | solution.py:28
  294.4 1.3 copy-start.2

commit v3 on v2

--- a/solution.py
+++ b/solution.py
@@ -61,6 +61,7 @@
 def fetch(index, src, block=512):
     depth, width = src.shape
     rows = index.shape[0]
+    assert index.shape == (rows, 1)
     return pl.pallas_call(
         fetch_kernel,
         grid=(rows // block,),
@@ -72,7 +73,72 @@
         out_shape=jax.ShapeDtypeStruct((rows, width), BF16),
         compiler_params=params(),
         name="fetch",
-    )(index.reshape(rows, 1), src)
+    )(index, src)
+
+
+def deliver_kernel(count, out_ref, pos_ref, in_ref, in_pos_ref, sems, own_sems):
+    me = lax.axis_index("pts")
+    barrier = pltpu.get_barrier_semaphore()
+
+    def greet(k, carry):
+        pl.semaphore_signal(
+            barrier, inc=1, device_id={"pts": lax.rem(me + k, count)}, device_id_type=MESH
+        )
+        return carry
+
+    lax.fori_loop(1, count, greet, 0)
+    pl.semaphore_wait(barrier, count - 1)
+    own = [
+        pltpu.make_async_copy(pos_ref.at[me], in_pos_ref.at[me], own_sems.at[0]),
+        pltpu.make_async_copy(out_ref.at[me], in_ref.at[me], own_sems.at[1]),
+    ]
+    for copy in own:
+        copy.start()
+
+    def copies(j):
+        near = j // 2 + 1
+        k = near + lax.rem(j, 2) * (count - 2 * near)
+        peer = lax.rem(me + k, count)
+        return [
+            pltpu.make_async_remote_copy(
+                src_ref=src.at[peer], dst_ref=dst.at[me],
+                send_sem=sems.at[2 * row, k], recv_sem=sems.at[2 * row + 1, k],
+                device_id={"pts": peer}, device_id_type=MESH,
+            )
+            for row, (src, dst) in enumerate(((pos_ref, in_pos_ref), (out_ref, in_ref)))
+        ]
+
+    def start(j, carry):
+        for copy in copies(j):
+            copy.start()
+        return carry
+
+    def finish(j, carry):
+        for copy in copies(j):
+            copy.wait()
+        return carry
+
+    lax.fori_loop(0, count - 1, start, 0)
+    lax.fori_loop(0, count - 1, finish, 0)
+    for copy in own:
+        copy.wait()
+
+
+def deliver(outgoing, position):
+    count = outgoing.shape[0]
+    anywhere = pl.BlockSpec(memory_space=pl.ANY)
+    return pl.pallas_call(
+        functools.partial(deliver_kernel, count),
+        in_specs=[anywhere, anywhere],
+        out_specs=[anywhere, anywhere],
+        out_shape=[
+            jax.ShapeDtypeStruct(outgoing.shape, outgoing.dtype),
+            jax.ShapeDtypeStruct(position.shape, position.dtype),
+        ],
+        scratch_shapes=[pltpu.SemaphoreType.DMA((4, count)), pltpu.SemaphoreType.DMA((2,))],
+        compiler_params=params(collective_id=1, has_side_effects=True),
+        name="deliver",
+    )(outgoing, position)
 
 
 def unit_of(values):
@@ -284,10 +350,10 @@
     )(half.reshape(1), normed, d, mixed, cot)
 
 
-def reduce_kernel(
-    sizes, q_ref, s_ref, out_ref, t_ref,
+def return_kernel(
+    sizes, count, q_ref, s_ref, back_ref, out_ref, t_ref, arrived_ref,
     band, in_z, in_x, small, small_core, small_y, small_z, small_x,
-    send_sem, recv_sem, small_send, small_recv,
+    send_sem, recv_sem, small_send, small_recv, slot_sems, own_sem,
 ):
     nx, ny, nz = sizes
     rows, part_w = q_ref.shape
@@ -306,11 +372,49 @@
     by_y = [(at(x, lax.rem(y + k, ny), z, core), lax.rem(y + k, ny)) for k in range(1, ny)]
     by_z = [(at(x, y, lax.rem(z + k, nz), core), lax.rem(z + k, nz)) for k in range(1, nz)]
     by_x = [(at(lax.rem(x + k, nx), y, z, core), lax.rem(x + k, nx)) for k in range(1, nx)]
-    everyone = by_core + by_y + by_z + by_x
     barrier = pltpu.get_barrier_semaphore()
-    for device, _ in everyone:
+
+    def greet(k, carry):
+        pl.semaphore_signal(
+            barrier, inc=1, device_id={"pts": lax.rem(me + k, count)}, device_id_type=MESH
+        )
+        return carry
+
+    lax.fori_loop(1, count, greet, 0)
+    for device, _ in by_y:
         pl.semaphore_signal(barrier, inc=1, device_id=device, device_id_type=MESH)
-    pl.semaphore_wait(barrier, len(everyone))
+    pl.semaphore_wait(barrier, count - 1 + len(by_y))
+
+    def slot_copy(j):
+        near = j // 2 + 1
+        k = near + lax.rem(j, 2) * (count - 2 * near)
+        peer = lax.rem(me + k, count)
+        return pltpu.make_async_remote_copy(
+            src_ref=back_ref.at[peer], dst_ref=arrived_ref.at[me],
+            send_sem=slot_sems.at[0, k], recv_sem=slot_sems.at[1, k],
+            device_id={"pts": peer}, device_id_type=MESH,
+        )
+
+    batches = 9
+    edges = [(count - 1) * b // batches for b in range(batches + 1)]
+
+    def start_slot(j, carry):
+        slot_copy(j).start()
+        return carry
+
+    def sent_slot(j, carry):
+        slot_copy(j).wait_send()
+        return carry
+
+    def came_slot(j, carry):
+        slot_copy(j).wait_recv()
+        return carry
+
+    def issue(b):
+        lax.fori_loop(edges[b], edges[b + 1], start_slot, 0)
+
+    def drain(b):
+        lax.fori_loop(edges[b], edges[b + 1], sent_slot, 0)
 
     used = [0]
     small_used = [0]
@@ -359,6 +463,10 @@
         send(q_ref.at[lines(i, band_h), :], in_z.at[k], device) for k, (device, i) in enumerate(by_z)
     ]
     small_copies = send_small(by_z, small_z, z)
+    own_slot = pltpu.make_async_copy(back_ref.at[me], arrived_ref.at[me], own_sem)
+    own_slot.start()
+    issue(0)
+    issue(1)
     for copy in copies:
         copy.wait()
     total = q_ref[lines(z, band_h), :].astype(F32)
@@ -370,6 +478,8 @@
     ]
     add_small(small_copies, small_z)
     small_copies = send_small(by_x, small_x, x)
+    drain(0)
+    issue(2)
     for copy in copies:
         copy.wait()
     total = band[lines(x, piece_h), :].astype(F32)
@@ -386,11 +496,15 @@
     copies = spread(by_x, out_ref.at[pl.ds(first, piece_h), column])
     add_small(small_copies, small_x)
     small_copies = send_small(by_y, small_y, y)
+    drain(1)
+    issue(3)
     for copy in copies:
         copy.wait()
     copies = spread(by_z, out_ref.at[lines(z, band_h), column])
     add_small(small_copies, small_y)
     small_copies = send_small(by_core, small_core, core)
+    drain(2)
+    issue(4)
     for copy in copies:
         copy.wait()
     own = out_ref.at[:, column]
@@ -399,37 +513,52 @@
         ahead = at(x, lax.rem(y + turn + ny, ny), z, core)
         behind = at(x, lax.rem(y - turn + ny, ny), z, core)
         forth, back = send(own, own, ahead), send(own, own, behind)
+        drain(3)
+        issue(5)
         forth.wait()
         came = out_ref.at[:, columns(core * ny + lax.rem(y - turn + ny, ny), part_w)]
-        passed = send(came, came, ahead)
-        add_small(small_copies, small_core)
-        back.wait()
-        passed.wait()
+        copies = [back, send(came, came, ahead)]
     else:
         copies = spread(by_y, own)
-        add_small(small_copies, small_core)
-        for copy in copies:
-            copy.wait()
+        drain(3)
+        issue(5)
+    add_small(small_copies, small_core)
     t_ref[...] = small[...]
-    for copy in spread(by_core, out_ref.at[:, columns(core, half_w)]):
+    drain(4)
+    issue(6)
+    for copy in copies:
         copy.wait()
-
-
-def reduce_all(quarter, small, sizes):
+    copies = spread(by_core, out_ref.at[:, columns(core, half_w)])
+    drain(5)
+    issue(7)
+    drain(6)
+    issue(8)
+    for copy in copies:
+        copy.wait()
+    own_slot.wait()
+    drain(7)
+    drain(8)
+    lax.fori_loop(0, count - 1, came_slot, 0)
+
+
+def give_back(quarter, small, back, sizes):
     nx, ny, nz = sizes
     rows, part = quarter.shape
+    count = back.shape[0]
     peers = 1 + (ny - 1) + (nz - 1) + (nx - 1)
     vmem = pl.BlockSpec(memory_space=pltpu.VMEM)
+    anywhere = pl.BlockSpec(memory_space=pl.ANY)
     buffers = [
         (rows // nz, part), (nz - 1, rows // nz, part), (max(nx - 1, 1), rows // nz // nx, part),
     ]
     return pl.pallas_call(
-        functools.partial(reduce_kernel, sizes),
-        in_specs=[vmem, vmem],
-        out_specs=[vmem, vmem],
+        functools.partial(return_kernel, sizes, count),
+        in_specs=[vmem, vmem, anywhere],
+        out_specs=[vmem, vmem, anywhere],
         out_shape=[
             jax.ShapeDtypeStruct((rows, part * ny * 2), BF16),
             jax.ShapeDtypeStruct(small.shape, F32),
+            jax.ShapeDtypeStruct(back.shape, BF16),
         ],
         scratch_shapes=[pltpu.VMEM(shape, BF16) for shape in buffers]
         + [pltpu.VMEM(small.shape, F32)]
@@ -439,10 +568,12 @@
             pltpu.SemaphoreType.DMA((2 * peers,)),
             pltpu.SemaphoreType.DMA((peers,)),
             pltpu.SemaphoreType.DMA((peers,)),
+            pltpu.SemaphoreType.DMA((2, count)),
+            pltpu.SemaphoreType.DMA,
         ],
         compiler_params=params(collective_id=0, has_side_effects=True),
-        name="reduce_all",
-    )(quarter, small)
+        name="give_back",
+    )(quarter, small, back)
 
 
 def scatter_core(normed, d, mixed, cot):
@@ -507,12 +638,17 @@
     )
     outgoing = place(target, points[0], slot_total)
     outgoing, cot_next = lax.optimization_barrier((outgoing, cot_next))
-    in_position = lax.all_to_all(
-        out_position.reshape(shard_count, slot_size), "pts", split_axis=0, concat_axis=0, tiled=True
-    ).reshape(slot_total)
-    incoming = lax.all_to_all(
-        outgoing.reshape(shard_count, slot_size, width), "pts", split_axis=0, concat_axis=0, tiled=True
-    ).reshape(slot_total, width)
+    lanes = -(-slot_size // 128) * 128
+    sent_position = jnp.pad(
+        out_position.reshape(shard_count, 1, slot_size),
+        ((0, 0), (0, 0), (0, lanes - slot_size)),
+        constant_values=-1,
+    )
+    incoming, in_position = deliver(
+        outgoing.reshape(shard_count, slot_size, width), sent_position
+    )
+    incoming = incoming.reshape(slot_total, width)
+    in_position = in_position[:, 0, :slot_size].reshape(slot_total)
 
     cot_window = lax.dynamic_slice_in_dim(
         jnp.concatenate([cot_rows, cot_next], axis=0), offset, row_count, 0
@@ -521,35 +657,36 @@
 
     rolled = place(in_position, incoming, row_count)
     rolled_next = shifted(rolled, "pts", -1)
+    target_column = target.reshape(slot_total, 1)
+    position_column = in_position.reshape(slot_total, 1)
+    rolled_next, target_column, position_column, grad_mixed = lax.optimization_barrier(
+        (rolled_next, target_column, position_column, grad_mixed)
+    )
     window, normed, qkv = project(limit.reshape(1), rolled, rolled_next, norm_gain, project_in)
     mixed, d_qkv = attend(qkv, grad_mixed)
     grad_window, scale = input_grad(d_qkv, project_in, window, cot_window, norm_gain)
     grad_back = shifted(grad_window, "pts", 1)
 
     half = scatter_core(normed, d_qkv, mixed, cot_window)
-    grad_back, half = lax.optimization_barrier((grad_back, half))
-    quarter = scatter_rep(half)
     block_window = (
         window.astype(F32) + jnp.dot(mixed, project_out, preferred_element_type=F32)
     ).astype(BF16)
+    grad_back, half, block_window = lax.optimization_barrier((grad_back, half, block_window))
+    quarter = scatter_rep(half)
+    block_back = shifted(block_window, "pts", 1)
 
     grad_rolled = jnp.where(own_row, grad_window, grad_back)
-    returning = fetch(in_position, grad_rolled)
-    quarter, scale, block_window, _ = lax.optimization_barrier(
-        (quarter, scale, block_window, returning)
-    )
-    arrived = lax.all_to_all(
-        returning.reshape(shard_count, slot_size, width), "pts", split_axis=0, concat_axis=0, tiled=True
-    ).reshape(slot_total, width)
-    block_back = shifted(block_window, "pts", 1)
-
+    returning = fetch(position_column, grad_rolled)
     small = jnp.zeros((8, 128), F32).at[: width // 128].set(scale.reshape(width // 128, 128))
-    summed, small = reduce_all(quarter, small, sizes)
+    summed, small, arrived = give_back(
+        quarter, small, returning.reshape(shard_count, slot_size, width), sizes
+    )
+    arrived = arrived.reshape(slot_total, width)
 
     block_rows = lax.dynamic_slice_in_dim(
         jnp.concatenate([block_back, block_window], axis=0), limit, row_count, 0
     )
-    grad_points = fetch(target, arrived)
+    grad_points = fetch(target_column, arrived)
     factor = 1.0 / math.sqrt(total * lax.axis_size("rep"))
     return (
         block_rows[None],

time: 307 us -> 273 us (0.89)
  Pallas kernels: 146 us -> 215 us
  waiting for transfers between devices: 71.5 us -> 11.3 us
  starting transfers between devices: 41.6 us -> 11.7 us
  local copies, waits for them, and re-layouts: 11.9 us -> 5.13 us
  other arithmetic: 25.9 us -> 20.6 us
    pallas_call x1 -> x2, Pallas kernels: 65.4 us -> 134 us  [the longest x1 72.4 us: give_back(): pl.pallas_call(functools.partial(return_kernel, sizes, count), in_specs=[...]
    all_to_all x3 -> x0, waiting for transfers between devices: 47 us -> none  [the longest x1 47 us: on_device(): lax.all_to_all(outgoing.reshape(shard_count, slot_size, width), 'pts', sp...]
    all_to_all x3 -> x0, starting transfers between devices: 31.3 us -> none  [the longest x1 10.6 us: on_device(): lax.all_to_all(returning.reshape(shard_count, slot_size, width), 'pts', s...]
    ppermute x7, waiting for transfers between devices: 24.5 us -> 11.3 us  [shifted(): return lax.ppermute(value, axis, pairs)]
    unnamed x24 -> x22, local copies, waits for them, and re-layouts: 4.62 us -> 0.05 us
  transfers between devices with their start and end apart: 11 -> 8, of which waited for: 5 -> 2; matrix products, arithmetic and copies ran while one was open for 12% -> 9% of each run, Pallas kernels for 27% -> 39%
where the time goes in v3:
time: 273 us; the launch traced here: 270 us
  Pallas kernels  215 us (79%)
  other arithmetic  20.6 us (8%)
  starting transfers between devices  11.7 us (4%)
  waiting for transfers between devices  11.3 us (4%)
  local copies, waits for them, and re-layouts  5.13 us (2%)
  matrix products  4.12 us (2%)
    pallas_call x1, Pallas kernels, give_back(): pl.pallas_call(functools.partial(return_kernel, sizes, count), in_specs=[...  72.4 us
    pallas_call x1, Pallas kernels, deliver(): pl.pallas_call(functools.partial(deliver_kernel, count), in_specs=[anywhe...  61.2 us
    pallas_call x1, Pallas kernels, attend(): pl.pallas_call(functools.partial(attend_kernel, chunk=chunk), grid=(pairs...  34.8 us
    pallas_call x2, Pallas kernels, fetch(): pl.pallas_call(fetch_kernel, grid=(rows // block,), in_specs=[pl.BlockSpe...  13.4 us
    pallas_call x2, Pallas kernels, place(): pl.pallas_call(place_kernel, grid=(rows // block,), in_specs=[pl.BlockSpe...  12.3 us
    ppermute x7, starting transfers between devices, shifted(): return lax.ppermute(value, axis, pairs)  11.7 us
    ppermute x7, waiting for transfers between devices, shifted(): return lax.ppermute(value, axis, pairs)  11.3 us
    pallas_call x2, Pallas kernels, weight_grad(): pl.pallas_call(weight_grad_kernel, grid_spec=pltpu.PrefetchScalarGridSpec...  9.37 us
  transfers between devices with their start and end apart: 8, of which 2 were waited for; matrix products, arithmetic and copies ran while one was open for 9% of the time, Pallas kernels for 39%

profile of v3, /device:TPU:97, one launch (start us, length us, event | category | flops | bytes accessed | tf_op | source)
XLA Modules:
  0.0 270.1 jit_solution(12592201295079302222)
XLA Ops:
  0.6 0.8 collective-permute-start
  3.4 1.7 fusion.2
  5.1 3.3 %select_reduce_fusion = s32[2048]{0:T(1024)S(1)} fusion(s32[2048]{0:T(1024)S(1)} %get-tuple-element.64, s32[2048]{0:T(1024)S(1)} %add_select_fusion.6), kind=kLoop, calls=%fused_computation | loop fusion | flops 12580864 | bytes 24576 | tf_op jit(solution)/shard_map/reduce_max | solution.py:636
  9.8 7.4 %place.2 = bf16[2048,512]{1,0:T(8,128)(2,1)} custom-call(s32[1,2048]{1,0:T(1,128)} %compare_select_fusion.5.dest_ref, bf16[2048,512]{1,0:T(8,128)(2,1)} %bitcast.50), custom_call_target="tpu_custom_call" | custom-call | tf_op jit(solution)/shard_map/place/pallas_call | solution.py:40
  17.2 61.2 %deliver.1 = (bf16[64,32,512]{2,1,0:T(8,128)(2,1)}, s32[64,1,128]{2,1,0:T(1,128)}) custom-call(bf16[64,32,512]{2,1,0:T(8,128)(2,1)} %bitcast.48, s32[64,1,128]{2,1,0:T(1,128)} %pad.7.pos_ref), custom_call_target="tpu_custom_call" | custom-call | tf_op jit(solution)/shard_map/deliver/pallas_call | solution.py:130
  78.4 0.9 fusion.26
  80.0 4.9 %place.3.own_ref = bf16[1024,512]{1,0:T(8,128)(2,1)} custom-call(s32[1,2048]{1,0:T(1,128)} %reshape_reshape_squeeze.6.dest_ref, bf16[2048,512]{1,0:T(8,128)(2,1)} %bitcast.49), custom_call_target="tpu_custom_call" | custom-call | tf_op jit(solution)/shard_map/place/pallas_call | solution.py:40
  86.0 2.1 fusion.8.index_ref
  88.2 2.2 fusion.11.cot_ref
  90.5 1.8 convolution_convert_fusion.g_ref
  92.2 8.4 %collective-permute-done.1.next_ref = bf16[1024,512]{1,0:T(8,128)(2,1)} collective-permute-done((bf16[1024,512]{1,0:T(8,128)(2,1)}, bf16[1024,512]{1,0:T(8,128)(2,1)}, u32[]{:S(2)}, u32[]{:S(2)}) %collective-permute-start.1) | collective-permute-done | bytes 1048608 | tf_op jit(solution)/shard_map/ppermute | solution.py:28
  100.6 5.5 %project.1 = (bf16[1024,512]{1,0:T(8,128)(2,1)}, bf16[1024,512]{1,0:T(8,128)(2,1)}, bf16[1024,1536]{1,0:T(8,128)(2,1)}) custom-call(s32[1]{0:T(128)} %bitcast.1.limit_ref, bf16[1024,512]{1,0:T(8,128)(2,1)} %place.3.own_ref, bf16[1024,512]{1,0:T(8,128)(2,1)} %collective-permute-done.1.next_ref, f32[1,512]{1,0:T(1,128)} %bitcast.61, bf16[512,1536]{1,0:T(8,128)(2,1)} %weight_ref.3), custom_call_target="tpu_custom_call" | custom-call | tf_op jit(solution)/shard_map/project/pallas_call | solution.py:168
  106.1 34.8 %attend.1 = (bf16[1024,512]{1,0:T(8,128)(2,1)}, bf16[3,1024,512]{2,1,0:T(8,128)(2,1)}) custom-call(bf16[1024,1536]{1,0:T(8,128)(2,1)} %get-tuple-element.43.q_ref.k_ref.v_ref, bf16[1024,1536]{1,0:T(8,128)(2,1)} %get-tuple-element.43.q_ref.k_ref.v_ref, bf16[1024,1536]{1,0:T(8,128)(2,1)} %get-tuple-element.43.q_ref.k_ref.v_ref, ...), custom_call_target="tpu_custom_call" | custom-call | tf_op jit(solution)/shard_map/attend/pallas_call | solution.py:238
  140.9 4.5 %weight_grad.3 = bf16[4,512,256]{2,1,0:T(8,128)(2,1)} custom-call(s32[1]{0:T(128)} %bitcast.14.half_ref, bf16[1024,512]{1,0:T(8,128)(2,1)} %get-tuple-element.48.normed_ref, bf16[3,1024,512]{2,1,0:T(8,128)(2,1)} %get-tuple-element.45.d_ref, bf16[1024,512]{1,0:T(8,128)(2,1)} %get-tuple-element.49.mixed_ref, bf16[1024,512]{1,0:T(8,128)(2,1)} %copy-done.1), custom_call_target="tpu_custom_call" | custom-call | tf_op jit(solution)/shard_map/weight_grad/pallas_call | solution.py:332
  145.4 6.1 %input_grad.1 = (bf16[1024,512]{1,0:T(8,128)(2,1)}, f32[1,512]{1,0:T(1,128)}) custom-call(bf16[3,1024,512]{2,1,0:T(8,128)(2,1)} %get-tuple-element.45.d_ref, bf16[512,1536]{1,0:T(8,128)(2,1)} %weight_ref.3, bf16[1024,512]{1,0:T(8,128)(2,1)} %get-tuple-element.46.win_ref, bf16[1024,512]{1,0:T(8,128)(2,1)} %copy-done.1, f32[1,512]{1,0:T(1,128)} %bitcast.62), custom_call_target="tpu_custom_call" | custom-call | tf_op jit(solution)/shard_map/input_grad/pallas_call | solution.py:291
  151.5 1.0 collective-permute-start.2
  152.5 4.9 %weight_grad.2 = bf16[4,512,256]{2,1,0:T(8,128)(2,1)} custom-call(s32[1]{0:T(128)} %bitcast.13.half_ref, bf16[1024,512]{1,0:T(8,128)(2,1)} %get-tuple-element.48.normed_ref, bf16[3,1024,512]{2,1,0:T(8,128)(2,1)} %get-tuple-element.45.d_ref, bf16[1024,512]{1,0:T(8,128)(2,1)} %get-tuple-element.49.mixed_ref, bf16[1024,512]{1,0:T(8,128)(2,1)} %copy-done.1), custom_call_target="tpu_custom_call" | custom-call | tf_op jit(solution)/shard_map/weight_grad/pallas_call | solution.py:332
  157.4 1.4 copy.24.index_ref
  160.1 1.5 add_convert_fusion.1
  161.6 2.9 %collective-permute-done.2 = bf16[1024,512]{1,0:T(8,128)(2,1)} collective-permute-done((bf16[1024,512]{1,0:T(8,128)(2,1)}, bf16[1024,512]{1,0:T(8,128)(2,1)}, u32[]{:S(2)}, u32[]{:S(2)}) %collective-permute-start.2) | collective-permute-done | bytes 1048608 | tf_op jit(solution)/shard_map/ppermute | solution.py:28
  164.6 1.4 collective-permute-start.5
  166.0 2.6 collective-permute-start.6
  168.6 1.1 collective-permute-start.7
  169.7 4.5 %collective-permute-start.4 = (bf16[1024,512]{1,0:T(8,128)(2,1)S(1)}, bf16[1024,512]{1,0:T(8,128)(2,1)S(1)}, u32[]{:S(2)}, u32[]{:S(2)}) collective-permute-start(bf16[1024,512]{1,0:T(8,128)(2,1)S(1)} %add_convert_fusion), channel_id=1, source_target_pairs={{0,4},{4,8},{8,12},{12,16},{16,20},{20,24},{24,28},{28,32},{32,36}... | collective-permute-start | bytes 3145736 | tf_op jit(solution)/shard_map/ppermute | solution.py:28
  174.2 2.4 broadcast_select_fusion.src_ref
  176.6 5.6 %fetch.2 = bf16[2048,512]{1,0:T(8,128)(2,1)} custom-call(s32[2048,1]{1,0:T(8,128)} %copy.24.index_ref, bf16[1024,512]{1,0:T(8,128)(2,1)} %broadcast_select_fusion.src_ref), custom_call_target="tpu_custom_call" | custom-call | tf_op jit(solution)/shard_map/fetch/pallas_call | solution.py:65
  182.2 0.8 fusion.15.q_ref
  183.0 72.4 %give_back.1 = (bf16[512,2048]{1,0:T(8,128)(2,1)}, f32[8,128]{1,0:T(8,128)}, bf16[64,32,512]{2,1,0:T(8,128)(2,1)}) custom-call(bf16[512,256]{1,0:T(8,128)(2,1)} %fusion.15.q_ref, f32[8,128]{1,0:T(8,128)} %scatter.4.s_ref, bf16[64,32,512]{2,1,0:T(8,128)(2,1)} %bitcast.47), custom_call_target="tpu_custom_call" | custom-call | tf_op jit(solution)/shard_map/give_back/pallas_call | solution.py:554
  255.5 7.8 %fetch.3 = bf16[2048,512]{1,0:T(8,128)(2,1)} custom-call(s32[2048,1]{1,0:T(8,128)} %fusion.8.index_ref, bf16[2048,512]{1,0:T(8,128)(2,1)} %bitcast.52), custom_call_target="tpu_custom_call" | custom-call | tf_op jit(solution)/shard_map/fetch/pallas_call | solution.py:65
  263.9 1.1 convert_multiply_fusion.1
  265.0 2.1 convert_multiply_fusion
  267.1 3.0 %fusion.10 = bf16[1,1024,512]{2,1,0:T(8,128)(2,1)} fusion(s32[]{:T(128)S(6)} %select_n.147, bf16[1024,512]{1,0:T(8,128)(2,1)S(1)} %collective-permute-done.4, bf16[1024,512]{1,0:T(8,128)(2,1)S(1)} %add_convert_fusion), kind=kLoop, calls=%fused_computation.28 | loop fusion | flops 2097152 | bytes 3145732 | tf_op jit(solution)/shard_map/broadcast_in_dim | solution.py:692
  (45 shorter events, 6.0 us)
Async XLA Ops:
  0.6 89.8 %copy-start = (bf16[512,512]{1,0:T(8,128)(2,1)S(1)}, bf16[512,512]{1,0:T(8,128)(2,1)}, u32[]{:S(2)}) copy-start(bf16[512,512]{1,0:T(8,128)(2,1)} %param.16) | copy-start | bytes 1572868
  0.6 16.6 %collective-permute-start = (bf16[1024,512]{1,0:T(8,128)(2,1)}, bf16[1024,512]{1,0:T(8,128)(2,1)S(1)}, u32[]{:S(2)}, u32[]{:S(2)}) collective-permute-start(bf16[1024,512]{1,0:T(8,128)(2,1)} %bitcast.53), channel_id=1, source_target_pairs={{0,252},{4,0},{8,4},{12,8},{16,12},{20,16},{24,20},{28,24},{32,28}... | collective-permute-start | bytes 3145736 | tf_op jit(solution)/shard_map/ppermute | solution.py:28
  3.4 5.7 %copy-start.8 = (s32[1,2048]{1,0:T(1,128)S(1)}, s32[1,2048]{1,0:T(1,128)}, u32[]{:S(2)}) copy-start(s32[1,2048]{1,0:T(1,128)} %param.12) | copy-start | bytes 24580
  17.2 67.7 %copy-start.7 = (bf16[1024,512]{1,0:T(8,128)(2,1)}, bf16[1024,512]{1,0:T(8,128)(2,1)S(1)}, u32[]{:S(2)}) copy-start(bf16[1024,512]{1,0:T(8,128)(2,1)S(1)} %collective-permute-done) | copy-start | bytes 3145732
  84.9 15.8 %collective-permute-start.1 = (bf16[1024,512]{1,0:T(8,128)(2,1)}, bf16[1024,512]{1,0:T(8,128)(2,1)}, u32[]{:S(2)}, u32[]{:S(2)}) collective-permute-start(bf16[1024,512]{1,0:T(8,128)(2,1)} %place.3.own_ref), channel_id=1, source_target_pairs={{0,252},{4,0},{8,4},{12,8},{16,12},{20,16},{24,20},{28,24},{32,28}... | collective-permute-start | bytes 3145736 | tf_op jit(solution)/shard_map/ppermute | solution.py:28
  90.5 15.6 %copy-start.1 = (bf16[1024,512]{1,0:T(8,128)(2,1)}, bf16[1024,512]{1,0:T(8,128)(2,1)S(1)}, u32[]{:S(2)}) copy-start(bf16[1024,512]{1,0:T(8,128)(2,1)S(1)} %fusion.11.cot_ref) | copy-start | bytes 3145732
  145.4 14.7 %collective-permute-start.3 = (bf16[4,512,256]{2,1,0:T(8,128)(2,1)}, bf16[4,512,256]{2,1,0:T(8,128)(2,1)}, u32[]{:S(2)}, u32[]{:S(2)}) collective-permute-start(bf16[4,512,256]{2,1,0:T(8,128)(2,1)} %weight_grad.3), channel_id=1, source_target_pairs={{0,4},{4,0},{8,12},{12,8},{16,20},{20,16},{24,28},{28,24},{32,36},... | collective-permute-start | bytes 3145736 | tf_op jit(solution)/shard_map/ppermute | solution.py:583
  151.5 13.1 %collective-permute-start.2 = (bf16[1024,512]{1,0:T(8,128)(2,1)}, bf16[1024,512]{1,0:T(8,128)(2,1)}, u32[]{:S(2)}, u32[]{:S(2)}) collective-permute-start(bf16[1024,512]{1,0:T(8,128)(2,1)} %get-tuple-element.47), channel_id=1, source_target_pairs={{0,4},{4,8},{8,12},{12,16},{16,20},{20,24},{24,28},{28,32},{32,36}... | collective-permute-start | bytes 3145736 | tf_op jit(solution)/shard_map/ppermute | solution.py:28
  152.5 6.3 %copy-start.9 = (f32[1,512]{1,0:T(1,128)S(1)}, f32[1,512]{1,0:T(1,128)}, u32[]{:S(2)}) copy-start(f32[1,512]{1,0:T(1,128)} %get-tuple-element.53) | copy-start | bytes 6148
  152.5 6.9 %copy-start.3 = (bf16[1024,512]{1,0:T(8,128)(2,1)S(1)}, bf16[1024,512]{1,0:T(8,128)(2,1)}, u32[]{:S(2)}) copy-start(bf16[1024,512]{1,0:T(8,128)(2,1)} %get-tuple-element.49.mixed_ref) | copy-start | bytes 3145732
  152.5 6.9 %copy-start.5 = (bf16[1024,512]{1,0:T(8,128)(2,1)S(1)}, bf16[1024,512]{1,0:T(8,128)(2,1)}, u32[]{:S(2)}) copy-start(bf16[1024,512]{1,0:T(8,128)(2,1)} %get-tuple-element.46.win_ref) | copy-start | bytes 3145732
  158.7 1.3 copy-start.2
  160.0 14.1 %copy-start.6 = (bf16[1024,512]{1,0:T(8,128)(2,1)S(1)}, bf16[1024,512]{1,0:T(8,128)(2,1)}, u32[]{:S(2)}) copy-start(bf16[1024,512]{1,0:T(8,128)(2,1)} %get-tuple-element.47) | copy-start | bytes 3145732
  164.6 17.6 %collective-permute-start.5 = (bf16[512,256]{1,0:T(8,128)(2,1)S(1)}, bf16[512,256]{1,0:T(8,128)(2,1)S(1)}, u32[]{:S(2)}, u32[]{:S(2)}) collective-permute-start(bf16[512,256]{1,0:T(8,128)(2,1)S(1)} %get-tuple-element.59), channel_id=1, source_target_pairs={{0,1},{1,2},{2,3},{3,0},{4,5},{5,6},{6,7},{7,4},{8,9},{9,10},{10,1... | collective-permute-start | bytes 786440 | tf_op jit(solution)/shard_map/ppermute | solution.py:28
  166.0 16.2 %collective-permute-start.6 = (bf16[512,256]{1,0:T(8,128)(2,1)S(1)}, bf16[512,256]{1,0:T(8,128)(2,1)S(1)}, u32[]{:S(2)}, u32[]{:S(2)}) collective-permute-start(bf16[512,256]{1,0:T(8,128)(2,1)S(1)} %get-tuple-element.61), channel_id=1, source_target_pairs={{0,2},{1,3},{2,0},{3,1},{4,6},{5,7},{6,4},{7,5},{8,10},{9,11},{10,... | collective-permute-start | bytes 786440 | tf_op jit(solution)/shard_map/ppermute | solution.py:28
  168.6 13.6 %collective-permute-start.7 = (bf16[512,256]{1,0:T(8,128)(2,1)S(1)}, bf16[512,256]{1,0:T(8,128)(2,1)S(1)}, u32[]{:S(2)}, u32[]{:S(2)}) collective-permute-start(bf16[512,256]{1,0:T(8,128)(2,1)S(1)} %get-tuple-element.60), channel_id=1, source_target_pairs={{0,3},{1,0},{2,1},{3,2},{4,7},{5,4},{6,5},{7,6},{8,11},{9,8},{10,9... | collective-permute-start | bytes 786440 | tf_op jit(solution)/shard_map/ppermute | solution.py:28
  169.7 97.5 %collective-permute-start.4 = (bf16[1024,512]{1,0:T(8,128)(2,1)S(1)}, bf16[1024,512]{1,0:T(8,128)(2,1)S(1)}, u32[]{:S(2)}, u32[]{:S(2)}) collective-permute-start(bf16[1024,512]{1,0:T(8,128)(2,1)S(1)} %add_convert_fusion), channel_id=1, source_target_pairs={{0,4},{4,8},{8,12},{12,16},{16,20},{20,24},{24,28},{28,32},{32,36}... | collective-permute-start | bytes 3145736 | tf_op jit(solution)/shard_map/ppermute | solution.py:28
  255.5 7.9 %copy-start.10 = (f32[8,128]{1,0:T(8,128)S(1)}, f32[8,128]{1,0:T(8,128)}, u32[]{:S(2)}) copy-start(f32[8,128]{1,0:T(8,128)} %get-tuple-element.58) | copy-start | bytes 12292
  255.5 8.4 %copy-start.4 = (bf16[512,2048]{1,0:T(8,128)(2,1)S(1)}, bf16[512,2048]{1,0:T(8,128)(2,1)}, u32[]{:S(2)}) copy-start(bf16[512,2048]{1,0:T(8,128)(2,1)} %get-tuple-element.57) | copy-start | bytes 6291460

commit v4 on v3

--- a/solution.py
+++ b/solution.py
@@ -139,6 +139,41 @@
         compiler_params=params(collective_id=1, has_side_effects=True),
         name="deliver",
     )(outgoing, position)
+
+
+def finish_kernel(index_ref, src_ref, grad_ref, out_ref, in_ref, outer_ref, *, factor):
+    fetch_kernel(index_ref, src_ref, out_ref)
+    inner = in_ref.shape[1]
+    in_ref[...] = grad_ref[:, :inner].astype(F32) * factor
+    outer_ref[...] = grad_ref[:, inner:].astype(F32) * factor
+
+
+def finish(index, src, grads, factor, steps=4):
+    depth, width = src.shape
+    rows, tall = index.shape[0], grads.shape[0]
+    block, part = rows // steps, tall // steps
+    inner = grads.shape[1] - width
+    return pl.pallas_call(
+        functools.partial(finish_kernel, factor=factor),
+        grid=(steps,),
+        in_specs=[
+            pl.BlockSpec((block, 1), lambda i: (i, 0)),
+            pl.BlockSpec((depth, width), lambda i: (0, 0)),
+            pl.BlockSpec((part, inner + width), lambda i: (i, 0)),
+        ],
+        out_specs=[
+            pl.BlockSpec((block, width), lambda i: (i, 0)),
+            pl.BlockSpec((part, inner), lambda i: (i, 0)),
+            pl.BlockSpec((part, width), lambda i: (i, 0)),
+        ],
+        out_shape=[
+            jax.ShapeDtypeStruct((rows, width), BF16),
+            jax.ShapeDtypeStruct((tall, inner), F32),
+            jax.ShapeDtypeStruct((tall, width), F32),
+        ],
+        compiler_params=params(),
+        name="finish",
+    )(index, src, grads)
 
 
 def unit_of(values):
@@ -352,13 +387,13 @@
 
 def return_kernel(
     sizes, count, q_ref, s_ref, back_ref, out_ref, t_ref, arrived_ref,
-    band, in_z, in_x, small, small_core, small_y, small_z, small_x,
+    band, in_x, in_z, small, small_core, small_y, small_z, small_x,
     send_sem, recv_sem, small_send, small_recv, slot_sems, own_sem,
 ):
     nx, ny, nz = sizes
     rows, part_w = q_ref.shape
     half_w = part_w * ny
-    band_h, piece_h = rows // nz, rows // nz // nx
+    band_h, piece_h = rows // nx, rows // nx // nz
     me = lax.axis_index("pts")
     y = lax.axis_index("rep")
     core = lax.rem(me, 2)
@@ -460,47 +495,47 @@
 
     small[...] = s_ref[...]
     copies = [
-        send(q_ref.at[lines(i, band_h), :], in_z.at[k], device) for k, (device, i) in enumerate(by_z)
+        send(q_ref.at[lines(i, band_h), :], in_x.at[k], device) for k, (device, i) in enumerate(by_x)
     ]
-    small_copies = send_small(by_z, small_z, z)
+    small_copies = send_small(by_x, small_x, x)
     own_slot = pltpu.make_async_copy(back_ref.at[me], arrived_ref.at[me], own_sem)
     own_slot.start()
     issue(0)
     issue(1)
     for copy in copies:
         copy.wait()
-    total = q_ref[lines(z, band_h), :].astype(F32)
-    for k in range(nz - 1):
-        total += in_z[k].astype(F32)
+    total = q_ref[lines(x, band_h), :].astype(F32)
+    for k in range(nx - 1):
+        total += in_x[k].astype(F32)
     band[...] = total.astype(BF16)
     copies = [
-        send(band.at[lines(i, piece_h), :], in_x.at[k], device) for k, (device, i) in enumerate(by_x)
+        send(band.at[lines(i, piece_h), :], in_z.at[k], device) for k, (device, i) in enumerate(by_z)
     ]
-    add_small(small_copies, small_z)
-    small_copies = send_small(by_x, small_x, x)
+    add_small(small_copies, small_x)
+    small_copies = send_small(by_z, small_z, z)
     drain(0)
     issue(2)
     for copy in copies:
         copy.wait()
-    total = band[lines(x, piece_h), :].astype(F32)
-    for k in range(nx - 1):
-        total += in_x[k].astype(F32)
+    total = band[lines(z, piece_h), :].astype(F32)
+    for k in range(nz - 1):
+        total += in_z[k].astype(F32)
 
     column = columns(core * ny + y, part_w)
-    first = pl.multiple_of(z * band_h + x * piece_h, piece_h)
+    first = pl.multiple_of(x * band_h + z * piece_h, piece_h)
     out_ref[pl.ds(first, piece_h), column] = total.astype(BF16)
 
     def spread(peers, view):
         return [send(view, view, device) for device, _ in peers]
 
-    copies = spread(by_x, out_ref.at[pl.ds(first, piece_h), column])
-    add_small(small_copies, small_x)
+    copies = spread(by_z, out_ref.at[pl.ds(first, piece_h), column])
+    add_small(small_copies, small_z)
     small_copies = send_small(by_y, small_y, y)
     drain(1)
     issue(3)
     for copy in copies:
         copy.wait()
-    copies = spread(by_z, out_ref.at[lines(z, band_h), column])
+    copies = spread(by_x, out_ref.at[lines(x, band_h), column])
     add_small(small_copies, small_y)
     small_copies = send_small(by_core, small_core, core)
     drain(2)
@@ -512,28 +547,41 @@
         turn = 1 - 2 * core
         ahead = at(x, lax.rem(y + turn + ny, ny), z, core)
         behind = at(x, lax.rem(y - turn + ny, ny), z, core)
+
+        def block(step):
+            return out_ref.at[:, columns(core * ny + lax.rem(y + step * turn + ny, ny), part_w)]
+
         forth, back = send(own, own, ahead), send(own, own, behind)
+        last = spread(by_core, own)
         drain(3)
         issue(5)
         forth.wait()
-        came = out_ref.at[:, columns(core * ny + lax.rem(y - turn + ny, ny), part_w)]
-        copies = [back, send(came, came, ahead)]
+        passed = send(block(-1), block(-1), ahead)
+        last += spread(by_core, block(-1))
+        add_small(small_copies, small_core)
+        t_ref[...] = small[...]
+        drain(4)
+        issue(6)
+        back.wait()
+        last += spread(by_core, block(1))
+        passed.wait()
+        last += spread(by_core, block(2))
     else:
         copies = spread(by_y, own)
+        add_small(small_copies, small_core)
+        t_ref[...] = small[...]
         drain(3)
         issue(5)
-    add_small(small_copies, small_core)
-    t_ref[...] = small[...]
-    drain(4)
-    issue(6)
-    for copy in copies:
-        copy.wait()
-    copies = spread(by_core, out_ref.at[:, columns(core, half_w)])
+        drain(4)
+        issue(6)
+        for copy in copies:
+            copy.wait()
+        last = spread(by_core, out_ref.at[:, columns(core, half_w)])
     drain(5)
     issue(7)
     drain(6)
     issue(8)
-    for copy in copies:
+    for copy in last:
         copy.wait()
     own_slot.wait()
     drain(7)
@@ -549,7 +597,7 @@
     vmem = pl.BlockSpec(memory_space=pltpu.VMEM)
     anywhere = pl.BlockSpec(memory_space=pl.ANY)
     buffers = [
-        (rows // nz, part), (nz - 1, rows // nz, part), (max(nx - 1, 1), rows // nz // nx, part),
+        (rows // nx, part), (max(nx - 1, 1), rows // nx, part), (nz - 1, rows // nx // nz, part),
     ]
     return pl.pallas_call(
         functools.partial(return_kernel, sizes, count),
@@ -564,8 +612,8 @@
         + [pltpu.VMEM(small.shape, F32)]
         + [pltpu.VMEM((n,) + small.shape, F32) for n in (2, ny, nz, nx)]
         + [
-            pltpu.SemaphoreType.DMA((2 * peers,)),
-            pltpu.SemaphoreType.DMA((2 * peers,)),
+            pltpu.SemaphoreType.DMA((2 * peers + ny,)),
+            pltpu.SemaphoreType.DMA((2 * peers + ny,)),
             pltpu.SemaphoreType.DMA((peers,)),
             pltpu.SemaphoreType.DMA((peers,)),
             pltpu.SemaphoreType.DMA((2, count)),
@@ -580,7 +628,8 @@
     pts = lax.axis_size("pts")
     core = lax.rem(lax.axis_index("pts"), 2)
     swap = [(source, source ^ 1) for source in range(pts)]
-    theirs = lax.ppermute(weight_grad(1 - core, normed, d, mixed, cot), "pts", swap)
+    sent = weight_grad(1 - core, normed, d, mixed, cot)
+    theirs = lax.ppermute(sent, "pts", swap)
     return (
         weight_grad(core, normed, d, mixed, cot).astype(F32) + theirs.astype(F32)
     ).astype(BF16)
@@ -686,13 +735,13 @@
     block_rows = lax.dynamic_slice_in_dim(
         jnp.concatenate([block_back, block_window], axis=0), limit, row_count, 0
     )
-    grad_points = fetch(target_column, arrived)
     factor = 1.0 / math.sqrt(total * lax.axis_size("rep"))
+    grad_points, grad_in, grad_out = finish(target_column, arrived, summed, factor)
     return (
         block_rows[None],
         grad_points[None],
-        summed[:, : 3 * width].astype(F32) * factor,
-        summed[:, 3 * width :].astype(F32) * factor,
+        grad_in,
+        grad_out,
         small[: width // 128].reshape(width) * factor,
     )
 

time: 273 us -> 271 us (level)
  waiting for transfers between devices: 11.3 us -> 16.2 us
  other arithmetic: 20.6 us -> 16.7 us
    pallas_call x0 -> x1, Pallas kernels: none -> 8.73 us  [finish(): pl.pallas_call(functools.partial(finish_kernel, factor=factor), grid=(ste...]
    pallas_call x2 -> x1, Pallas kernels: 13.4 us -> 5.56 us  [fetch(): pl.pallas_call(fetch_kernel, grid=(rows // block,), in_specs=[pl.BlockSpe...]
    ppermute x7, waiting for transfers between devices: 11.3 us -> 16.2 us  [shifted(): return lax.ppermute(value, axis, pairs)]
    mul x2 -> x0, other arithmetic: 3.19 us -> none  [the longest x1 2.08 us: on_device(): summed[:, :3 * width].astype(F32) * factor]
    pallas_call x1, Pallas kernels: 72.4 us -> 69.3 us  [give_back(): pl.pallas_call(functools.partial(return_kernel, sizes, count), in_specs=[...]
  transfers between devices with their start and end apart: 8 -> 8, of which waited for: 2 -> 3; matrix products, arithmetic and copies ran while one was open for 9% -> 8% of each run, Pallas kernels for 39% -> 38%
where the time goes in v4:
time: 271 us; the launch traced here: 268 us
  Pallas kernels  213 us (79%)
  other arithmetic  16.7 us (6%)
  waiting for transfers between devices  16.2 us (6%)
  starting transfers between devices  10.9 us (4%)
  local copies, waits for them, and re-layouts  5.6 us (2%)
  matrix products  4.12 us (2%)
    pallas_call x1, Pallas kernels, give_back(): pl.pallas_call(functools.partial(return_kernel, sizes, count), in_specs=[...  69.3 us
    pallas_call x1, Pallas kernels, deliver(): pl.pallas_call(functools.partial(deliver_kernel, count), in_specs=[anywhe...  61.2 us
    pallas_call x1, Pallas kernels, attend(): pl.pallas_call(functools.partial(attend_kernel, chunk=chunk), grid=(pairs...  34.8 us
    ppermute x7, waiting for transfers between devices, shifted(): return lax.ppermute(value, axis, pairs)  16.2 us
    pallas_call x2, Pallas kernels, place(): pl.pallas_call(place_kernel, grid=(rows // block,), in_specs=[pl.BlockSpe...  12.3 us
    ppermute x7, starting transfers between devices, shifted(): return lax.ppermute(value, axis, pairs)  10.9 us
    pallas_call x2, Pallas kernels, weight_grad(): pl.pallas_call(weight_grad_kernel, grid_spec=pltpu.PrefetchScalarGridSpec...  9.15 us
    pallas_call x1, Pallas kernels, finish(): pl.pallas_call(functools.partial(finish_kernel, factor=factor), grid=(ste...  8.73 us
  transfers between devices with their start and end apart: 8, of which 3 were waited for; matrix products, arithmetic and copies ran while one was open for 8% of the time, Pallas kernels for 38%

profile of v4, /device:TPU:97, one launch (start us, length us, event | category | flops | bytes accessed | tf_op | source)
XLA Modules:
  0.0 268.2 jit_solution(3152805574670474714)
XLA Ops:
  0.6 0.8 collective-permute-start
  2.7 0.7 add_select_fusion.2
  3.4 1.7 fusion.2
  5.1 3.3 %select_reduce_fusion = s32[2048]{0:T(1024)S(1)} fusion(s32[2048]{0:T(1024)S(1)} %get-tuple-element.70, s32[2048]{0:T(1024)S(1)} %add_select_fusion.6), kind=kLoop, calls=%fused_computation | loop fusion | flops 12580864 | bytes 24576 | tf_op jit(solution)/shard_map/reduce_max | solution.py:685
  9.8 7.4 %place.2 = bf16[2048,512]{1,0:T(8,128)(2,1)} custom-call(s32[1,2048]{1,0:T(1,128)} %compare_select_fusion.5.dest_ref, bf16[2048,512]{1,0:T(8,128)(2,1)} %bitcast.50), custom_call_target="tpu_custom_call" | custom-call | tf_op jit(solution)/shard_map/place/pallas_call | solution.py:40
  17.2 61.2 %deliver.1 = (bf16[64,32,512]{2,1,0:T(8,128)(2,1)}, s32[64,1,128]{2,1,0:T(1,128)}) custom-call(bf16[64,32,512]{2,1,0:T(8,128)(2,1)} %bitcast.48, s32[64,1,128]{2,1,0:T(1,128)} %pad.7.pos_ref), custom_call_target="tpu_custom_call" | custom-call | tf_op jit(solution)/shard_map/deliver/pallas_call | solution.py:130
  78.4 0.9 fusion.26
  80.0 4.9 %place.3.own_ref = bf16[1024,512]{1,0:T(8,128)(2,1)} custom-call(s32[1,2048]{1,0:T(1,128)} %reshape_reshape_squeeze.6.dest_ref, bf16[2048,512]{1,0:T(8,128)(2,1)} %bitcast.49), custom_call_target="tpu_custom_call" | custom-call | tf_op jit(solution)/shard_map/place/pallas_call | solution.py:40
  86.0 2.1 fusion.8.index_ref
  88.2 2.2 fusion.11.cot_ref
  90.5 1.8 convolution_convert_fusion.g_ref
  92.2 8.4 %collective-permute-done.1.next_ref = bf16[1024,512]{1,0:T(8,128)(2,1)} collective-permute-done((bf16[1024,512]{1,0:T(8,128)(2,1)}, bf16[1024,512]{1,0:T(8,128)(2,1)}, u32[]{:S(2)}, u32[]{:S(2)}) %collective-permute-start.1) | collective-permute-done | bytes 1048608 | tf_op jit(solution)/shard_map/ppermute | solution.py:28
  100.6 5.5 %project.1 = (bf16[1024,512]{1,0:T(8,128)(2,1)}, bf16[1024,512]{1,0:T(8,128)(2,1)}, bf16[1024,1536]{1,0:T(8,128)(2,1)}) custom-call(s32[1]{0:T(128)} %bitcast.1.limit_ref, bf16[1024,512]{1,0:T(8,128)(2,1)} %place.3.own_ref, bf16[1024,512]{1,0:T(8,128)(2,1)} %collective-permute-done.1.next_ref, f32[1,512]{1,0:T(1,128)} %bitcast.60, bf16[512,1536]{1,0:T(8,128)(2,1)} %weight_ref.3), custom_call_target="tpu_custom_call" | custom-call | tf_op jit(solution)/shard_map/project/pallas_call | solution.py:203
  106.1 34.8 %attend.1 = (bf16[1024,512]{1,0:T(8,128)(2,1)}, bf16[3,1024,512]{2,1,0:T(8,128)(2,1)}) custom-call(bf16[1024,1536]{1,0:T(8,128)(2,1)} %get-tuple-element.46.q_ref.k_ref.v_ref, bf16[1024,1536]{1,0:T(8,128)(2,1)} %get-tuple-element.46.q_ref.k_ref.v_ref, bf16[1024,1536]{1,0:T(8,128)(2,1)} %get-tuple-element.46.q_ref.k_ref.v_ref, ...), custom_call_target="tpu_custom_call" | custom-call | tf_op jit(solution)/shard_map/attend/pallas_call | solution.py:273
  140.9 4.5 %weight_grad.3 = bf16[4,512,256]{2,1,0:T(8,128)(2,1)} custom-call(s32[1]{0:T(128)} %bitcast.14.half_ref, bf16[1024,512]{1,0:T(8,128)(2,1)} %get-tuple-element.51.normed_ref, bf16[3,1024,512]{2,1,0:T(8,128)(2,1)} %get-tuple-element.48.d_ref, bf16[1024,512]{1,0:T(8,128)(2,1)} %get-tuple-element.52.mixed_ref, bf16[1024,512]{1,0:T(8,128)(2,1)} %copy-done.1), custom_call_target="tpu_custom_call" | custom-call | tf_op jit(solution)/shard_map/weight_grad/pallas_call | solution.py:367
  145.4 6.1 %input_grad.1 = (bf16[1024,512]{1,0:T(8,128)(2,1)}, f32[1,512]{1,0:T(1,128)}) custom-call(bf16[3,1024,512]{2,1,0:T(8,128)(2,1)} %get-tuple-element.48.d_ref, bf16[512,1536]{1,0:T(8,128)(2,1)} %weight_ref.3, bf16[1024,512]{1,0:T(8,128)(2,1)} %get-tuple-element.49.win_ref, bf16[1024,512]{1,0:T(8,128)(2,1)} %copy-done.1, f32[1,512]{1,0:T(1,128)} %bitcast.61), custom_call_target="tpu_custom_call" | custom-call | tf_op jit(solution)/shard_map/input_grad/pallas_call | solution.py:326
  151.5 1.0 collective-permute-start.2
  152.5 4.7 %weight_grad.2 = bf16[4,512,256]{2,1,0:T(8,128)(2,1)} custom-call(s32[1]{0:T(128)} %bitcast.13.half_ref, bf16[1024,512]{1,0:T(8,128)(2,1)} %get-tuple-element.51.normed_ref, bf16[3,1024,512]{2,1,0:T(8,128)(2,1)} %get-tuple-element.48.d_ref, bf16[1024,512]{1,0:T(8,128)(2,1)} %get-tuple-element.52.mixed_ref, bf16[1024,512]{1,0:T(8,128)(2,1)} %copy-done.1), custom_call_target="tpu_custom_call" | custom-call | tf_op jit(solution)/shard_map/weight_grad/pallas_call | solution.py:367
  157.1 0.7 add_convert_fusion
  158.6 5.9 %collective-permute-done.2 = bf16[1024,512]{1,0:T(8,128)(2,1)} collective-permute-done((bf16[1024,512]{1,0:T(8,128)(2,1)}, bf16[1024,512]{1,0:T(8,128)(2,1)}, u32[]{:S(2)}, u32[]{:S(2)}) %collective-permute-start.2) | collective-permute-done | bytes 1048608 | tf_op jit(solution)/shard_map/ppermute | solution.py:28
  164.5 3.7 %collective-permute-start.4 = (bf16[1024,512]{1,0:T(8,128)(2,1)S(1)}, bf16[1024,512]{1,0:T(8,128)(2,1)}, u32[]{:S(2)}, u32[]{:S(2)}) collective-permute-start(bf16[1024,512]{1,0:T(8,128)(2,1)S(1)} %add_convert_fusion), channel_id=1, source_target_pairs={{0,4},{4,8},{8,12},{12,16},{16,20},{20,24},{24,28},{28,32},{32,36}... | collective-permute-start | bytes 3145736 | tf_op jit(solution)/shard_map/ppermute | solution.py:28
  168.2 1.3 copy.24.index_ref
  170.2 1.4 collective-permute-start.5
  171.6 2.6 collective-permute-start.6
  174.2 1.1 collective-permute-start.7
  175.3 2.4 broadcast_select_fusion.src_ref
  177.7 5.6 %fetch.1 = bf16[2048,512]{1,0:T(8,128)(2,1)} custom-call(s32[2048,1]{1,0:T(8,128)} %copy.24.index_ref, bf16[1024,512]{1,0:T(8,128)(2,1)} %broadcast_select_fusion.src_ref), custom_call_target="tpu_custom_call" | custom-call | tf_op jit(solution)/shard_map/fetch/pallas_call | solution.py:65
  183.3 1.9 collective-permute-done.6
  185.2 0.8 fusion.15.q_ref
  186.0 69.3 %give_back.1 = (bf16[512,2048]{1,0:T(8,128)(2,1)}, f32[8,128]{1,0:T(8,128)}, bf16[64,32,512]{2,1,0:T(8,128)(2,1)}) custom-call(bf16[512,256]{1,0:T(8,128)(2,1)} %fusion.15.q_ref, f32[8,128]{1,0:T(8,128)} %scatter.4.s_ref, bf16[64,32,512]{2,1,0:T(8,128)(2,1)} %bitcast.47), custom_call_target="tpu_custom_call" | custom-call | tf_op jit(solution)/shard_map/give_back/pallas_call | solution.py:602
  255.3 8.7 %finish.1 = (bf16[2048,512]{1,0:T(8,128)(2,1)}, f32[512,1536]{1,0:T(8,128)}, f32[512,512]{1,0:T(8,128)}) custom-call(s32[2048,1]{1,0:T(8,128)} %fusion.8.index_ref, bf16[2048,512]{1,0:T(8,128)(2,1)} %bitcast.51, bf16[512,2048]{1,0:T(8,128)(2,1)} %get-tuple-element.60.grad_ref), custom_call_target="tpu_custom_call" | custom-call | tf_op jit(solution)/shard_map/finish/pallas_call | solution.py:156
  264.6 3.6 %fusion.10 = bf16[1,1024,512]{2,1,0:T(8,128)(2,1)} fusion(s32[]{:T(128)S(6)} %select_n.147, bf16[1024,512]{1,0:T(8,128)(2,1)} %collective-permute-done.4, bf16[1024,512]{1,0:T(8,128)(2,1)S(1)} %add_convert_fusion), kind=kLoop, calls=%fused_computation.27 | loop fusion | flops 2097152 | bytes 3145732 | tf_op jit(solution)/shard_map/broadcast_in_dim | solution.py:741
  (41 shorter events, 5.3 us)
Async XLA Ops:
  0.6 89.8 %copy-start = (bf16[512,512]{1,0:T(8,128)(2,1)S(1)}, bf16[512,512]{1,0:T(8,128)(2,1)}, u32[]{:S(2)}) copy-start(bf16[512,512]{1,0:T(8,128)(2,1)} %param.16) | copy-start | bytes 1572868
  0.6 16.6 %collective-permute-start = (bf16[1024,512]{1,0:T(8,128)(2,1)}, bf16[1024,512]{1,0:T(8,128)(2,1)S(1)}, u32[]{:S(2)}, u32[]{:S(2)}) collective-permute-start(bf16[1024,512]{1,0:T(8,128)(2,1)} %bitcast.52), channel_id=1, source_target_pairs={{0,252},{4,0},{8,4},{12,8},{16,12},{20,16},{24,20},{28,24},{32,28}... | collective-permute-start | bytes 3145736 | tf_op jit(solution)/shard_map/ppermute | solution.py:28
  3.4 5.7 %copy-start.7 = (s32[1,2048]{1,0:T(1,128)S(1)}, s32[1,2048]{1,0:T(1,128)}, u32[]{:S(2)}) copy-start(s32[1,2048]{1,0:T(1,128)} %param.12) | copy-start | bytes 24580
  17.2 67.7 %copy-start.6 = (bf16[1024,512]{1,0:T(8,128)(2,1)}, bf16[1024,512]{1,0:T(8,128)(2,1)S(1)}, u32[]{:S(2)}) copy-start(bf16[1024,512]{1,0:T(8,128)(2,1)S(1)} %collective-permute-done) | copy-start | bytes 3145732
  84.9 15.8 %collective-permute-start.1 = (bf16[1024,512]{1,0:T(8,128)(2,1)}, bf16[1024,512]{1,0:T(8,128)(2,1)}, u32[]{:S(2)}, u32[]{:S(2)}) collective-permute-start(bf16[1024,512]{1,0:T(8,128)(2,1)} %place.3.own_ref), channel_id=1, source_target_pairs={{0,252},{4,0},{8,4},{12,8},{16,12},{20,16},{24,20},{28,24},{32,28}... | collective-permute-start | bytes 3145736 | tf_op jit(solution)/shard_map/ppermute | solution.py:28
  90.5 15.6 %copy-start.1 = (bf16[1024,512]{1,0:T(8,128)(2,1)}, bf16[1024,512]{1,0:T(8,128)(2,1)S(1)}, u32[]{:S(2)}) copy-start(bf16[1024,512]{1,0:T(8,128)(2,1)S(1)} %fusion.11.cot_ref) | copy-start | bytes 3145732
  145.4 12.5 %collective-permute-start.3 = (bf16[4,512,256]{2,1,0:T(8,128)(2,1)}, bf16[4,512,256]{2,1,0:T(8,128)(2,1)S(1)}, u32[]{:S(2)}, u32[]{:S(2)}) collective-permute-start(bf16[4,512,256]{2,1,0:T(8,128)(2,1)} %weight_grad.3), channel_id=1, source_target_pairs={{0,4},{4,0},{8,12},{12,8},{16,20},{20,16},{24,28},{28,24},{32,36},... | collective-permute-start | bytes 3145736 | tf_op jit(solution)/shard_map/ppermute | solution.py:632
  151.5 13.1 %collective-permute-start.2 = (bf16[1024,512]{1,0:T(8,128)(2,1)}, bf16[1024,512]{1,0:T(8,128)(2,1)}, u32[]{:S(2)}, u32[]{:S(2)}) collective-permute-start(bf16[1024,512]{1,0:T(8,128)(2,1)} %get-tuple-element.50), channel_id=1, source_target_pairs={{0,4},{4,8},{8,12},{12,16},{16,20},{20,24},{24,28},{28,32},{32,36}... | collective-permute-start | bytes 3145736 | tf_op jit(solution)/shard_map/ppermute | solution.py:28
  152.5 4.7 %copy-start.3 = (bf16[1024,512]{1,0:T(8,128)(2,1)S(1)}, bf16[1024,512]{1,0:T(8,128)(2,1)}, u32[]{:S(2)}) copy-start(bf16[1024,512]{1,0:T(8,128)(2,1)} %get-tuple-element.52.mixed_ref) | copy-start | bytes 3145732
  152.5 4.7 %copy-start.4 = (bf16[1024,512]{1,0:T(8,128)(2,1)S(1)}, bf16[1024,512]{1,0:T(8,128)(2,1)}, u32[]{:S(2)}) copy-start(bf16[1024,512]{1,0:T(8,128)(2,1)} %get-tuple-element.49.win_ref) | copy-start | bytes 3145732
  157.1 1.2 copy-start.2
  157.8 11.7 %copy-start.8 = (f32[1,512]{1,0:T(1,128)S(1)}, f32[1,512]{1,0:T(1,128)}, u32[]{:S(2)}) copy-start(f32[1,512]{1,0:T(1,128)} %get-tuple-element.56) | copy-start | bytes 6148
  164.5 100.1 %collective-permute-start.4 = (bf16[1024,512]{1,0:T(8,128)(2,1)S(1)}, bf16[1024,512]{1,0:T(8,128)(2,1)}, u32[]{:S(2)}, u32[]{:S(2)}) collective-permute-start(bf16[1024,512]{1,0:T(8,128)(2,1)S(1)} %add_convert_fusion), channel_id=1, source_target_pairs={{0,4},{4,8},{8,12},{12,16},{16,20},{20,24},{24,28},{28,32},{32,36}... | collective-permute-start | bytes 3145736 | tf_op jit(solution)/shard_map/ppermute | solution.py:28
  169.6 5.7 %copy-start.5 = (bf16[1024,512]{1,0:T(8,128)(2,1)S(1)}, bf16[1024,512]{1,0:T(8,128)(2,1)}, u32[]{:S(2)}) copy-start(bf16[1024,512]{1,0:T(8,128)(2,1)} %get-tuple-element.50) | copy-start | bytes 3145732
  170.2 13.1 %collective-permute-start.5 = (bf16[512,256]{1,0:T(8,128)(2,1)S(1)}, bf16[512,256]{1,0:T(8,128)(2,1)S(1)}, u32[]{:S(2)}, u32[]{:S(2)}) collective-permute-start(bf16[512,256]{1,0:T(8,128)(2,1)S(1)} %get-tuple-element.65), channel_id=1, source_target_pairs={{0,1},{1,2},{2,3},{3,0},{4,5},{5,6},{6,7},{7,4},{8,9},{9,10},{10,1... | collective-permute-start | bytes 786440 | tf_op jit(solution)/shard_map/ppermute | solution.py:28
  171.6 13.6 %collective-permute-start.6 = (bf16[512,256]{1,0:T(8,128)(2,1)S(1)}, bf16[512,256]{1,0:T(8,128)(2,1)S(1)}, u32[]{:S(2)}, u32[]{:S(2)}) collective-permute-start(bf16[512,256]{1,0:T(8,128)(2,1)S(1)} %get-tuple-element.67), channel_id=1, source_target_pairs={{0,2},{1,3},{2,0},{3,1},{4,6},{5,7},{6,4},{7,5},{8,10},{9,11},{10,... | collective-permute-start | bytes 786440 | tf_op jit(solution)/shard_map/ppermute | solution.py:28
  174.2 10.9 %collective-permute-start.7 = (bf16[512,256]{1,0:T(8,128)(2,1)S(1)}, bf16[512,256]{1,0:T(8,128)(2,1)S(1)}, u32[]{:S(2)}, u32[]{:S(2)}) collective-permute-start(bf16[512,256]{1,0:T(8,128)(2,1)S(1)} %get-tuple-element.66), channel_id=1, source_target_pairs={{0,3},{1,0},{2,1},{3,2},{4,7},{5,4},{6,5},{7,6},{8,11},{9,8},{10,9... | collective-permute-start | bytes 786440 | tf_op jit(solution)/shard_map/ppermute | solution.py:28
  255.3 8.7 %copy-start.9 = (f32[8,128]{1,0:T(8,128)S(1)}, f32[8,128]{1,0:T(8,128)}, u32[]{:S(2)}) copy-start(f32[8,128]{1,0:T(8,128)} %get-tuple-element.64) | copy-start | bytes 12292

commit v5 on v4

--- a/solution.py
+++ b/solution.py
@@ -12,6 +12,8 @@
 HEAD_DIM = 64
 EPSILON = 1e-05
 MESH = pl.DeviceIdType.MESH
+BATCHES = 9
+LEAD = 4
 BF16 = jnp.bfloat16
 F32 = jnp.float32
 NT = (((1,), (1,)), ((), ()))
@@ -141,39 +143,54 @@
     )(outgoing, position)
 
 
-def finish_kernel(index_ref, src_ref, grad_ref, out_ref, in_ref, outer_ref, *, factor):
+def finish_kernel(
+    offset_ref, index_ref, src_ref, grad_ref, window_ref, back_ref,
+    out_ref, in_ref, outer_ref, block_ref, *, factor,
+):
     fetch_kernel(index_ref, src_ref, out_ref)
+    rows = window_ref.shape[0]
+    row = lax.broadcasted_iota(jnp.int32, window_ref.shape, 0)
+    rolled = jnp.where(
+        row < rows - offset_ref[0], window_ref[...].astype(F32), back_ref[...].astype(F32)
+    )
+    block_ref[...] = pltpu.roll(rolled, offset_ref[0], 0).astype(BF16)
     inner = in_ref.shape[1]
     in_ref[...] = grad_ref[:, :inner].astype(F32) * factor
     outer_ref[...] = grad_ref[:, inner:].astype(F32) * factor
 
 
-def finish(index, src, grads, factor, steps=4):
+def finish(offset, index, src, grads, window, back, factor, steps=4):
     depth, width = src.shape
     rows, tall = index.shape[0], grads.shape[0]
-    block, part = rows // steps, tall // steps
+    block, part, lanes = rows // steps, tall // steps, width // steps
     inner = grads.shape[1] - width
+    strip = pl.BlockSpec((window.shape[0], lanes), lambda i: (0, i))
     return pl.pallas_call(
         functools.partial(finish_kernel, factor=factor),
         grid=(steps,),
         in_specs=[
+            pl.BlockSpec(memory_space=pltpu.SMEM),
             pl.BlockSpec((block, 1), lambda i: (i, 0)),
             pl.BlockSpec((depth, width), lambda i: (0, 0)),
             pl.BlockSpec((part, inner + width), lambda i: (i, 0)),
+            strip,
+            strip,
         ],
         out_specs=[
             pl.BlockSpec((block, width), lambda i: (i, 0)),
             pl.BlockSpec((part, inner), lambda i: (i, 0)),
             pl.BlockSpec((part, width), lambda i: (i, 0)),
+            strip,
         ],
         out_shape=[
             jax.ShapeDtypeStruct((rows, width), BF16),
             jax.ShapeDtypeStruct((tall, inner), F32),
             jax.ShapeDtypeStruct((tall, width), F32),
+            jax.ShapeDtypeStruct(window.shape, BF16),
         ],
         compiler_params=params(),
         name="finish",
-    )(index, src, grads)
+    )(offset, index, src, grads, window, back)
 
 
 def unit_of(values):
@@ -430,7 +447,7 @@
             device_id={"pts": peer}, device_id_type=MESH,
         )
 
-    batches = 9
+    batches, lead = BATCHES, LEAD
     edges = [(count - 1) * b // batches for b in range(batches + 1)]
 
     def start_slot(j, carry):
@@ -450,6 +467,14 @@
 
     def drain(b):
         lax.fori_loop(edges[b], edges[b + 1], sent_slot, 0)
+
+    done = [0]
+
+    def advance():
+        if done[0] + lead < batches:
+            drain(done[0])
+            issue(done[0] + lead)
+            done[0] += 1
 
     used = [0]
     small_used = [0]
@@ -500,8 +525,8 @@
     small_copies = send_small(by_x, small_x, x)
     own_slot = pltpu.make_async_copy(back_ref.at[me], arrived_ref.at[me], own_sem)
     own_slot.start()
-    issue(0)
-    issue(1)
+    for b in range(lead):
+        issue(b)
     for copy in copies:
         copy.wait()
     total = q_ref[lines(x, band_h), :].astype(F32)
@@ -513,8 +538,7 @@
     ]
     add_small(small_copies, small_x)
     small_copies = send_small(by_z, small_z, z)
-    drain(0)
-    issue(2)
+    advance()
     for copy in copies:
         copy.wait()
     total = band[lines(z, piece_h), :].astype(F32)
@@ -531,15 +555,13 @@
     copies = spread(by_z, out_ref.at[pl.ds(first, piece_h), column])
     add_small(small_copies, small_z)
     small_copies = send_small(by_y, small_y, y)
-    drain(1)
-    issue(3)
+    advance()
     for copy in copies:
         copy.wait()
     copies = spread(by_x, out_ref.at[lines(x, band_h), column])
     add_small(small_copies, small_y)
     small_copies = send_small(by_core, small_core, core)
-    drain(2)
-    issue(4)
+    advance()
     for copy in copies:
         copy.wait()
     own = out_ref.at[:, column]
@@ -553,15 +575,13 @@
 
         forth, back = send(own, own, ahead), send(own, own, behind)
         last = spread(by_core, own)
-        drain(3)
-        issue(5)
+        advance()
         forth.wait()
         passed = send(block(-1), block(-1), ahead)
         last += spread(by_core, block(-1))
         add_small(small_copies, small_core)
         t_ref[...] = small[...]
-        drain(4)
-        issue(6)
+        advance()
         back.wait()
         last += spread(by_core, block(1))
         passed.wait()
@@ -570,22 +590,18 @@
         copies = spread(by_y, own)
         add_small(small_copies, small_core)
         t_ref[...] = small[...]
-        drain(3)
-        issue(5)
-        drain(4)
-        issue(6)
+        advance()
+        advance()
         for copy in copies:
             copy.wait()
         last = spread(by_core, out_ref.at[:, columns(core, half_w)])
-    drain(5)
-    issue(7)
-    drain(6)
-    issue(8)
+    advance()
+    advance()
     for copy in last:
         copy.wait()
     own_slot.wait()
-    drain(7)
-    drain(8)
+    for b in range(done[0], batches):
+        drain(b)
     lax.fori_loop(0, count - 1, came_slot, 0)
 
 
@@ -659,7 +675,18 @@
     before = jnp.dot(earlier, matches.astype(BF16), preferred_element_type=F32)
     ordinal = jnp.sum(jnp.where(matches, before, 0.0), axis=1).astype(jnp.int32)
     target = jnp.where(live_slot, target_shard * send_size + ordinal, shard_count * send_size)
-    return target, (moved % row_count - offset) % row_count
+    position = (moved % row_count - offset) % row_count
+    here = (ordinal[:, None] == jnp.arange(send_size, dtype=jnp.int32)[None, :]) & live_slot[:, None]
+    digits = jnp.concatenate(
+        [
+            jnp.where(here, digit[:, None], 0).astype(BF16)
+            for digit in (position // 32, position % 32, jnp.ones_like(position))
+        ],
+        axis=1,
+    )
+    found = lax.dot_general(matches.astype(BF16), digits, TN, preferred_element_type=F32)
+    high, low, live = jnp.split(found, 3, axis=1)
+    return target, jnp.where(live > 0.5, high * 32 + low, -1.0).astype(jnp.int32)
 
 
 def on_device(
@@ -678,12 +705,8 @@
     cot_rows = cotangent[0]
     cot_next = shifted(cot_rows, "pts", -1)
 
-    target, position = route_slots(
+    target, out_position = route_slots(
         hilbert_rank[0], counts[0, 0], total, row_count, shard_count, slot_size, offset
-    )
-    slot = jnp.arange(slot_total, dtype=jnp.int32)
-    out_position = jnp.max(
-        jnp.where(target[:, None] == slot[None, :], position[:, None], -1), axis=0
     )
     outgoing = place(target, points[0], slot_total)
     outgoing, cot_next = lax.optimization_barrier((outgoing, cot_next))
@@ -707,7 +730,7 @@
     rolled = place(in_position, incoming, row_count)
     rolled_next = shifted(rolled, "pts", -1)
     target_column = target.reshape(slot_total, 1)
-    position_column = in_position.reshape(slot_total, 1)
+    position_column = jnp.maximum(in_position, -1).reshape(slot_total, 1)
     rolled_next, target_column, position_column, grad_mixed = lax.optimization_barrier(
         (rolled_next, target_column, position_column, grad_mixed)
     )
@@ -720,23 +743,24 @@
     block_window = (
         window.astype(F32) + jnp.dot(mixed, project_out, preferred_element_type=F32)
     ).astype(BF16)
-    grad_back, half, block_window = lax.optimization_barrier((grad_back, half, block_window))
+    small = jnp.pad(scale.reshape(width // 128, 128), ((0, 8 - width // 128), (0, 0)))
+    grad_back, half, block_window, position_column, small = lax.optimization_barrier(
+        (grad_back, half, block_window, position_column, small)
+    )
     quarter = scatter_rep(half)
     block_back = shifted(block_window, "pts", 1)
 
     grad_rolled = jnp.where(own_row, grad_window, grad_back)
     returning = fetch(position_column, grad_rolled)
-    small = jnp.zeros((8, 128), F32).at[: width // 128].set(scale.reshape(width // 128, 128))
     summed, small, arrived = give_back(
         quarter, small, returning.reshape(shard_count, slot_size, width), sizes
     )
     arrived = arrived.reshape(slot_total, width)
 
-    block_rows = lax.dynamic_slice_in_dim(
-        jnp.concatenate([block_back, block_window], axis=0), limit, row_count, 0
-    )
     factor = 1.0 / math.sqrt(total * lax.axis_size("rep"))
-    grad_points, grad_in, grad_out = finish(target_column, arrived, summed, factor)
+    grad_points, grad_in, grad_out, block_rows = finish(
+        offset.reshape(1), target_column, arrived, summed, block_window, block_back, factor
+    )
     return (
         block_rows[None],
         grad_points[None],

time: 271 us -> 265 us (0.978)
  Pallas kernels: 213 us -> 208 us
    pallas_call x1, Pallas kernels: 69.3 us -> 63.3 us  [give_back(): pl.pallas_call(functools.partial(return_kernel, sizes, count), in_specs=[...]
    broadcast_in_dim x1 -> x0, other arithmetic: 3.56 us -> none  [on_device(): block_rows[None]]
    reduce_max x1 -> x0, other arithmetic: 3.25 us -> none  [on_device(): jnp.max(jnp.where(target[:, None] == slot[None, :], position[:, None], -1...]
  transfers between devices with their start and end apart: 8 -> 8, of which waited for: 3 -> 4; matrix products, arithmetic and copies ran while one was open for 8% -> 9% of each run, Pallas kernels for 38% -> 33%
where the time goes in v5:
time: 265 us; the launch traced here: 261 us
  Pallas kernels  208 us (78%)
  waiting for transfers between devices  15 us (6%)
  other arithmetic  14.5 us (5%)
  starting transfers between devices  10.1 us (4%)
  matrix products  5.77 us (2%)
  local copies, waits for them, and re-layouts  4.87 us (2%)
    pallas_call x1, Pallas kernels, give_back(): pl.pallas_call(functools.partial(return_kernel, sizes, count), in_specs=[...  63.3 us
    pallas_call x1, Pallas kernels, deliver(): pl.pallas_call(functools.partial(deliver_kernel, count), in_specs=[anywhe...  61.1 us
    pallas_call x1, Pallas kernels, attend(): pl.pallas_call(functools.partial(attend_kernel, chunk=chunk), grid=(pairs...  34.8 us
    ppermute x7, waiting for transfers between devices, shifted(): return lax.ppermute(value, axis, pairs)  15 us
    pallas_call x2, Pallas kernels, place(): pl.pallas_call(place_kernel, grid=(rows // block,), in_specs=[pl.BlockSpe...  12.3 us
    pallas_call x1, Pallas kernels, finish(): pl.pallas_call(functools.partial(finish_kernel, factor=factor), grid=(ste...  10.2 us
    ppermute x7, starting transfers between devices, shifted(): return lax.ppermute(value, axis, pairs)  10.1 us
    pallas_call x2, Pallas kernels, weight_grad(): pl.pallas_call(weight_grad_kernel, grid_spec=pltpu.PrefetchScalarGridSpec...  9.32 us
  transfers between devices with their start and end apart: 8, of which 4 were waited for; matrix products, arithmetic and copies ran while one was open for 9% of the time, Pallas kernels for 33%

profile of v5, /device:TPU:97, one launch (start us, length us, event | category | flops | bytes accessed | tf_op | source)
XLA Modules:
  0.0 260.5 jit_solution(10537754400977338571)
XLA Ops:
  0.6 0.8 collective-permute-start
  3.5 1.7 fusion.2
  5.2 1.9 select_convert_fusion.2
  9.1 7.4 %place.2 = bf16[2048,512]{1,0:T(8,128)(2,1)} custom-call(s32[1,2048]{1,0:T(1,128)} %compare_select_fusion.5.dest_ref, bf16[2048,512]{1,0:T(8,128)(2,1)} %bitcast.47), custom_call_target="tpu_custom_call" | custom-call | tf_op jit(solution)/shard_map/place/pallas_call | solution.py:42
  16.9 61.1 %deliver.1 = (bf16[64,32,512]{2,1,0:T(8,128)(2,1)}, s32[64,1,128]{2,1,0:T(1,128)}) custom-call(bf16[64,32,512]{2,1,0:T(8,128)(2,1)} %bitcast.45, s32[64,1,128]{2,1,0:T(1,128)} %pad.8.pos_ref), custom_call_target="tpu_custom_call" | custom-call | tf_op jit(solution)/shard_map/deliver/pallas_call | solution.py:132
  78.1 0.9 maximum_reduce_fusion
  79.7 4.9 %place.3.own_ref = bf16[1024,512]{1,0:T(8,128)(2,1)} custom-call(s32[1,2048]{1,0:T(1,128)} %reshape_reshape_squeeze.3.dest_ref, bf16[2048,512]{1,0:T(8,128)(2,1)} %bitcast.46), custom_call_target="tpu_custom_call" | custom-call | tf_op jit(solution)/shard_map/place/pallas_call | solution.py:42
  85.7 2.1 fusion.8.index_ref
  88.0 2.2 fusion.9.cot_ref
  90.2 1.7 convolution_convert_fusion.g_ref
  92.0 8.4 %collective-permute-done.1.next_ref = bf16[1024,512]{1,0:T(8,128)(2,1)} collective-permute-done((bf16[1024,512]{1,0:T(8,128)(2,1)}, bf16[1024,512]{1,0:T(8,128)(2,1)}, u32[]{:S(2)}, u32[]{:S(2)}) %collective-permute-start.1) | collective-permute-done | bytes 1048608 | tf_op jit(solution)/shard_map/ppermute | solution.py:30
  100.4 5.5 %project.1 = (bf16[1024,512]{1,0:T(8,128)(2,1)}, bf16[1024,512]{1,0:T(8,128)(2,1)}, bf16[1024,1536]{1,0:T(8,128)(2,1)}) custom-call(s32[1]{0:T(128)} %bitcast.11.limit_ref, bf16[1024,512]{1,0:T(8,128)(2,1)} %place.3.own_ref, bf16[1024,512]{1,0:T(8,128)(2,1)} %collective-permute-done.1.next_ref, f32[1,512]{1,0:T(1,128)} %bitcast.56, bf16[512,1536]{1,0:T(8,128)(2,1)} %weight_ref.3), custom_call_target="tpu_custom_call" | custom-call | tf_op jit(solution)/shard_map/project/pallas_call | solution.py:220
  105.8 34.8 %attend.1 = (bf16[1024,512]{1,0:T(8,128)(2,1)}, bf16[3,1024,512]{2,1,0:T(8,128)(2,1)}) custom-call(bf16[1024,1536]{1,0:T(8,128)(2,1)} %get-tuple-element.38.q_ref.k_ref.v_ref, bf16[1024,1536]{1,0:T(8,128)(2,1)} %get-tuple-element.38.q_ref.k_ref.v_ref, bf16[1024,1536]{1,0:T(8,128)(2,1)} %get-tuple-element.38.q_ref.k_ref.v_ref, ...), custom_call_target="tpu_custom_call" | custom-call | tf_op jit(solution)/shard_map/attend/pallas_call | solution.py:290
  140.6 4.5 %weight_grad.3 = bf16[4,512,256]{2,1,0:T(8,128)(2,1)} custom-call(s32[1]{0:T(128)} %bitcast.14.half_ref, bf16[1024,512]{1,0:T(8,128)(2,1)} %get-tuple-element.43.normed_ref, bf16[3,1024,512]{2,1,0:T(8,128)(2,1)} %get-tuple-element.40.d_ref, bf16[1024,512]{1,0:T(8,128)(2,1)} %get-tuple-element.44.mixed_ref, bf16[1024,512]{1,0:T(8,128)(2,1)} %copy-done.1), custom_call_target="tpu_custom_call" | custom-call | tf_op jit(solution)/shard_map/weight_grad/pallas_call | solution.py:384
  145.1 6.1 %input_grad.1 = (bf16[1024,512]{1,0:T(8,128)(2,1)}, f32[1,512]{1,0:T(1,128)}) custom-call(bf16[3,1024,512]{2,1,0:T(8,128)(2,1)} %get-tuple-element.40.d_ref, bf16[512,1536]{1,0:T(8,128)(2,1)} %weight_ref.3, bf16[1024,512]{1,0:T(8,128)(2,1)} %get-tuple-element.41.win_ref, bf16[1024,512]{1,0:T(8,128)(2,1)} %copy-done.1, f32[1,512]{1,0:T(1,128)} %bitcast.57), custom_call_target="tpu_custom_call" | custom-call | tf_op jit(solution)/shard_map/input_grad/pallas_call | solution.py:343
  151.2 0.9 collective-permute-start.2
  152.1 4.8 %weight_grad.2 = bf16[4,512,256]{2,1,0:T(8,128)(2,1)} custom-call(s32[1]{0:T(128)} %bitcast.13.half_ref, bf16[1024,512]{1,0:T(8,128)(2,1)} %get-tuple-element.43.normed_ref, bf16[3,1024,512]{2,1,0:T(8,128)(2,1)} %get-tuple-element.40.d_ref, bf16[1024,512]{1,0:T(8,128)(2,1)} %get-tuple-element.44.mixed_ref, bf16[1024,512]{1,0:T(8,128)(2,1)} %copy-done.1), custom_call_target="tpu_custom_call" | custom-call | tf_op jit(solution)/shard_map/weight_grad/pallas_call | solution.py:384
  157.6 1.7 add_convert_fusion.window_ref
  159.5 4.6 %collective-permute-done.2 = bf16[1024,512]{1,0:T(8,128)(2,1)} collective-permute-done((bf16[1024,512]{1,0:T(8,128)(2,1)}, bf16[1024,512]{1,0:T(8,128)(2,1)}, u32[]{:S(2)}, u32[]{:S(2)}) %collective-permute-start.2) | collective-permute-done | bytes 1048608 | tf_op jit(solution)/shard_map/ppermute | solution.py:30
  164.2 3.7 %collective-permute-start.7 = (bf16[1024,512]{1,0:T(8,128)(2,1)}, bf16[1024,512]{1,0:T(8,128)(2,1)}, u32[]{:S(2)}, u32[]{:S(2)}) collective-permute-start(bf16[1024,512]{1,0:T(8,128)(2,1)} %add_convert_fusion.window_ref), channel_id=1, source_target_pairs={{0,4},{4,8},{8,12},{12,16},{16,20},{20,24},{24,28},{28,32},{32,36}... | collective-permute-start | bytes 3145736 | tf_op jit(solution)/shard_map/ppermute | solution.py:30
  167.9 0.8 dynamic-slice_bitcast_fusion.2
  168.6 1.3 collective-permute-start.4
  169.9 1.4 collective-permute-start.6
  171.4 1.6 collective-permute-start.5
  173.0 1.3 copy.17.index_ref
  174.4 2.4 broadcast_select_fusion.src_ref
  176.8 5.6 %fetch.1 = bf16[2048,512]{1,0:T(8,128)(2,1)} custom-call(s32[2048,1]{1,0:T(8,128)} %copy.17.index_ref, bf16[1024,512]{1,0:T(8,128)(2,1)} %broadcast_select_fusion.src_ref), custom_call_target="tpu_custom_call" | custom-call | tf_op jit(solution)/shard_map/fetch/pallas_call | solution.py:67
  182.3 1.6 collective-permute-done.5
  183.9 1.9 fusion.20.q_ref
  185.8 63.3 %give_back.1 = (bf16[512,2048]{1,0:T(8,128)(2,1)}, f32[8,128]{1,0:T(8,128)}, bf16[64,32,512]{2,1,0:T(8,128)(2,1)}) custom-call(bf16[512,256]{1,0:T(8,128)(2,1)} %fusion.20.q_ref, f32[8,128]{1,0:T(8,128)} %pad.9.s_ref, bf16[64,32,512]{2,1,0:T(8,128)(2,1)} %bitcast.44), custom_call_target="tpu_custom_call" | custom-call | tf_op jit(solution)/shard_map/give_back/pallas_call | solution.py:618
  249.1 1.3 multiply_bitcast_fusion
  250.3 10.2 %finish.1 = (bf16[2048,512]{1,0:T(8,128)(2,1)}, f32[512,1536]{1,0:T(8,128)}, f32[512,512]{1,0:T(8,128)}, bf16[1024,512]{1,0:T(8,128)(2,1)}) custom-call(s32[1]{0:T(128)} %copy.19.offset_ref, s32[2048,1]{1,0:T(8,128)} %fusion.8.index_ref, bf16[2048,512]{1,0:T(8,128)(2,1)} %bitcast.48, bf16[512,2048]{1,0:T(8,128)(2,1)} %get-tuple-element.52.grad_ref, ...), custom_call_target="tpu_custom_call" | custom-call | tf_op jit(solution)/shard_map/finish/pallas_call | solution.py:168
  (38 shorter events, 5.9 us)
Async XLA Ops:
  0.6 89.6 %copy-start = (bf16[512,512]{1,0:T(8,128)(2,1)S(1)}, bf16[512,512]{1,0:T(8,128)(2,1)}, u32[]{:S(2)}) copy-start(bf16[512,512]{1,0:T(8,128)(2,1)} %param.14) | copy-start | bytes 1572868
  0.6 16.3 %collective-permute-start = (bf16[1024,512]{1,0:T(8,128)(2,1)}, bf16[1024,512]{1,0:T(8,128)(2,1)}, u32[]{:S(2)}, u32[]{:S(2)}) collective-permute-start(bf16[1024,512]{1,0:T(8,128)(2,1)} %bitcast.49), channel_id=1, source_target_pairs={{0,252},{4,0},{8,4},{12,8},{16,12},{20,16},{24,20},{28,24},{32,28}... | collective-permute-start | bytes 3145736 | tf_op jit(solution)/shard_map/ppermute | solution.py:30
  5.1 3.3 %copy-start.6 = (s32[1,2048]{1,0:T(1,128)S(1)}, s32[1,2048]{1,0:T(1,128)}, u32[]{:S(2)}) copy-start(s32[1,2048]{1,0:T(1,128)} %param.10) | copy-start | bytes 24580
  84.6 15.8 %collective-permute-start.1 = (bf16[1024,512]{1,0:T(8,128)(2,1)}, bf16[1024,512]{1,0:T(8,128)(2,1)}, u32[]{:S(2)}, u32[]{:S(2)}) collective-permute-start(bf16[1024,512]{1,0:T(8,128)(2,1)} %place.3.own_ref), channel_id=1, source_target_pairs={{0,252},{4,0},{8,4},{12,8},{16,12},{20,16},{24,20},{28,24},{32,28}... | collective-permute-start | bytes 3145736 | tf_op jit(solution)/shard_map/ppermute | solution.py:30
  90.2 15.6 %copy-start.1 = (bf16[1024,512]{1,0:T(8,128)(2,1)}, bf16[1024,512]{1,0:T(8,128)(2,1)S(1)}, u32[]{:S(2)}) copy-start(bf16[1024,512]{1,0:T(8,128)(2,1)S(1)} %fusion.9.cot_ref) | copy-start | bytes 3145732
  145.1 14.2 %collective-permute-start.3 = (bf16[4,512,256]{2,1,0:T(8,128)(2,1)}, bf16[4,512,256]{2,1,0:T(8,128)(2,1)S(1)}, u32[]{:S(2)}, u32[]{:S(2)}) collective-permute-start(bf16[4,512,256]{2,1,0:T(8,128)(2,1)} %weight_grad.3), channel_id=1, source_target_pairs={{0,4},{4,0},{8,12},{12,8},{16,20},{20,16},{24,28},{28,24},{32,36},... | collective-permute-start | bytes 3145736 | tf_op jit(solution)/shard_map/ppermute | solution.py:648
  151.2 12.9 %collective-permute-start.2 = (bf16[1024,512]{1,0:T(8,128)(2,1)}, bf16[1024,512]{1,0:T(8,128)(2,1)}, u32[]{:S(2)}, u32[]{:S(2)}) collective-permute-start(bf16[1024,512]{1,0:T(8,128)(2,1)} %get-tuple-element.42), channel_id=1, source_target_pairs={{0,4},{4,8},{8,12},{12,16},{16,20},{20,24},{24,28},{28,32},{32,36}... | collective-permute-start | bytes 3145736 | tf_op jit(solution)/shard_map/ppermute | solution.py:30
  152.1 4.8 %copy-start.7 = (f32[1,512]{1,0:T(1,128)S(1)}, f32[1,512]{1,0:T(1,128)}, u32[]{:S(2)}) copy-start(f32[1,512]{1,0:T(1,128)} %get-tuple-element.46) | copy-start | bytes 6148
  152.1 5.4 %copy-start.3 = (bf16[1024,512]{1,0:T(8,128)(2,1)S(1)}, bf16[1024,512]{1,0:T(8,128)(2,1)}, u32[]{:S(2)}) copy-start(bf16[1024,512]{1,0:T(8,128)(2,1)} %get-tuple-element.44.mixed_ref) | copy-start | bytes 3145732
  152.1 5.4 %copy-start.4 = (bf16[1024,512]{1,0:T(8,128)(2,1)S(1)}, bf16[1024,512]{1,0:T(8,128)(2,1)}, u32[]{:S(2)}) copy-start(bf16[1024,512]{1,0:T(8,128)(2,1)} %get-tuple-element.41.win_ref) | copy-start | bytes 3145732
  157.0 2.3 copy-start.2
  159.5 14.8 %copy-start.5 = (bf16[1024,512]{1,0:T(8,128)(2,1)S(1)}, bf16[1024,512]{1,0:T(8,128)(2,1)}, u32[]{:S(2)}) copy-start(bf16[1024,512]{1,0:T(8,128)(2,1)} %get-tuple-element.42) | copy-start | bytes 3145732
  164.2 86.2 %collective-permute-start.7 = (bf16[1024,512]{1,0:T(8,128)(2,1)}, bf16[1024,512]{1,0:T(8,128)(2,1)}, u32[]{:S(2)}, u32[]{:S(2)}) collective-permute-start(bf16[1024,512]{1,0:T(8,128)(2,1)} %add_convert_fusion.window_ref), channel_id=1, source_target_pairs={{0,4},{4,8},{8,12},{12,16},{16,20},{20,24},{24,28},{28,32},{32,36}... | collective-permute-start | bytes 3145736 | tf_op jit(solution)/shard_map/ppermute | solution.py:30
  168.6 13.7 %collective-permute-start.4 = (bf16[512,256]{1,0:T(8,128)(2,1)}, bf16[512,256]{1,0:T(8,128)(2,1)S(1)}, u32[]{:S(2)}, u32[]{:S(2)}) collective-permute-start(bf16[512,256]{1,0:T(8,128)(2,1)} %get-tuple-element.63), channel_id=1, source_target_pairs={{0,1},{1,2},{2,3},{3,0},{4,5},{5,6},{6,7},{7,4},{8,9},{9,10},{10,1... | collective-permute-start | bytes 786440 | tf_op jit(solution)/shard_map/ppermute | solution.py:30
  169.9 12.4 %collective-permute-start.6 = (bf16[512,256]{1,0:T(8,128)(2,1)S(1)}, bf16[512,256]{1,0:T(8,128)(2,1)}, u32[]{:S(2)}, u32[]{:S(2)}) collective-permute-start(bf16[512,256]{1,0:T(8,128)(2,1)S(1)} %get-tuple-element.64), channel_id=1, source_target_pairs={{0,3},{1,0},{2,1},{3,2},{4,7},{5,4},{6,5},{7,6},{8,11},{9,8},{10,9... | collective-permute-start | bytes 786440 | tf_op jit(solution)/shard_map/ppermute | solution.py:30
  171.4 12.6 %collective-permute-start.5 = (bf16[512,256]{1,0:T(8,128)(2,1)S(1)}, bf16[512,256]{1,0:T(8,128)(2,1)}, u32[]{:S(2)}, u32[]{:S(2)}) collective-permute-start(bf16[512,256]{1,0:T(8,128)(2,1)S(1)} %get-tuple-element.65), channel_id=1, source_target_pairs={{0,2},{1,3},{2,0},{3,1},{4,6},{5,7},{6,4},{7,5},{8,10},{9,11},{10,... | collective-permute-start | bytes 786440 | tf_op jit(solution)/shard_map/ppermute | solution.py:30

commit v6 on v5

--- a/solution.py
+++ b/solution.py
@@ -53,29 +53,43 @@
     )(dest.reshape(1, depth), src)
 
 
-def fetch_kernel(index_ref, src_ref, out_ref):
+def take(index_ref, src_ref, out_ref):
     block, depth = out_ref.shape[0], src_ref.shape[0]
+    index = jnp.broadcast_to(index_ref[...].astype(F32), (128, block)).T[:, :1].astype(jnp.int32)
     column = lax.broadcasted_iota(jnp.int32, (block, depth), 1)
-    hot = jnp.where(column == index_ref[...], 1.0, 0.0).astype(BF16)
+    hot = jnp.where(column == index, 1.0, 0.0).astype(BF16)
     out_ref[...] = jnp.dot(hot, src_ref[...], preferred_element_type=F32).astype(BF16)
 
 
-def fetch(index, src, block=512):
-    depth, width = src.shape
-    rows = index.shape[0]
-    assert index.shape == (rows, 1)
+def fetch_kernel(limit_ref, index_ref, own_ref, back_ref, out_ref, src_ref):
+    @pl.when(pl.program_id(0) == 0)
+    def _():
+        row = lax.broadcasted_iota(jnp.int32, own_ref.shape, 0)
+        src_ref[...] = jnp.where(
+            row < limit_ref[0], own_ref[...].astype(F32), back_ref[...].astype(F32)
+        ).astype(BF16)
+
+    take(index_ref, src_ref, out_ref)
+
+
+def fetch(limit, index, own, back, block=512):
+    rows = index.shape[1]
+    whole = pl.BlockSpec(own.shape, lambda i: (0, 0))
     return pl.pallas_call(
         fetch_kernel,
         grid=(rows // block,),
         in_specs=[
-            pl.BlockSpec((block, 1), lambda i: (i, 0)),
-            pl.BlockSpec((depth, width), lambda i: (0, 0)),
-        ],
-        out_specs=pl.BlockSpec((block, width), lambda i: (i, 0)),
-        out_shape=jax.ShapeDtypeStruct((rows, width), BF16),
+            pl.BlockSpec(memory_space=pltpu.SMEM),
+            pl.BlockSpec((1, block), lambda i: (0, i)),
+            whole,
+            whole,
+        ],
+        out_specs=pl.BlockSpec((block, own.shape[1]), lambda i: (i, 0)),
+        out_shape=jax.ShapeDtypeStruct((rows, own.shape[1]), BF16),
+        scratch_shapes=[pltpu.VMEM(own.shape, BF16)],
         compiler_params=params(),
         name="fetch",
-    )(index, src)
+    )(limit, index, own, back)
 
 
 def deliver_kernel(count, out_ref, pos_ref, in_ref, in_pos_ref, sems, own_sems):
@@ -144,10 +158,12 @@
 
 
 def finish_kernel(
-    offset_ref, index_ref, src_ref, grad_ref, window_ref, back_ref,
-    out_ref, in_ref, outer_ref, block_ref, *, factor,
+    offset_ref, index_ref, src_ref, grad_ref, window_ref, back_ref, small_ref,
+    out_ref, in_ref, outer_ref, block_ref, gain_ref, *, factor,
 ):
-    fetch_kernel(index_ref, src_ref, out_ref)
+    take(index_ref, src_ref, out_ref)
+    for line in range(gain_ref.shape[1] // 128):
+        gain_ref[:, line * 128 : (line + 1) * 128] = small_ref[line : line + 1, :] * factor
     rows = window_ref.shape[0]
     row = lax.broadcasted_iota(jnp.int32, window_ref.shape, 0)
     rolled = jnp.where(
@@ -159,9 +175,9 @@
     outer_ref[...] = grad_ref[:, inner:].astype(F32) * factor
 
 
-def finish(offset, index, src, grads, window, back, factor, steps=4):
+def finish(offset, index, src, grads, window, back, small, factor, steps=4):
     depth, width = src.shape
-    rows, tall = index.shape[0], grads.shape[0]
+    rows, tall = index.shape[1], grads.shape[0]
     block, part, lanes = rows // steps, tall // steps, width // steps
     inner = grads.shape[1] - width
     strip = pl.BlockSpec((window.shape[0], lanes), lambda i: (0, i))
@@ -170,27 +186,30 @@
         grid=(steps,),
         in_specs=[
             pl.BlockSpec(memory_space=pltpu.SMEM),
-            pl.BlockSpec((block, 1), lambda i: (i, 0)),
+            pl.BlockSpec((1, block), lambda i: (0, i)),
             pl.BlockSpec((depth, width), lambda i: (0, 0)),
             pl.BlockSpec((part, inner + width), lambda i: (i, 0)),
             strip,
             strip,
+            pl.BlockSpec(small.shape, lambda i: (0, 0)),
         ],
         out_specs=[
             pl.BlockSpec((block, width), lambda i: (i, 0)),
             pl.BlockSpec((part, inner), lambda i: (i, 0)),
             pl.BlockSpec((part, width), lambda i: (i, 0)),
             strip,
+            pl.BlockSpec((1, width), lambda i: (0, 0)),
         ],
         out_shape=[
             jax.ShapeDtypeStruct((rows, width), BF16),
             jax.ShapeDtypeStruct((tall, inner), F32),
             jax.ShapeDtypeStruct((tall, width), F32),
             jax.ShapeDtypeStruct(window.shape, BF16),
+            jax.ShapeDtypeStruct((1, width), F32),
         ],
         compiler_params=params(),
         name="finish",
-    )(offset, index, src, grads, window, back)
+    )(offset, index, src, grads, window, back, small)
 
 
 def unit_of(values):
@@ -402,12 +421,14 @@
     )(half.reshape(1), normed, d, mixed, cot)
 
 
-def return_kernel(
-    sizes, count, q_ref, s_ref, back_ref, out_ref, t_ref, arrived_ref,
-    band, in_x, in_z, small, small_core, small_y, small_z, small_x,
-    send_sem, recv_sem, small_send, small_recv, slot_sems, own_sem,
-):
+def return_kernel(sizes, count, *refs):
     nx, ny, nz = sizes
+    parts = refs[:ny]
+    (
+        s_ref, back_ref, out_ref, t_ref, arrived_ref,
+        q_ref, band, in_x, in_z, small, small_core, small_y, small_z, small_x,
+        send_sem, recv_sem, small_send, small_recv, slot_sems, own_sem,
+    ) = refs[ny:]
     rows, part_w = q_ref.shape
     half_w = part_w * ny
     band_h, piece_h = rows // nx, rows // nx // nz
@@ -435,6 +456,11 @@
     lax.fori_loop(1, count, greet, 0)
     for device, _ in by_y:
         pl.semaphore_signal(barrier, inc=1, device_id=device, device_id_type=MESH)
+    total = parts[0][...].astype(F32)
+    for k in range(1, ny):
+        total += parts[k][...].astype(F32)
+    q_ref[...] = total.astype(BF16)
+    small[...] = s_ref[...]
     pl.semaphore_wait(barrier, count - 1 + len(by_y))
 
     def slot_copy(j):
@@ -518,7 +544,6 @@
     def lines(index, height):
         return pl.ds(pl.multiple_of(index * height, height), height)
 
-    small[...] = s_ref[...]
     copies = [
         send(q_ref.at[lines(i, band_h), :], in_x.at[k], device) for k, (device, i) in enumerate(by_x)
     ]
@@ -605,19 +630,20 @@
     lax.fori_loop(0, count - 1, came_slot, 0)
 
 
-def give_back(quarter, small, back, sizes):
+def give_back(parts, small, back, sizes):
     nx, ny, nz = sizes
-    rows, part = quarter.shape
+    rows, part = parts[0].shape
     count = back.shape[0]
     peers = 1 + (ny - 1) + (nz - 1) + (nx - 1)
     vmem = pl.BlockSpec(memory_space=pltpu.VMEM)
     anywhere = pl.BlockSpec(memory_space=pl.ANY)
     buffers = [
+        (rows, part),
         (rows // nx, part), (max(nx - 1, 1), rows // nx, part), (nz - 1, rows // nx // nz, part),
     ]
     return pl.pallas_call(
         functools.partial(return_kernel, sizes, count),
-        in_specs=[vmem, vmem, anywhere],
+        in_specs=[vmem] * (ny + 1) + [anywhere],
         out_specs=[vmem, vmem, anywhere],
         out_shape=[
             jax.ShapeDtypeStruct((rows, part * ny * 2), BF16),
@@ -637,7 +663,7 @@
         ],
         compiler_params=params(collective_id=0, has_side_effects=True),
         name="give_back",
-    )(quarter, small, back)
+    )(*parts, small, back)
 
 
 def scatter_core(normed, d, mixed, cot):
@@ -658,10 +684,7 @@
     def piece(step):
         return lax.dynamic_index_in_dim(half, lax.rem(y + step, reps), 0, keepdims=False)
 
-    total = piece(0).astype(F32)
-    for step in range(1, reps):
-        total += shifted(piece(step), "rep", step).astype(F32)
-    return total.astype(BF16)
+    return [piece(0)] + [shifted(piece(step), "rep", step) for step in range(1, reps)]
 
 
 def route_slots(rank_row, point_count, total, row_count, shard_count, send_size, offset):
@@ -700,7 +723,6 @@
     total = row_count * shard_count
     offset = patch_shift[0]
     limit = row_count - offset
-    own_row = jnp.arange(row_count, dtype=jnp.int32)[:, None] < limit
 
     cot_rows = cotangent[0]
     cot_next = shifted(cot_rows, "pts", -1)
@@ -729,11 +751,7 @@
 
     rolled = place(in_position, incoming, row_count)
     rolled_next = shifted(rolled, "pts", -1)
-    target_column = target.reshape(slot_total, 1)
-    position_column = jnp.maximum(in_position, -1).reshape(slot_total, 1)
-    rolled_next, target_column, position_column, grad_mixed = lax.optimization_barrier(
-        (rolled_next, target_column, position_column, grad_mixed)
-    )
+    rolled_next, grad_mixed = lax.optimization_barrier((rolled_next, grad_mixed))
     window, normed, qkv = project(limit.reshape(1), rolled, rolled_next, norm_gain, project_in)
     mixed, d_qkv = attend(qkv, grad_mixed)
     grad_window, scale = input_grad(d_qkv, project_in, window, cot_window, norm_gain)
@@ -744,29 +762,29 @@
         window.astype(F32) + jnp.dot(mixed, project_out, preferred_element_type=F32)
     ).astype(BF16)
     small = jnp.pad(scale.reshape(width // 128, 128), ((0, 8 - width // 128), (0, 0)))
-    grad_back, half, block_window, position_column, small = lax.optimization_barrier(
-        (grad_back, half, block_window, position_column, small)
-    )
-    quarter = scatter_rep(half)
+    grad_back, half, block_window, small = lax.optimization_barrier(
+        (grad_back, half, block_window, small)
+    )
+    parts = scatter_rep(half)
     block_back = shifted(block_window, "pts", 1)
 
-    grad_rolled = jnp.where(own_row, grad_window, grad_back)
-    returning = fetch(position_column, grad_rolled)
+    returning = fetch(limit.reshape(1), in_position.reshape(1, slot_total), grad_window, grad_back)
     summed, small, arrived = give_back(
-        quarter, small, returning.reshape(shard_count, slot_size, width), sizes
+        parts, small, returning.reshape(shard_count, slot_size, width), sizes
     )
     arrived = arrived.reshape(slot_total, width)
 
     factor = 1.0 / math.sqrt(total * lax.axis_size("rep"))
-    grad_points, grad_in, grad_out, block_rows = finish(
-        offset.reshape(1), target_column, arrived, summed, block_window, block_back, factor
+    grad_points, grad_in, grad_out, block_rows, gain = finish(
+        offset.reshape(1), target.reshape(1, slot_total), arrived, summed,
+        block_window, block_back, small, factor,
     )
     return (
         block_rows[None],
         grad_points[None],
         grad_in,
         grad_out,
-        small[: width // 128].reshape(width) * factor,
+        gain.reshape(width),
     )
 
 

time: 265 us -> 267 us (level)
  other arithmetic: 14.5 us -> 6.35 us
  waiting for transfers between devices: 15 us -> 22.8 us
  Pallas kernels: 208 us -> 211 us
    ppermute x7, waiting for transfers between devices: 15 us -> 22.8 us  [shifted(): return lax.ppermute(value, axis, pairs)]
  transfers between devices with their start and end apart: 8 -> 8, of which waited for: 4 -> 5; matrix products, arithmetic and copies ran while one was open for 9% -> 5% of each run, Pallas kernels for 33% -> 34%
where the time goes in v6:
time: 267 us; the launch traced here: 263 us
  Pallas kernels  211 us (79%)
  waiting for transfers between devices  22.8 us (9%)
  starting transfers between devices  9.34 us (3%)
  other arithmetic  6.35 us (2%)
  local copies, waits for them, and re-layouts  6.29 us (2%)
  matrix products  5.74 us (2%)
    pallas_call x1, Pallas kernels, give_back(): pl.pallas_call(functools.partial(return_kernel, sizes, count), in_specs=[...  63.9 us
    pallas_call x1, Pallas kernels, deliver(): pl.pallas_call(functools.partial(deliver_kernel, count), in_specs=[anywhe...  61.1 us
    pallas_call x1, Pallas kernels, attend(): pl.pallas_call(functools.partial(attend_kernel, chunk=chunk), grid=(pairs...  34.8 us
    ppermute x7, waiting for transfers between devices, shifted(): return lax.ppermute(value, axis, pairs)  22.8 us
    pallas_call x2, Pallas kernels, place(): pl.pallas_call(place_kernel, grid=(rows // block,), in_specs=[pl.BlockSpe...  12.3 us
    pallas_call x1, Pallas kernels, finish(): pl.pallas_call(functools.partial(finish_kernel, factor=factor), grid=(ste...  11 us
    ppermute x7, starting transfers between devices, shifted(): return lax.ppermute(value, axis, pairs)  9.34 us
    pallas_call x2, Pallas kernels, weight_grad(): pl.pallas_call(weight_grad_kernel, grid_spec=pltpu.PrefetchScalarGridSpec...  9.13 us
  transfers between devices with their start and end apart: 8, of which 5 were waited for; matrix products, arithmetic and copies ran while one was open for 5% of the time, Pallas kernels for 34%

profile of v6, /device:TPU:97, one launch (start us, length us, event | category | flops | bytes accessed | tf_op | source)
XLA Modules:
  0.0 263.3 jit_solution(4187166940437106857)
XLA Ops:
  0.6 0.8 collective-permute-start
  2.7 0.7 add_select_fusion.1
  3.5 1.7 fusion.2
  5.2 1.9 select_convert_fusion.2
  8.5 0.7 compare_select_fusion.5.dest_ref.index_ref
  9.1 7.4 %place.2 = bf16[2048,512]{1,0:T(8,128)(2,1)} custom-call(s32[1,2048]{1,0:T(1,128)} %compare_select_fusion.5.dest_ref.index_ref, bf16[2048,512]{1,0:T(8,128)(2,1)} %bitcast.42), custom_call_target="tpu_custom_call" | custom-call | tf_op jit(solution)/shard_map/place/pallas_call | solution.py:42
  16.8 1.0 copy-done.8
  17.8 61.1 %deliver.1 = (bf16[64,32,512]{2,1,0:T(8,128)(2,1)}, s32[64,1,128]{2,1,0:T(1,128)}) custom-call(bf16[64,32,512]{2,1,0:T(8,128)(2,1)} %bitcast.40, s32[64,1,128]{2,1,0:T(1,128)} %pad.8.pos_ref), custom_call_target="tpu_custom_call" | custom-call | tf_op jit(solution)/shard_map/deliver/pallas_call | solution.py:146
  79.0 0.9 slice_reduce_fusion
  80.5 4.9 %place.3.own_ref = bf16[1024,512]{1,0:T(8,128)(2,1)} custom-call(s32[1,2048]{1,0:T(1,128)} %reshape_reshape_squeeze.4.dest_ref.index_ref, bf16[2048,512]{1,0:T(8,128)(2,1)} %bitcast.41), custom_call_target="tpu_custom_call" | custom-call | tf_op jit(solution)/shard_map/place/pallas_call | solution.py:42
  85.8 2.6 %fusion.3.cot_ref = bf16[1024,512]{1,0:T(8,128)(2,1)S(1)} fusion(s32[]{:T(128)S(6)} %select_n.134, bf16[1024,512]{1,0:T(8,128)(2,1)S(1)} %bitcast.45, bf16[1024,512]{1,0:T(8,128)(2,1)} %copy-done.8), kind=kLoop, calls=%fused_computation.9 | loop fusion | flops 2097152 | bytes 3145732 | tf_op jit(solution)/shard_map/concatenate | solution.py:748
  88.5 1.7 convolution_convert_fusion.g_ref
  90.2 10.9 %collective-permute-done.1.next_ref = bf16[1024,512]{1,0:T(8,128)(2,1)S(1)} collective-permute-done((bf16[1024,512]{1,0:T(8,128)(2,1)}, bf16[1024,512]{1,0:T(8,128)(2,1)S(1)}, u32[]{:S(2)}, u32[]{:S(2)}) %collective-permute-start.1) | collective-permute-done | bytes 1048608 | tf_op jit(solution)/shard_map/ppermute | solution.py:30
  101.1 1.0 copy-done.5
  102.1 5.5 %project.1 = (bf16[1024,512]{1,0:T(8,128)(2,1)}, bf16[1024,512]{1,0:T(8,128)(2,1)}, bf16[1024,1536]{1,0:T(8,128)(2,1)}) custom-call(s32[1]{0:T(128)} %bitcast.4.limit_ref, bf16[1024,512]{1,0:T(8,128)(2,1)} %place.3.own_ref, bf16[1024,512]{1,0:T(8,128)(2,1)} %copy-done.5, f32[1,512]{1,0:T(1,128)} %bitcast.49, bf16[512,1536]{1,0:T(8,128)(2,1)} %weight_ref.3), custom_call_target="tpu_custom_call" | custom-call | tf_op jit(solution)/shard_map/project/pallas_call | solution.py:239
  107.5 34.8 %attend.1 = (bf16[1024,512]{1,0:T(8,128)(2,1)}, bf16[3,1024,512]{2,1,0:T(8,128)(2,1)}) custom-call(bf16[1024,1536]{1,0:T(8,128)(2,1)} %get-tuple-element.35.q_ref.k_ref.v_ref, bf16[1024,1536]{1,0:T(8,128)(2,1)} %get-tuple-element.35.q_ref.k_ref.v_ref, bf16[1024,1536]{1,0:T(8,128)(2,1)} %get-tuple-element.35.q_ref.k_ref.v_ref, ...), custom_call_target="tpu_custom_call" | custom-call | tf_op jit(solution)/shard_map/attend/pallas_call | solution.py:309
  142.3 4.5 %weight_grad.3 = bf16[4,512,256]{2,1,0:T(8,128)(2,1)} custom-call(s32[1]{0:T(128)} %bitcast.12.half_ref, bf16[1024,512]{1,0:T(8,128)(2,1)} %get-tuple-element.40.normed_ref, bf16[3,1024,512]{2,1,0:T(8,128)(2,1)} %get-tuple-element.37.d_ref, bf16[1024,512]{1,0:T(8,128)(2,1)} %get-tuple-element.41.mixed_ref, bf16[1024,512]{1,0:T(8,128)(2,1)} %copy-done.1), custom_call_target="tpu_custom_call" | custom-call | tf_op jit(solution)/shard_map/weight_grad/pallas_call | solution.py:403
  146.8 6.1 %input_grad.1 = (bf16[1024,512]{1,0:T(8,128)(2,1)}, f32[1,512]{1,0:T(1,128)}) custom-call(bf16[3,1024,512]{2,1,0:T(8,128)(2,1)} %get-tuple-element.37.d_ref, bf16[512,1536]{1,0:T(8,128)(2,1)} %weight_ref.3, bf16[1024,512]{1,0:T(8,128)(2,1)} %get-tuple-element.38.win_ref, bf16[1024,512]{1,0:T(8,128)(2,1)} %copy-done.1, f32[1,512]{1,0:T(1,128)} %bitcast.50), custom_call_target="tpu_custom_call" | custom-call | tf_op jit(solution)/shard_map/input_grad/pallas_call | solution.py:362
  152.9 0.9 collective-permute-start.2
  153.8 4.6 %weight_grad.2 = bf16[4,512,256]{2,1,0:T(8,128)(2,1)} custom-call(s32[1]{0:T(128)} %bitcast.11.half_ref, bf16[1024,512]{1,0:T(8,128)(2,1)} %get-tuple-element.40.normed_ref, bf16[3,1024,512]{2,1,0:T(8,128)(2,1)} %get-tuple-element.37.d_ref, bf16[1024,512]{1,0:T(8,128)(2,1)} %get-tuple-element.41.mixed_ref, bf16[1024,512]{1,0:T(8,128)(2,1)} %copy-done.1), custom_call_target="tpu_custom_call" | custom-call | tf_op jit(solution)/shard_map/weight_grad/pallas_call | solution.py:403
  159.0 1.7 add_convert_fusion.window_ref
  161.0 4.8 %collective-permute-done.2.back_ref = bf16[1024,512]{1,0:T(8,128)(2,1)S(1)} collective-permute-done((bf16[1024,512]{1,0:T(8,128)(2,1)}, bf16[1024,512]{1,0:T(8,128)(2,1)S(1)}, u32[]{:S(2)}, u32[]{:S(2)}) %collective-permute-start.2) | collective-permute-done | bytes 1048608 | tf_op jit(solution)/shard_map/ppermute | solution.py:30
  165.9 3.6 %collective-permute-start.7 = (bf16[1024,512]{1,0:T(8,128)(2,1)}, bf16[1024,512]{1,0:T(8,128)(2,1)}, u32[]{:S(2)}, u32[]{:S(2)}) collective-permute-start(bf16[1024,512]{1,0:T(8,128)(2,1)} %add_convert_fusion.window_ref), channel_id=1, source_target_pairs={{0,4},{4,8},{8,12},{12,16},{16,20},{20,24},{24,28},{28,32},{32,36}... | collective-permute-start | bytes 3145736 | tf_op jit(solution)/shard_map/ppermute | solution.py:30
  169.4 0.8 dynamic-slice_bitcast_fusion
  170.2 2.7 %collective-permute-start.6 = (bf16[512,256]{1,0:T(8,128)(2,1)S(1)}, bf16[512,256]{1,0:T(8,128)(2,1)S(1)}, u32[]{:S(2)}, u32[]{:S(2)}) collective-permute-start(bf16[512,256]{1,0:T(8,128)(2,1)S(1)} %get-tuple-element.57), channel_id=1, source_target_pairs={{0,3},{1,0},{2,1},{3,2},{4,7},{5,4},{6,5},{7,6},{8,11},{9,8},{10,9... | collective-permute-start | bytes 786440 | tf_op jit(solution)/shard_map/ppermute | solution.py:30
  173.3 0.7 collective-permute-start.4
  174.0 6.7 %fetch.1 = bf16[2048,512]{1,0:T(8,128)(2,1)} custom-call(s32[1]{0:T(128)} %bitcast.4.limit_ref, s32[1,2048]{1,0:T(1,128)} %reshape_reshape_squeeze.4.dest_ref.index_ref, bf16[1024,512]{1,0:T(8,128)(2,1)} %get-tuple-element.39.own_ref, bf16[1024,512]{1,0:T(8,128)(2,1)} %copy-done.4), custom_call_target="tpu_custom_call" | custom-call | tf_op jit(solution)/shard_map/fetch/pallas_call | solution.py:78
  180.7 2.9 %collective-permute-done.6.refs_3_ = bf16[512,256]{1,0:T(8,128)(2,1)S(1)} collective-permute-done((bf16[512,256]{1,0:T(8,128)(2,1)S(1)}, bf16[512,256]{1,0:T(8,128)(2,1)S(1)}, u32[]{:S(2)}, u32[]{:S(2)}) %collective-permute-start.6) | collective-permute-done | bytes 262176 | tf_op jit(solution)/shard_map/ppermute | solution.py:30
  183.6 3.9 %collective-permute-done.4.refs_1_ = bf16[512,256]{1,0:T(8,128)(2,1)S(1)} collective-permute-done((bf16[512,256]{1,0:T(8,128)(2,1)S(1)}, bf16[512,256]{1,0:T(8,128)(2,1)S(1)}, u32[]{:S(2)}, u32[]{:S(2)}) %collective-permute-start.4) | collective-permute-done | bytes 262176 | tf_op jit(solution)/shard_map/ppermute | solution.py:30
  187.6 0.7 copy-done.11
  188.3 63.9 %give_back.1 = (bf16[512,2048]{1,0:T(8,128)(2,1)}, f32[8,128]{1,0:T(8,128)}, bf16[64,32,512]{2,1,0:T(8,128)(2,1)}) custom-call(bf16[512,256]{1,0:T(8,128)(2,1)} %get-tuple-element.60.refs_0_, bf16[512,256]{1,0:T(8,128)(2,1)} %copy-done.11, bf16[512,256]{1,0:T(8,128)(2,1)} %copy-done.10, bf16[512,256]{1,0:T(8,128)(2,1)} %copy-done.9, f32[8,128]{1,0:T(8,128)} %pad.9.refs_4_, ...), custom_call_target="tpu_custom_call" | custom-call | tf_op jit(solution)/shard_map/give_back/pallas_call | solution.py:644
  252.2 11.0 %finish.1 = (bf16[2048,512]{1,0:T(8,128)(2,1)}, f32[512,1536]{1,0:T(8,128)}, f32[512,512]{1,0:T(8,128)}, bf16[1024,512]{1,0:T(8,128)(2,1)}, f32[1,512]{1,0:T(1,128)}) custom-call(s32[1]{0:T(128)} %copy.14.offset_ref, s32[1,2048]{1,0:T(1,128)} %compare_select_fusion.5.dest_ref.index_ref, bf16[2048,512]{1,0:T(8,128)(2,1)} %bitcast.43, ...), custom_call_target="tpu_custom_call" | custom-call | tf_op jit(solution)/shard_map/finish/pallas_call | solution.py:184
  (41 shorter events, 4.0 us)
Async XLA Ops:
  0.6 87.8 %copy-start = (bf16[512,512]{1,0:T(8,128)(2,1)S(1)}, bf16[512,512]{1,0:T(8,128)(2,1)}, u32[]{:S(2)}) copy-start(bf16[512,512]{1,0:T(8,128)(2,1)} %param.14) | copy-start | bytes 1572868
  0.6 16.2 %collective-permute-start = (bf16[1024,512]{1,0:T(8,128)(2,1)}, bf16[1024,512]{1,0:T(8,128)(2,1)S(1)}, u32[]{:S(2)}, u32[]{:S(2)}) collective-permute-start(bf16[1024,512]{1,0:T(8,128)(2,1)} %bitcast.44), channel_id=1, source_target_pairs={{0,252},{4,0},{8,4},{12,8},{16,12},{20,16},{24,20},{28,24},{32,28}... | collective-permute-start | bytes 3145736 | tf_op jit(solution)/shard_map/ppermute | solution.py:30
  5.1 3.3 %copy-start.12 = (s32[1,2048]{1,0:T(1,128)S(1)}, s32[1,2048]{1,0:T(1,128)}, u32[]{:S(2)}) copy-start(s32[1,2048]{1,0:T(1,128)} %param.10) | copy-start | bytes 24580
  16.8 1.0 copy-start.8
  78.9 6.9 %copy-start.7 = (bf16[1,1024,512]{2,1,0:T(8,128)(2,1)S(1)}, bf16[1,1024,512]{2,1,0:T(8,128)(2,1)}, u32[]{:S(2)}) copy-start(bf16[1,1024,512]{2,1,0:T(8,128)(2,1)} %param.15) | copy-start | bytes 3145732
  85.5 15.6 %collective-permute-start.1 = (bf16[1024,512]{1,0:T(8,128)(2,1)}, bf16[1024,512]{1,0:T(8,128)(2,1)S(1)}, u32[]{:S(2)}, u32[]{:S(2)}) collective-permute-start(bf16[1024,512]{1,0:T(8,128)(2,1)} %place.3.own_ref), channel_id=1, source_target_pairs={{0,252},{4,0},{8,4},{12,8},{16,12},{20,16},{24,20},{28,24},{32,28}... | collective-permute-start | bytes 3145736 | tf_op jit(solution)/shard_map/ppermute | solution.py:30
  88.5 19.1 %copy-start.1 = (bf16[1024,512]{1,0:T(8,128)(2,1)}, bf16[1024,512]{1,0:T(8,128)(2,1)S(1)}, u32[]{:S(2)}) copy-start(bf16[1024,512]{1,0:T(8,128)(2,1)S(1)} %fusion.3.cot_ref) | copy-start | bytes 3145732
  101.1 1.0 copy-start.5
  146.8 13.9 %collective-permute-start.3 = (bf16[4,512,256]{2,1,0:T(8,128)(2,1)}, bf16[4,512,256]{2,1,0:T(8,128)(2,1)S(1)}, u32[]{:S(2)}, u32[]{:S(2)}) collective-permute-start(bf16[4,512,256]{2,1,0:T(8,128)(2,1)} %weight_grad.3), channel_id=1, source_target_pairs={{0,4},{4,0},{8,12},{12,8},{16,20},{20,16},{24,28},{28,24},{32,36},... | collective-permute-start | bytes 3145736 | tf_op jit(solution)/shard_map/ppermute | solution.py:674
  152.9 12.9 %collective-permute-start.2 = (bf16[1024,512]{1,0:T(8,128)(2,1)}, bf16[1024,512]{1,0:T(8,128)(2,1)S(1)}, u32[]{:S(2)}, u32[]{:S(2)}) collective-permute-start(bf16[1024,512]{1,0:T(8,128)(2,1)} %get-tuple-element.39.own_ref), channel_id=1, source_target_pairs={{0,4},{4,8},{8,12},{12,16},{16,20},{20,24},{24,28},{28,32},{32,36}... | collective-permute-start | bytes 3145736 | tf_op jit(solution)/shard_map/ppermute | solution.py:30
  153.8 4.6 %copy-start.13 = (f32[1,512]{1,0:T(1,128)S(1)}, f32[1,512]{1,0:T(1,128)}, u32[]{:S(2)}) copy-start(f32[1,512]{1,0:T(1,128)} %get-tuple-element.42) | copy-start | bytes 6148
  153.8 5.2 %copy-start.3 = (bf16[1024,512]{1,0:T(8,128)(2,1)S(1)}, bf16[1024,512]{1,0:T(8,128)(2,1)}, u32[]{:S(2)}) copy-start(bf16[1024,512]{1,0:T(8,128)(2,1)} %get-tuple-element.41.mixed_ref) | copy-start | bytes 3145732
  153.8 5.2 %copy-start.6 = (bf16[1024,512]{1,0:T(8,128)(2,1)S(1)}, bf16[1024,512]{1,0:T(8,128)(2,1)}, u32[]{:S(2)}) copy-start(bf16[1024,512]{1,0:T(8,128)(2,1)} %get-tuple-element.38.win_ref) | copy-start | bytes 3145732
  158.4 2.3 copy-start.2
  165.9 8.1 %copy-start.4 = (bf16[1024,512]{1,0:T(8,128)(2,1)}, bf16[1024,512]{1,0:T(8,128)(2,1)S(1)}, u32[]{:S(2)}) copy-start(bf16[1024,512]{1,0:T(8,128)(2,1)S(1)} %collective-permute-done.2.back_ref) | copy-start | bytes 3145732
  165.9 86.3 %collective-permute-start.7 = (bf16[1024,512]{1,0:T(8,128)(2,1)}, bf16[1024,512]{1,0:T(8,128)(2,1)}, u32[]{:S(2)}, u32[]{:S(2)}) collective-permute-start(bf16[1024,512]{1,0:T(8,128)(2,1)} %add_convert_fusion.window_ref), channel_id=1, source_target_pairs={{0,4},{4,8},{8,12},{12,16},{16,20},{20,24},{24,28},{28,32},{32,36}... | collective-permute-start | bytes 3145736 | tf_op jit(solution)/shard_map/ppermute | solution.py:30
  170.2 13.4 %collective-permute-start.6 = (bf16[512,256]{1,0:T(8,128)(2,1)S(1)}, bf16[512,256]{1,0:T(8,128)(2,1)S(1)}, u32[]{:S(2)}, u32[]{:S(2)}) collective-permute-start(bf16[512,256]{1,0:T(8,128)(2,1)S(1)} %get-tuple-element.57), channel_id=1, source_target_pairs={{0,3},{1,0},{2,1},{3,2},{4,7},{5,4},{6,5},{7,6},{8,11},{9,8},{10,9... | collective-permute-start | bytes 786440 | tf_op jit(solution)/shard_map/ppermute | solution.py:30
  173.0 10.7 %collective-permute-start.5 = (bf16[512,256]{1,0:T(8,128)(2,1)S(1)}, bf16[512,256]{1,0:T(8,128)(2,1)S(1)}, u32[]{:S(2)}, u32[]{:S(2)}) collective-permute-start(bf16[512,256]{1,0:T(8,128)(2,1)S(1)} %get-tuple-element.58), channel_id=1, source_target_pairs={{0,2},{1,3},{2,0},{3,1},{4,6},{5,7},{6,4},{7,5},{8,10},{9,11},{10,... | collective-permute-start | bytes 786440 | tf_op jit(solution)/shard_map/ppermute | solution.py:30
  173.3 14.3 %collective-permute-start.4 = (bf16[512,256]{1,0:T(8,128)(2,1)S(1)}, bf16[512,256]{1,0:T(8,128)(2,1)S(1)}, u32[]{:S(2)}, u32[]{:S(2)}) collective-permute-start(bf16[512,256]{1,0:T(8,128)(2,1)S(1)} %get-tuple-element.59), channel_id=1, source_target_pairs={{0,1},{1,2},{2,3},{3,0},{4,5},{5,6},{6,7},{7,4},{8,9},{9,10},{10,1... | collective-permute-start | bytes 786440 | tf_op jit(solution)/shard_map/ppermute | solution.py:30
  183.6 3.9 %copy-start.9 = (bf16[512,256]{1,0:T(8,128)(2,1)}, bf16[512,256]{1,0:T(8,128)(2,1)S(1)}, u32[]{:S(2)}) copy-start(bf16[512,256]{1,0:T(8,128)(2,1)S(1)} %collective-permute-done.6.refs_3_) | copy-start | bytes 786436
  183.6 3.9 %copy-start.10 = (bf16[512,256]{1,0:T(8,128)(2,1)}, bf16[512,256]{1,0:T(8,128)(2,1)S(1)}, u32[]{:S(2)}) copy-start(bf16[512,256]{1,0:T(8,128)(2,1)S(1)} %collective-permute-done.5.refs_2_) | copy-start | bytes 786436
  187.6 0.7 copy-start.11
